TPU v7x, 512 devices: a whole 4x4x16 slice. The times are simulated.
512 devices in a mesh: dp: 32 (over y_lo, z), mp: 16 (over x, y_hi, core).
Axes of the slice: x: 4, y: 4 (y_hi: 2, y_lo: 2; y = y_hi * 2 + y_lo), z: 16, core: 2. Of those that a mesh axis runs over, the one named last changes fastest.
Arguments:
- hidden: bfloat16 [8192, 8192], P('dp', 'mp'), may hold values from -6 to 6
- target_gain: float32 [8192], replicated, may hold values from 0.1 to 1.9
- target_weight: bfloat16 [2048, 8192], P('mp'), may hold values from -0.0625 to 0.0625
- draft_gain: float32 [8192], P('mp'), may hold values from 0.1 to 1.9
- draft_weight: bfloat16 [2048, 8192], P('dp', 'mp'), may hold values from -0.0625 to 0.0625
- logits: bfloat16 [8192, 32000], P('dp', 'mp'), may hold values from -40 to 300
- seq_lens: int32 [32, 2], P('dp'), may hold values from 32 to 128, as said below
- tool_mask: int32 [8192], P('dp'), may hold values 0 or 1
- owners: int32 [8192, 1], P('dp'), may hold values from 0 to 31; in each aligned block of 256 rows (0 to 255, 256 to 511, ...) at most 10 rows name the same one
Outputs:
- grad_weight: float32 [2048, 8192], P('dp', 'mp')
- grad_gain: float32 [8192], P('mp')
- slot_loss: float32 [10240], P('dp')
Inputs may be any that keep to these rules, and one draw needn't show every extreme that they name: `owners`: in the rows of one index of dp at most 10 name the same owner, a bound that some block reaches. `seq_lens`: in each index of dp some sequence has length exactly 128.
All inputs are finite; a program needn't handle non-finite values. No bound on the sum of `tool_mask` on one device may be relied on, other than what follows from the above.
Results may differ from a plain program's by a relative error of at most 0.0085.
Values may be sent and summed in bfloat16 or wider, within the bound.
No kernel may reach another device: no remote copies, remote signals or barrier semaphores. Data moves between devices by JAX's collectives and lax.ppermute only.
A program may use at most 64 MiB of HBM per device.

v0:
```python
import math

import jax
import jax.numpy as jnp
from jax import lax
from jax.sharding import Mesh, PartitionSpec as P


VOCAB = 32000
LEN = 128
CAP = 10
EPSILON = 1e-05
DP = ("a", "zh", "zl")
MP = ("x", "b", "c")


def exchange(value, axes):
    return lax.all_to_all(value, axes, split_axis=0, concat_axis=0, tiled=True)


def spread(value, axes):
    copies = lax.axis_size(axes)
    return exchange(jnp.broadcast_to(value[None], (copies,) + value.shape), axes)


def halves(value):
    high = value.astype(jnp.bfloat16)
    low = (value - high.astype(jnp.float32)).astype(jnp.bfloat16)
    return high, low


def flipped(value, axes):
    sizes = [lax.axis_size(axis) for axis in axes]
    last = math.prod(sizes) - 1
    return lax.ppermute(value, axes, [(k, last - k) for k in range(last + 1)])


def teacher_block(target_weight, a, zl, slab, width):
    x, b, c = (lax.axis_index(axis) for axis in MP)
    quarter = 4 * width

    def piece(column):
        return lax.dynamic_slice(target_weight, (zl * slab, column * quarter), (slab, quarter))

    def turn(swap):
        moves = []
        for k in range(8):
            side, at = divmod(k, 4)
            moves.append((k, at // 2 * 4 + 2 * side + (at % 2) ^ swap))
        return moves

    near = lax.ppermute(piece(2 * a + x % 2), ("a", "x"), turn(0))
    far = lax.ppermute(piece(2 * a + 1 - x % 2), ("a", "x"), turn(1))
    block = jnp.stack([near, far]).reshape(2, slab, 2, 2 * width)

    def halve(block, mine, axis):
        kept = lax.dynamic_index_in_dim(block, mine, axis=block.ndim - 2, keepdims=False)
        sent = lax.dynamic_index_in_dim(block, 1 - mine, axis=block.ndim - 2, keepdims=False)
        return kept, flipped(sent, (axis,))

    kept, came = halve(block, b, "b")
    block = jnp.stack([kept, came], axis=1).reshape(2, 2, slab, 2, width)
    kept, came = halve(block, c, "c")
    block = jnp.stack([kept, came], axis=2)
    block = jnp.where(x % 2 == 1, block[::-1], block)
    block = jnp.where(b == 1, block[:, ::-1], block)
    block = jnp.where(c == 1, block[:, :, ::-1], block)
    return block.reshape(8 * slab, width)


def softmax_parts(logit_rows):
    values = logit_rows.astype(jnp.float32)
    highest = jnp.max(values, axis=1)
    shifted = values - highest[:, None]
    expsum = jnp.exp(shifted)
    return highest, jnp.sum(expsum, axis=1), jnp.sum(expsum * shifted, axis=1)


def on_device(
    hidden,
    target_gain,
    target_weight,
    draft_gain,
    draft_weight,
    logits,
    seq_lens,
    tool_mask,
    owners,
):
    rows, width = hidden.shape
    features = target_gain.shape[0]
    models = lax.axis_size(MP)
    groups = lax.axis_size(DP)
    pairs = lax.axis_size("zh")
    quads = groups // pairs
    slab = draft_weight.shape[0]
    columns = pairs * slab
    all_rows = quads * rows
    mine = all_rows // models
    a, zl = lax.axis_index("a"), lax.axis_index("zl")
    model = lax.axis_index(MP)
    scale = 1.0 / math.sqrt(rows * groups)

    index = jnp.arange(rows, dtype=jnp.int32)
    length = jnp.where(index < LEN, seq_lens[0, 0], seq_lens[0, 1])
    valid = jnp.logical_and(index % LEN < length - 1, tool_mask == 1)
    owner = owners[:, 0]
    earlier = jnp.logical_and(
        owner[:, None] == owner[None, :], index[:, None] < index[None, :]
    )
    rank = jnp.sum(earlier.astype(jnp.int32), axis=0)
    highest, total, moment = softmax_parts(logits)
    total_high, total_low = halves(total)
    moment_high, moment_low = halves(moment)
    facts = jnp.stack(
        [
            highest.astype(jnp.bfloat16),
            total_high,
            total_low,
            moment_high,
            moment_low,
            valid.astype(jnp.bfloat16),
            owner.astype(jnp.bfloat16),
            rank.astype(jnp.bfloat16),
        ]
    )
    kinds = facts.shape[0]

    wd = spread(draft_weight, "zh").reshape(columns, width)
    carried = jnp.concatenate(
        [hidden, jnp.pad(facts, ((0, 0), (0, width - rows)))], axis=0
    )
    carried = jnp.stack(
        [carried] + [flipped(carried, axes) for axes in (("zl",), ("a",), ("a", "zl"))]
    )
    features_here = carried[:, :rows].reshape(all_rows, width)
    facts_here = carried[:, rows:, :rows]
    wt = teacher_block(target_weight, a, zl, slab, width)

    gain_slice = lax.dynamic_slice_in_dim(target_gain, model * width, width)
    wd_float = wd.astype(jnp.float32)
    merged = (wd_float * draft_gain - wt.astype(jnp.float32) * gain_slice).astype(jnp.bfloat16)
    partial = lax.dot_general(
        features_here, merged, (((1,), (1,)), ((), ())), preferred_element_type=jnp.float32
    ).astype(jnp.bfloat16)
    float_rows = features_here.astype(jnp.float32)
    squares = jnp.stack(halves(jnp.sum(float_rows * float_rows, axis=1))).reshape(2, models, mine)
    facts_here = facts_here.swapaxes(0, 1).reshape(kinds, models, mine)
    side = jnp.concatenate([facts_here, squares], axis=0).swapaxes(0, 1)
    side = side.reshape(models, 1, (kinds + 2) * mine)
    side = jnp.pad(side, ((0, 0), (0, 0), (0, 8 * columns - side.shape[2]))).reshape(models, 8, columns)
    got = exchange(
        jnp.concatenate([partial.reshape(models, mine, columns), side], axis=1), MP
    )
    summed = jnp.sum(got[:, :mine].astype(jnp.float32), axis=0)
    side = got[:, mine:].reshape(models, 8 * columns)[:, : (kinds + 2) * mine]
    side = side.reshape(models, kinds + 2, mine).astype(jnp.float32)
    peaks = side[:, 0]
    totals = side[:, 1] + side[:, 2]
    moments = side[:, 3] + side[:, 4]
    peak = jnp.max(peaks, axis=0)
    below = peaks - peak
    factor = jnp.exp(below)
    total = jnp.sum(factor * totals, axis=0)
    moment = jnp.sum(factor * (moments + below * totals), axis=0)
    entropy = jnp.log(total) - moment / total
    weight = (side[0, 5] * entropy / math.log(VOCAB)).astype(jnp.bfloat16).astype(jnp.float32)
    square = jnp.sum(side[:, 8] + side[:, 9], axis=0)
    inverse = lax.rsqrt(square / features + EPSILON)
    error = summed * inverse[:, None]
    loss = 0.5 * weight * jnp.sum(error * error, axis=1) * scale
    slope = (error * (weight * inverse * scale)[:, None]).astype(jnp.bfloat16)
    tail = jnp.concatenate(
        [jnp.stack(halves(loss)), side[0, 6:8].astype(jnp.bfloat16)], axis=0
    )
    tail = jnp.pad(tail, ((0, 4), (0, columns - mine)))
    got = spread(jnp.concatenate([slope, tail], axis=0), MP)
    slope = got[:, :mine].reshape(all_rows, columns)
    tail = got[:, mine : mine + 4, :mine].swapaxes(0, 1).reshape(4, all_rows)
    grad = lax.dot_general(
        slope, features_here, (((0,), (0,)), ((), ())), preferred_element_type=jnp.float32
    )
    gain = jnp.sum(grad * wd_float, axis=0)

    named = tail[2][None, :] == jnp.arange(groups, dtype=jnp.bfloat16)[:, None]
    quad = (jnp.arange(all_rows, dtype=jnp.int32) // rows) ^ (2 * a + zl)
    place = quad * CAP + tail[3].astype(jnp.int32)
    there = place[:, None] == jnp.arange(128, dtype=jnp.int32)[None, :]
    zero = jnp.zeros((), jnp.bfloat16)
    named = named.astype(jnp.bfloat16)
    slots = jnp.dot(
        jnp.concatenate([named, named], axis=1),
        jnp.concatenate(
            [jnp.where(there, tail[0][:, None], zero), jnp.where(there, tail[1][:, None], zero)],
            axis=0,
        ),
        preferred_element_type=jnp.float32,
    )
    parts = exchange(grad.astype(jnp.bfloat16).reshape(pairs, slab, width), "zh")
    small = jnp.concatenate([slots, gain.reshape(width // 128, 128), jnp.zeros((4, 128), jnp.float32)])
    small = lax.all_gather(small, DP)
    grad_weight = jnp.sum(parts.astype(jnp.float32), axis=0) * draft_gain
    grad_gain = jnp.sum(small[:, groups : groups + width // 128], axis=0).reshape(width)
    slots = lax.dynamic_index_in_dim(small, lax.axis_index(DP), axis=1, keepdims=False)[:, : quads * CAP]
    slots = jnp.sum(slots.reshape(2, pairs, 2, quads * CAP), axis=(0, 2))
    slots = slots.reshape(pairs, 2, 2, CAP).transpose(1, 0, 2, 3)
    return (grad_weight, grad_gain, slots.reshape(groups * CAP))


def solution(mesh):
    fine = Mesh(mesh.devices.reshape(2, 8, 2, 4, 2, 2), DP + MP)
    in_specs = (
        P(DP, MP),
        P(),
        P(MP, None),
        P(MP),
        P(DP, MP),
        P(DP, MP),
        P(DP, None),
        P(DP),
        P(DP, None),
    )
    out_specs = (P(DP, MP), P(MP), P(DP))

    return jax.shard_map(
        on_device, mesh=fine, in_specs=in_specs, out_specs=out_specs, check_vma=False
    )
```

profile of v0, /device:TPU:40, one launch (start us, length us, event | category | flops | bytes accessed | tf_op | source)
XLA Modules:
  0.0 209.7 jit_solution(18087724200200674181)
XLA Ops:
  0.7 1.1 fusion.54
  1.9 4.7 %collective-permute-start.4 = (bf16[64,2048]{1,0:T(8,128)(2,1)S(1)}, bf16[64,2048]{1,0:T(8,128)(2,1)S(1)}, u32[]{:S(2)}, u32[]{:S(2)}) collective-permute-start(bf16[64,2048]{1,0:T(8,128)(2,1)S(1)} %get-tuple-element.16), channel_id=1, source_target_pairs={{0,4},{4,0},{8,260},{12,256},{256,12},{260,8},{264,268},{268,264},... | collective-permute-start | bytes 786440 | tf_op jit(solution)/shard_map/ppermute | solution.py:53
  6.6 3.7 %collective-permute-start.3 = (bf16[64,2048]{1,0:T(8,128)(2,1)S(1)}, bf16[64,2048]{1,0:T(8,128)(2,1)}, u32[]{:S(2)}, u32[]{:S(2)}) collective-permute-start(bf16[64,2048]{1,0:T(8,128)(2,1)S(1)} %get-tuple-element.17), channel_id=1, source_target_pairs={{0,0},{4,4},{8,256},{12,260},{256,8},{260,12},{264,264},{268,268},... | collective-permute-start | bytes 786440 | tf_op jit(solution)/shard_map/ppermute | solution.py:52
  11.7 1.3 and_convert_fusion
  13.3 1.9 collective-permute-start.1
  15.2 2.8 %collective-permute-start = (bf16[264,512]{1,0:T(8,128)(2,1)S(1)}, bf16[264,512]{1,0:T(8,128)(2,1)S(1)}, u32[]{:S(2)}, u32[]{:S(2)}) collective-permute-start(bf16[264,512]{1,0:T(8,128)(2,1)S(1)} %get-tuple-element.25), channel_id=1, source_target_pairs={{0,16},{16,0},{1,17},{17,1},{2,18},{18,2},{3,19},{19,3},{4,20},{20... | collective-permute-start | bytes 811016 | tf_op jit(solution)/shard_map/ppermute | solution.py:35
  18.0 4.5 %collective-permute-start.2 = (bf16[264,512]{1,0:T(8,128)(2,1)S(1)}, bf16[264,512]{1,0:T(8,128)(2,1)S(1)}, u32[]{:S(2)}, u32[]{:S(2)}) collective-permute-start(bf16[264,512]{1,0:T(8,128)(2,1)S(1)} %get-tuple-element.25), channel_id=1, source_target_pairs={{0,272},{16,256},{256,16},{272,0},{1,273},{17,257},{257,17},{273,1... | collective-permute-start | bytes 811016 | tf_op jit(solution)/shard_map/ppermute | solution.py:35
  23.4 14.2 %all-to-all-start = ((bf16[8,64,512]{2,1,0:T(8,128)(2,1)}), bf16[8,64,512]{2,1,0:T(8,128)(2,1)S(1)}, u32[]{:S(2)}, u32[]{:S(2)}) async-start(bf16[8,64,512]{2,1,0:T(8,128)(2,1)} %broadcast_in_dim.59), calls=%async_computation | async-start | bytes 1048576 | tf_op jit(solution)/shard_map/all_to_all | solution.py:18
  38.3 1.1 stack.71
  40.1 2.2 %constant_dynamic-slice_fusion.3 = (bf16[2,64,1,1024]{3,2,1,0:T(2,128)(2,1)S(1)}, bf16[2,64,1024]{2,1,0:T(8,128)(2,1)S(1)}) fusion(bf16[2,64,2,1024]{3,2,1,0:T(2,128)(2,1)S(1)} %constant_dynamic-update-slice_fusion, s32[]{:T(128)S(6)} %select_n.98, s32[]{:T(128)S(6)} %select_n.97), kind=kLoop, calls=%fused_computation.96 | loop fusion | bytes 1048584 | tf_op jit(solution)/shard_map/jit(dynamic_index_in_dim)/dynamic_slice | solution.py:58
  42.5 4.2 %collective-permute-start.5 = (bf16[2,64,1024]{2,1,0:T(8,128)(2,1)S(1)}, bf16[2,64,1024]{2,1,0:T(8,128)(2,1)}, u32[]{:S(2)}, u32[]{:S(2)}) collective-permute-start(bf16[2,64,1024]{2,1,0:T(8,128)(2,1)S(1)} %bitcast.129), channel_id=1, source_target_pairs={{0,2},{2,0},{1,3},{3,1},{4,6},{6,4},{5,7},{7,5},{8,10},{10,8},{9,1... | collective-permute-start | bytes 786440 | tf_op jit(solution)/shard_map/ppermute | solution.py:35
  47.7 4.7 %collective-permute-done.5 = bf16[2,64,1024]{2,1,0:T(8,128)(2,1)} collective-permute-done((bf16[2,64,1024]{2,1,0:T(8,128)(2,1)S(1)}, bf16[2,64,1024]{2,1,0:T(8,128)(2,1)}, u32[]{:S(2)}, u32[]{:S(2)}) %collective-permute-start.5) | collective-permute-done | bytes 262176 | tf_op jit(solution)/shard_map/ppermute | solution.py:35
  52.4 1.1 stack.75
  53.8 1.1 constant_dynamic-slice_fusion.2
  54.9 1.9 collective-permute-start.6
  57.1 1.2 collective-permute-done.6
  58.9 5.6 %all-to-all-done = bf16[8,64,512]{2,1,0:T(8,128)(2,1)S(1)} async-done(((bf16[8,64,512]{2,1,0:T(8,128)(2,1)}), bf16[8,64,512]{2,1,0:T(8,128)(2,1)S(1)}, u32[]{:S(2)}, u32[]{:S(2)}) %all-to-all-start) | async-done | bytes 524320 | tf_op jit(solution)/shard_map/all_to_all | solution.py:18
  65.5 24.0 %all_to_all.20 = bf16[16,72,512]{2,1,0:T(8,128)(2,1)S(1)} all-to-all(bf16[16,72,512]{2,1,0:T(8,128)(2,1)S(1)} %pad_maximum_fusion), channel_id=1, replica_groups=mesh['a'=2,'zh'=8,'zl'=2,'x'=4,'b'=2,'c'=2] {'x','b','c'}, dimensions={0} | all-to-all | bytes 2359296 | tf_op jit(solution)/shard_map/all_to_all | solution.py:18
  90.3 1.1 broadcast_in_dim.60
  91.4 3.7 %all-to-all-start.2 = ((bf16[16,72,512]{2,1,0:T(8,128)(2,1)}), bf16[16,72,512]{2,1,0:T(8,128)(2,1)S(1)}, u32[]{:S(2)}, u32[]{:S(2)}) async-start(bf16[16,72,512]{2,1,0:T(8,128)(2,1)} %broadcast_in_dim.60), calls=%async_computation.2 | async-start | bytes 2359296 | tf_op jit(solution)/shard_map/all_to_all | solution.py:18
  95.2 19.2 %all-to-all-done.2 = bf16[16,72,512]{2,1,0:T(8,128)(2,1)S(1)} async-done(((bf16[16,72,512]{2,1,0:T(8,128)(2,1)}), bf16[16,72,512]{2,1,0:T(8,128)(2,1)S(1)}, u32[]{:S(2)}, u32[]{:S(2)}) %all-to-all-start.2) | async-done | bytes 1179680 | tf_op jit(solution)/shard_map/all_to_all | solution.py:18
  114.5 1.5 fusion.1
  116.0 6.9 %all-to-all-start.3 = ((bf16[8,64,512]{2,1,0:T(8,128)(2,1)}), bf16[8,64,512]{2,1,0:T(8,128)(2,1)S(1)}, u32[]{:S(2)}, u32[]{:S(2)}) async-start(bf16[8,64,512]{2,1,0:T(8,128)(2,1)} %bitcast.28), calls=%async_computation.3 | async-start | bytes 1048576 | tf_op jit(solution)/shard_map/all_to_all | solution.py:18
  124.2 83.3 %all-gather = f32[1280,128]{1,0:T(8,128)S(1)} all-gather(f32[40,128]{1,0:T(8,128)S(1)} %maximum_maximum_fusion), channel_id=2, replica_groups=mesh['a'=2,'zh'=8,'zl'=2,'x'=4,'b'=2,'c'=2] {'a','zh','zl'}, dimensions={0}, use_global_device_ids=true | all-gather | bytes 675840 | tf_op jit(solution)/shard_map/all_gather | solution.py:201
  (107 shorter events, 11.2 us)
Async XLA Ops:
  0.6 9.7 %copy-start = (bf16[256,2000]{0,1:T(8,128)(2,1)S(1)}, bf16[256,2000]{0,1:T(8,128)(2,1)}, u32[]{:S(2)}) copy-start(bf16[256,2000]{0,1:T(8,128)(2,1)} %param.14) | copy-start | bytes 3072004
  0.6 10.0 %copy-start.3 = (s32[256,1]{0,1:T(1,128)S(1)}, s32[256,1]{0,1:T(1,128)}, u32[]{:S(2)}) copy-start(s32[256,1]{0,1:T(1,128)} %param.17) | copy-start | bytes 3076
  1.8 9.3 %copy-start.5 = (s32[1,2]{1,0:T(1,128)S(1)}, s32[1,2]{1,0:T(1,128)}, u32[]{:S(2)}) copy-start(s32[1,2]{1,0:T(1,128)} %param.15) | copy-start | bytes 28
  1.8 9.9 %copy-start.6 = (s32[256]{0:T(256)S(1)}, s32[256]{0:T(256)}, u32[]{:S(2)}) copy-start(s32[256]{0:T(256)} %param.16) | copy-start | bytes 3076
  1.9 11.4 %copy-start.1 = (bf16[256,512]{1,0:T(8,128)(2,1)S(1)}, bf16[256,512]{1,0:T(8,128)(2,1)}, u32[]{:S(2)}) copy-start(bf16[256,512]{1,0:T(8,128)(2,1)} %param.9) | copy-start | bytes 786436
  1.9 37.8 %collective-permute-start.4 = (bf16[64,2048]{1,0:T(8,128)(2,1)S(1)}, bf16[64,2048]{1,0:T(8,128)(2,1)S(1)}, u32[]{:S(2)}, u32[]{:S(2)}) collective-permute-start(bf16[64,2048]{1,0:T(8,128)(2,1)S(1)} %get-tuple-element.16), channel_id=1, source_target_pairs={{0,4},{4,0},{8,260},{12,256},{256,12},{260,8},{264,268},{268,264},... | collective-permute-start | bytes 786440 | tf_op jit(solution)/shard_map/ppermute | solution.py:53
  6.6 31.8 %collective-permute-start.3 = (bf16[64,2048]{1,0:T(8,128)(2,1)S(1)}, bf16[64,2048]{1,0:T(8,128)(2,1)}, u32[]{:S(2)}, u32[]{:S(2)}) collective-permute-start(bf16[64,2048]{1,0:T(8,128)(2,1)S(1)} %get-tuple-element.17), channel_id=1, source_target_pairs={{0,0},{4,4},{8,256},{12,260},{256,8},{260,12},{264,264},{268,268},... | collective-permute-start | bytes 786440 | tf_op jit(solution)/shard_map/ppermute | solution.py:52
  10.6 12.0 %copy-start.2 = (bf16[64,512]{1,0:T(8,128)(2,1)S(1)}, bf16[64,512]{1,0:T(8,128)(2,1)}, u32[]{:S(2)}) copy-start(bf16[64,512]{1,0:T(8,128)(2,1)} %param.13) | copy-start | bytes 196612
  13.3 33.6 %collective-permute-start.1 = (bf16[264,512]{1,0:T(8,128)(2,1)S(1)}, bf16[264,512]{1,0:T(8,128)(2,1)S(1)}, u32[]{:S(2)}, u32[]{:S(2)}) collective-permute-start(bf16[264,512]{1,0:T(8,128)(2,1)S(1)} %get-tuple-element.25), channel_id=1, source_target_pairs={{0,256},{256,0},{1,257},{257,1},{2,258},{258,2},{3,259},{259,3},{4... | collective-permute-start | bytes 811016 | tf_op jit(solution)/shard_map/ppermute | solution.py:35
  15.2 31.7 %collective-permute-start = (bf16[264,512]{1,0:T(8,128)(2,1)S(1)}, bf16[264,512]{1,0:T(8,128)(2,1)S(1)}, u32[]{:S(2)}, u32[]{:S(2)}) collective-permute-start(bf16[264,512]{1,0:T(8,128)(2,1)S(1)} %get-tuple-element.25), channel_id=1, source_target_pairs={{0,16},{16,0},{1,17},{17,1},{2,18},{18,2},{3,19},{19,3},{4,20},{20... | collective-permute-start | bytes 811016 | tf_op jit(solution)/shard_map/ppermute | solution.py:35
  18.0 28.9 %collective-permute-start.2 = (bf16[264,512]{1,0:T(8,128)(2,1)S(1)}, bf16[264,512]{1,0:T(8,128)(2,1)S(1)}, u32[]{:S(2)}, u32[]{:S(2)}) collective-permute-start(bf16[264,512]{1,0:T(8,128)(2,1)S(1)} %get-tuple-element.25), channel_id=1, source_target_pairs={{0,272},{16,256},{256,16},{272,0},{1,273},{17,257},{257,17},{273,1... | collective-permute-start | bytes 811016 | tf_op jit(solution)/shard_map/ppermute | solution.py:35
  23.4 41.1 %all-to-all-start = ((bf16[8,64,512]{2,1,0:T(8,128)(2,1)}), bf16[8,64,512]{2,1,0:T(8,128)(2,1)S(1)}, u32[]{:S(2)}, u32[]{:S(2)}) async-start(bf16[8,64,512]{2,1,0:T(8,128)(2,1)} %broadcast_in_dim.59), calls=%async_computation | async-start | bytes 1048576 | tf_op jit(solution)/shard_map/all_to_all | solution.py:18
  42.5 9.9 %collective-permute-start.5 = (bf16[2,64,1024]{2,1,0:T(8,128)(2,1)S(1)}, bf16[2,64,1024]{2,1,0:T(8,128)(2,1)}, u32[]{:S(2)}, u32[]{:S(2)}) collective-permute-start(bf16[2,64,1024]{2,1,0:T(8,128)(2,1)S(1)} %bitcast.129), channel_id=1, source_target_pairs={{0,2},{2,0},{1,3},{3,1},{4,6},{6,4},{5,7},{7,5},{8,10},{10,8},{9,1... | collective-permute-start | bytes 786440 | tf_op jit(solution)/shard_map/ppermute | solution.py:35
  54.9 3.4 %collective-permute-start.6 = (bf16[2,2,64,512]{3,2,1,0:T(8,128)(2,1)S(1)}, bf16[2,2,64,512]{3,2,1,0:T(8,128)(2,1)S(1)}, u32[]{:S(2)}, u32[]{:S(2)}) collective-permute-start(bf16[2,2,64,512]{3,2,1,0:T(8,128)(2,1)S(1)} %bitcast.130), channel_id=1, source_target_pairs={{0,1},{1,0},{2,3},{3,2},{4,5},{5,4},{6,7},{7,6},{8,9},{9,8},{10,11... | collective-permute-start | bytes 786440 | tf_op jit(solution)/shard_map/ppermute | solution.py:35
  58.7 5.7 %copy-start.4 = (f32[512]{0:T(512)S(1)}, f32[512]{0:T(512)}, u32[]{:S(2)}) copy-start(f32[512]{0:T(512)} %param.12) | copy-start | bytes 6148
  91.4 23.0 %all-to-all-start.2 = ((bf16[16,72,512]{2,1,0:T(8,128)(2,1)}), bf16[16,72,512]{2,1,0:T(8,128)(2,1)S(1)}, u32[]{:S(2)}, u32[]{:S(2)}) async-start(bf16[16,72,512]{2,1,0:T(8,128)(2,1)} %broadcast_in_dim.60), calls=%async_computation.2 | async-start | bytes 2359296 | tf_op jit(solution)/shard_map/all_to_all | solution.py:18
  116.0 92.9 %all-to-all-start.3 = ((bf16[8,64,512]{2,1,0:T(8,128)(2,1)}), bf16[8,64,512]{2,1,0:T(8,128)(2,1)S(1)}, u32[]{:S(2)}, u32[]{:S(2)}) async-start(bf16[8,64,512]{2,1,0:T(8,128)(2,1)} %bitcast.28), calls=%async_computation.3 | async-start | bytes 1048576 | tf_op jit(solution)/shard_map/all_to_all | solution.py:18
where the time goes:
time: 210 us
  blocking collectives  107 us (51%)
  starting transfers between devices  48.5 us (23%)
  waiting for transfers between devices  30.8 us (15%)
  local copies, waits for them, and re-layouts  13.5 us (6%)
  other arithmetic  5.85 us (3%)
  matrix products  2.46 us (1%)
    all_gather x1, blocking collectives, on_device(): small = lax.all_gather(small, DP)  83.3 us
    all_to_all x3, waiting for transfers between devices, exchange(): return lax.all_to_all(value, axes, split_axis=0, concat_axis=0, tiled=True)  24.8 us
    all_to_all x3, starting transfers between devices, exchange(): return lax.all_to_all(value, axes, split_axis=0, concat_axis=0, tiled=True)  24.8 us
    all_to_all x1, blocking collectives, exchange(): return lax.all_to_all(value, axes, split_axis=0, concat_axis=0, tiled=True)  24 us
    ppermute x5, starting transfers between devices, flipped(): return lax.ppermute(value, axes, [(k, last - k) for k in range(last + 1)])  15.3 us
    ppermute x5, waiting for transfers between devices, flipped(): return lax.ppermute(value, axes, [(k, last - k) for k in range(last + 1)])  5.95 us
    ppermute x1, starting transfers between devices, teacher_block(): far = lax.ppermute(piece(2 * a + 1 - x % 2), ('a', 'x'), turn(1))  4.68 us
  transfers between devices with their start and end apart: 10, of which 4 were waited for; matrix products, arithmetic and copies ran while one was open for 7% of the time, Pallas kernels for 0%

commit v1 on v0

--- a/solution.py
+++ b/solution.py
@@ -3,6 +3,8 @@
 import jax
 import jax.numpy as jnp
 from jax import lax
+from jax.experimental import pallas as pl
+from jax.experimental.pallas import tpu as pltpu
 from jax.sharding import Mesh, PartitionSpec as P
 
 
@@ -51,21 +53,46 @@
 
     near = lax.ppermute(piece(2 * a + x % 2), ("a", "x"), turn(0))
     far = lax.ppermute(piece(2 * a + 1 - x % 2), ("a", "x"), turn(1))
-    block = jnp.stack([near, far]).reshape(2, slab, 2, 2 * width)
-
-    def halve(block, mine, axis):
-        kept = lax.dynamic_index_in_dim(block, mine, axis=block.ndim - 2, keepdims=False)
-        sent = lax.dynamic_index_in_dim(block, 1 - mine, axis=block.ndim - 2, keepdims=False)
-        return kept, flipped(sent, (axis,))
-
-    kept, came = halve(block, b, "b")
-    block = jnp.stack([kept, came], axis=1).reshape(2, 2, slab, 2, width)
-    kept, came = halve(block, c, "c")
-    block = jnp.stack([kept, came], axis=2)
-    block = jnp.where(x % 2 == 1, block[::-1], block)
-    block = jnp.where(b == 1, block[:, ::-1], block)
-    block = jnp.where(c == 1, block[:, :, ::-1], block)
-    return block.reshape(8 * slab, width)
+
+    def halve(parts, mine, axis):
+        half = parts[0].shape[1] // 2
+
+        def side(which):
+            return jnp.concatenate(
+                [lax.dynamic_slice_in_dim(part, which * half, half, axis=1) for part in parts]
+            )
+
+        return side(mine), flipped(side(1 - mine), (axis,))
+
+    parts = halve((near, far), b, "b")
+    parts = halve(parts, c, "c")
+    return [part.reshape(4, slab, width) for part in parts], 4 * (x % 2) + 2 * b + c
+
+
+def project(place, own, left, right, cross, wd, kept, came, gains, side, out):
+    slab = wd.shape[1]
+    mine = out.shape[1] - side.shape[1]
+    rows = 4 * mine
+    here = place[0]
+    draft_gain, target_gain = gains[0:1], gains[1:2]
+    for pair in range(4):
+        merged = []
+        for k in (2 * pair, 2 * pair + 1):
+            away = here ^ k
+            at = away // 2 % 2 * 2 + away // 4
+            parts = kept[at], came[at]
+            wt = jnp.where(away % 2 == 1, parts[1].astype(jnp.float32), parts[0].astype(jnp.float32))
+            merged.append(wd[k].astype(jnp.float32) * draft_gain - wt * target_gain)
+        merged = jnp.concatenate(merged).astype(jnp.bfloat16)
+        lanes = slice(pair * 2 * slab, (pair + 1) * 2 * slab)
+        for quad, block in enumerate((own, left, right, cross)):
+            value = lax.dot_general(
+                block[:rows], merged, (((1,), (1,)), ((), ())), preferred_element_type=jnp.float32
+            )
+            out[4 * quad : 4 * quad + 4, :mine, lanes] = value.astype(jnp.bfloat16).reshape(
+                4, mine, 2 * slab
+            )
+    out[:, mine:] = side[...]
 
 
 def softmax_parts(logit_rows):
@@ -130,28 +157,36 @@
     carried = jnp.concatenate(
         [hidden, jnp.pad(facts, ((0, 0), (0, width - rows)))], axis=0
     )
-    carried = jnp.stack(
-        [carried] + [flipped(carried, axes) for axes in (("zl",), ("a",), ("a", "zl"))]
-    )
+    blocks = [carried]
+    blocks += [flipped(carried, axes) for axes in (("zl",), ("a",), ("a", "zl"))]
+    carried = jnp.stack(blocks)
     features_here = carried[:, :rows].reshape(all_rows, width)
     facts_here = carried[:, rows:, :rows]
-    wt = teacher_block(target_weight, a, zl, slab, width)
+    (kept, came), place = teacher_block(target_weight, a, zl, slab, width)
 
     gain_slice = lax.dynamic_slice_in_dim(target_gain, model * width, width)
-    wd_float = wd.astype(jnp.float32)
-    merged = (wd_float * draft_gain - wt.astype(jnp.float32) * gain_slice).astype(jnp.bfloat16)
-    partial = lax.dot_general(
-        features_here, merged, (((1,), (1,)), ((), ())), preferred_element_type=jnp.float32
-    ).astype(jnp.bfloat16)
+    gains = jnp.stack([draft_gain, gain_slice])
     float_rows = features_here.astype(jnp.float32)
     squares = jnp.stack(halves(jnp.sum(float_rows * float_rows, axis=1))).reshape(2, models, mine)
     facts_here = facts_here.swapaxes(0, 1).reshape(kinds, models, mine)
     side = jnp.concatenate([facts_here, squares], axis=0).swapaxes(0, 1)
     side = side.reshape(models, 1, (kinds + 2) * mine)
     side = jnp.pad(side, ((0, 0), (0, 0), (0, 8 * columns - side.shape[2]))).reshape(models, 8, columns)
-    got = exchange(
-        jnp.concatenate([partial.reshape(models, mine, columns), side], axis=1), MP
-    )
+    partial = pl.pallas_call(
+        project,
+        out_shape=jax.ShapeDtypeStruct((models, mine + 8, columns), jnp.bfloat16),
+        in_specs=[pl.BlockSpec(memory_space=pltpu.SMEM)]
+        + [pl.BlockSpec(memory_space=pltpu.VMEM)] * 9,
+        out_specs=pl.BlockSpec(memory_space=pltpu.VMEM),
+        cost_estimate=pl.CostEstimate(
+            flops=2 * all_rows * width * columns,
+            bytes_accessed=2 * (2 * all_rows * width + 2 * columns * width),
+            transcendentals=0,
+        ),
+        compiler_params=pltpu.CompilerParams(vmem_limit_bytes=16 * 2**20),
+        name="project",
+    )(place.reshape(1), *blocks, wd.reshape(pairs, slab, width), kept, came, gains, side)
+    got = exchange(partial, MP)
     summed = jnp.sum(got[:, :mine].astype(jnp.float32), axis=0)
     side = got[:, mine:].reshape(models, 8 * columns)[:, : (kinds + 2) * mine]
     side = side.reshape(models, kinds + 2, mine).astype(jnp.float32)
@@ -180,7 +215,7 @@
     grad = lax.dot_general(
         slope, features_here, (((0,), (0,)), ((), ())), preferred_element_type=jnp.float32
     )
-    gain = jnp.sum(grad * wd_float, axis=0)
+    gain = jnp.sum(grad * wd.astype(jnp.float32), axis=0)
 
     named = tail[2][None, :] == jnp.arange(groups, dtype=jnp.bfloat16)[:, None]
     quad = (jnp.arange(all_rows, dtype=jnp.int32) // rows) ^ (2 * a + zl)
@@ -197,12 +232,29 @@
         preferred_element_type=jnp.float32,
     )
     parts = exchange(grad.astype(jnp.bfloat16).reshape(pairs, slab, width), "zh")
-    small = jnp.concatenate([slots, gain.reshape(width // 128, 128), jnp.zeros((4, 128), jnp.float32)])
-    small = lax.all_gather(small, DP)
+    slots = slots.reshape(2, pairs, 2, 128)
+
+    def toward(swap_a, swap_zl):
+        for_them = lax.dynamic_index_in_dim(slots, a ^ swap_a, axis=0, keepdims=False)
+        for_them = lax.dynamic_index_in_dim(for_them, zl ^ swap_zl, axis=1, keepdims=False)
+        return jnp.concatenate([for_them, gain.reshape(width // 128, 128)], axis=0)
+
+    small = toward(0, 0)
+    small += flipped(toward(0, 1), ("zl",))
+    small += flipped(toward(1, 0), ("a",))
+    small += flipped(toward(1, 1), ("a", "zl"))
+    zh = lax.axis_index("zh")
+    source = jnp.arange(pairs, dtype=jnp.int32)[:, None, None]
+    slots = jnp.where(source == zh, small[None, :pairs], 0.0).reshape(pairs * pairs, 128)
+    small = jnp.concatenate([slots, small[pairs:], jnp.zeros((4, 128), jnp.float32)], axis=0)
+    for step in (1, 2, 4):
+        moves = [(k, k ^ step) for k in range(pairs)]
+        small += lax.ppermute(small, "zh", moves)
     grad_weight = jnp.sum(parts.astype(jnp.float32), axis=0) * draft_gain
-    grad_gain = jnp.sum(small[:, groups : groups + width // 128], axis=0).reshape(width)
-    slots = lax.dynamic_index_in_dim(small, lax.axis_index(DP), axis=1, keepdims=False)[:, : quads * CAP]
-    slots = jnp.sum(slots.reshape(2, pairs, 2, quads * CAP), axis=(0, 2))
+    grad_gain = small[pairs * pairs : pairs * pairs + width // 128].reshape(width)
+    slots = lax.dynamic_index_in_dim(
+        small[: pairs * pairs].reshape(pairs, pairs, 128), zh, axis=1, keepdims=False
+    )[:, : quads * CAP]
     slots = slots.reshape(pairs, 2, 2, CAP).transpose(1, 0, 2, 3)
     return (grad_weight, grad_gain, slots.reshape(groups * CAP))
 

time: 210 us -> 191 us (0.910)
  the two profiles are of different devices: /device:TPU:40 before, /device:TPU:16 now
where the time goes in v1:
time: 191 us; the launch traced here: 190 us
  starting transfers between devices  84.9 us (44%)
  waiting for transfers between devices  61.7 us (32%)
  blocking collectives  21 us (11%)
  local copies, waits for them, and re-layouts  10.7 us (6%)
  other arithmetic  7.72 us (4%)
    all_to_all x3, starting transfers between devices, exchange(): return lax.all_to_all(value, axes, split_axis=0, concat_axis=0, tiled=True)  32.7 us
    ppermute x8, waiting for transfers between devices, flipped(): return lax.ppermute(value, axes, [(k, last - k) for k in range(last + 1)])  32 us
    ppermute x8, starting transfers between devices, flipped(): return lax.ppermute(value, axes, [(k, last - k) for k in range(last + 1)])  26.5 us
    all_to_all x1, blocking collectives, exchange(): return lax.all_to_all(value, axes, split_axis=0, concat_axis=0, tiled=True)  21 us
    ppermute x3, starting transfers between devices, on_device(): small += lax.ppermute(small, 'zh', moves)  20.7 us
    all_to_all x3, waiting for transfers between devices, exchange(): return lax.all_to_all(value, axes, split_axis=0, concat_axis=0, tiled=True)  16.4 us
    ppermute x3, waiting for transfers between devices, on_device(): small += lax.ppermute(small, 'zh', moves)  13.3 us
  transfers between devices with their start and end apart: 16, of which 9 were waited for; matrix products, arithmetic and copies ran while one was open for 8% of the time, Pallas kernels for 0%

profile of v1, /device:TPU:16, one launch (start us, length us, event | category | flops | bytes accessed | tf_op | source)
XLA Modules:
  0.0 190.3 jit_solution(13023442021822392313)
XLA Ops:
  1.9 3.5 %collective-permute-start.4 = (bf16[64,2048]{1,0:T(8,128)(2,1)S(1)}, bf16[64,2048]{1,0:T(8,128)(2,1)}, u32[]{:S(2)}, u32[]{:S(2)}) collective-permute-start(bf16[64,2048]{1,0:T(8,128)(2,1)S(1)} %get-tuple-element.19), channel_id=1, source_target_pairs={{0,4},{4,0},{8,260},{12,256},{256,12},{260,8},{264,268},{268,264},... | collective-permute-start | bytes 786440 | tf_op jit(solution)/shard_map/ppermute | solution.py:55
  8.5 15.2 %all-to-all-start = ((bf16[8,64,512]{2,1,0:T(8,128)(2,1)}), bf16[8,64,512]{2,1,0:T(8,128)(2,1)S(1)}, u32[]{:S(2)}, u32[]{:S(2)}) async-start(bf16[8,64,512]{2,1,0:T(8,128)(2,1)} %broadcast_in_dim.85), calls=%async_computation | async-start | bytes 1048576 | tf_op jit(solution)/shard_map/all_to_all | solution.py:20
  26.7 2.9 %collective-permute-start = (bf16[264,512]{1,0:T(8,128)(2,1)S(1)}, bf16[264,512]{1,0:T(8,128)(2,1)S(1)}, u32[]{:S(2)}, u32[]{:S(2)}) collective-permute-start(bf16[264,512]{1,0:T(8,128)(2,1)S(1)} %get-tuple-element.23.own), channel_id=1, source_target_pairs={{0,16},{16,0},{1,17},{17,1},{2,18},{18,2},{3,19},{19,3},{4,20},{20... | collective-permute-start | bytes 811016 | tf_op jit(solution)/shard_map/ppermute | solution.py:37
  29.6 6.7 %collective-permute-start.1 = (bf16[264,512]{1,0:T(8,128)(2,1)S(1)}, bf16[264,512]{1,0:T(8,128)(2,1)S(1)}, u32[]{:S(2)}, u32[]{:S(2)}) collective-permute-start(bf16[264,512]{1,0:T(8,128)(2,1)S(1)} %get-tuple-element.23.own), channel_id=1, source_target_pairs={{0,256},{256,0},{1,257},{257,1},{2,258},{258,2},{3,259},{259,3},{4... | collective-permute-start | bytes 811016 | tf_op jit(solution)/shard_map/ppermute | solution.py:37
  36.3 2.4 %collective-permute-start.2 = (bf16[264,512]{1,0:T(8,128)(2,1)S(1)}, bf16[264,512]{1,0:T(8,128)(2,1)S(1)}, u32[]{:S(2)}, u32[]{:S(2)}) collective-permute-start(bf16[264,512]{1,0:T(8,128)(2,1)S(1)} %get-tuple-element.23.own), channel_id=1, source_target_pairs={{0,272},{16,256},{256,16},{272,0},{1,273},{17,257},{257,17},{273,1... | collective-permute-start | bytes 811016 | tf_op jit(solution)/shard_map/ppermute | solution.py:37
  42.2 2.5 %collective-permute-start.5 = (bf16[128,1024]{1,0:T(8,128)(2,1)}, bf16[128,1024]{1,0:T(8,128)(2,1)S(1)}, u32[]{:S(2)}, u32[]{:S(2)}) collective-permute-start(bf16[128,1024]{1,0:T(8,128)(2,1)} %pad_maximum_fusion.3), channel_id=1, source_target_pairs={{0,2},{2,0},{1,3},{3,1},{4,6},{6,4},{5,7},{7,5},{8,10},{10,8},{9,1... | collective-permute-start | bytes 786440 | tf_op jit(solution)/shard_map/ppermute | solution.py:37
  45.4 9.3 %collective-permute-done.left = bf16[264,512]{1,0:T(8,128)(2,1)S(1)} collective-permute-done((bf16[264,512]{1,0:T(8,128)(2,1)S(1)}, bf16[264,512]{1,0:T(8,128)(2,1)S(1)}, u32[]{:S(2)}, u32[]{:S(2)}) %collective-permute-start) | collective-permute-done | bytes 270368 | tf_op jit(solution)/shard_map/ppermute | solution.py:37
  54.7 8.4 %collective-permute-done.2.cross = bf16[264,512]{1,0:T(8,128)(2,1)S(1)} collective-permute-done((bf16[264,512]{1,0:T(8,128)(2,1)S(1)}, bf16[264,512]{1,0:T(8,128)(2,1)S(1)}, u32[]{:S(2)}, u32[]{:S(2)}) %collective-permute-start.2) | collective-permute-done | bytes 270368 | tf_op jit(solution)/shard_map/ppermute | solution.py:37
  64.8 1.9 %collective-permute-start.6 = (bf16[256,512]{1,0:T(8,128)(2,1)}, bf16[256,512]{1,0:T(8,128)(2,1)S(1)}, u32[]{:S(2)}, u32[]{:S(2)}) collective-permute-start(bf16[256,512]{1,0:T(8,128)(2,1)} %pad_maximum_fusion.5), channel_id=1, source_target_pairs={{0,1},{1,0},{2,3},{3,2},{4,5},{5,4},{6,7},{7,6},{8,9},{9,8},{10,11... | collective-permute-start | bytes 786440 | tf_op jit(solution)/shard_map/ppermute | solution.py:37
  69.8 21.0 %all_to_all.20 = bf16[16,72,512]{2,1,0:T(8,128)(2,1)S(1)} all-to-all(bf16[16,72,512]{2,1,0:T(8,128)(2,1)S(1)} %project.1), channel_id=1, replica_groups=mesh['a'=2,'zh'=8,'zl'=2,'x'=4,'b'=2,'c'=2] {'x','b','c'}, dimensions={0} | all-to-all | bytes 2359296 | tf_op jit(solution)/shard_map/all_to_all | solution.py:20
  92.6 6.3 %all-to-all-start.2 = ((bf16[16,72,512]{2,1,0:T(8,128)(2,1)}), bf16[16,72,512]{2,1,0:T(8,128)(2,1)S(1)}, u32[]{:S(2)}, u32[]{:S(2)}) async-start(bf16[16,72,512]{2,1,0:T(8,128)(2,1)} %broadcast_in_dim.86), calls=%async_computation.2 | async-start | bytes 2359296 | tf_op jit(solution)/shard_map/all_to_all | solution.py:20
  98.9 16.4 %all-to-all-done.2 = bf16[16,72,512]{2,1,0:T(8,128)(2,1)S(1)} async-done(((bf16[16,72,512]{2,1,0:T(8,128)(2,1)}), bf16[16,72,512]{2,1,0:T(8,128)(2,1)S(1)}, u32[]{:S(2)}, u32[]{:S(2)}) %all-to-all-start.2) | async-done | bytes 1179680 | tf_op jit(solution)/shard_map/all_to_all | solution.py:20
  117.4 11.2 %all-to-all-start.3 = ((bf16[8,64,512]{2,1,0:T(8,128)(2,1)}), bf16[8,64,512]{2,1,0:T(8,128)(2,1)S(1)}, u32[]{:S(2)}, u32[]{:S(2)}) async-start(bf16[8,64,512]{2,1,0:T(8,128)(2,1)} %bitcast.27), calls=%async_computation.3 | async-start | bytes 1048576 | tf_op jit(solution)/shard_map/all_to_all | solution.py:20
  129.4 2.9 %collective-permute-start.7 = (f32[12,128]{1,0:T(8,128)S(1)}, f32[12,128]{1,0:T(8,128)S(1)}, u32[]{:S(2)}, u32[]{:S(2)}) collective-permute-start(f32[12,128]{1,0:T(8,128)S(1)} %get-tuple-element.45), channel_id=1, source_target_pairs={{0,16},{16,0},{1,17},{17,1},{2,18},{18,2},{3,19},{19,3},{4,20},{20... | collective-permute-start | bytes 18440 | tf_op jit(solution)/shard_map/ppermute | solution.py:37
  132.3 4.8 %collective-permute-start.8 = (f32[12,128]{1,0:T(8,128)S(1)}, f32[12,128]{1,0:T(8,128)S(1)}, u32[]{:S(2)}, u32[]{:S(2)}) collective-permute-start(f32[12,128]{1,0:T(8,128)S(1)} %get-tuple-element.46), channel_id=1, source_target_pairs={{0,256},{256,0},{1,257},{257,1},{2,258},{258,2},{3,259},{259,3},{4... | collective-permute-start | bytes 18440 | tf_op jit(solution)/shard_map/ppermute | solution.py:37
  137.2 2.4 %collective-permute-start.9 = (f32[12,128]{1,0:T(8,128)S(1)}, f32[12,128]{1,0:T(8,128)S(1)}, u32[]{:S(2)}, u32[]{:S(2)}) collective-permute-start(f32[12,128]{1,0:T(8,128)S(1)} %get-tuple-element.47), channel_id=1, source_target_pairs={{0,272},{16,256},{256,16},{272,0},{1,273},{17,257},{257,17},{273,1... | collective-permute-start | bytes 18440 | tf_op jit(solution)/shard_map/ppermute | solution.py:37
  139.8 11.2 %collective-permute-done.7 = f32[12,128]{1,0:T(8,128)S(1)} collective-permute-done((f32[12,128]{1,0:T(8,128)S(1)}, f32[12,128]{1,0:T(8,128)S(1)}, u32[]{:S(2)}, u32[]{:S(2)}) %collective-permute-start.7) | collective-permute-done | bytes 6176 | tf_op jit(solution)/shard_map/ppermute | solution.py:37
  151.0 2.8 %collective-permute-done.9 = f32[12,128]{1,0:T(8,128)S(1)} collective-permute-done((f32[12,128]{1,0:T(8,128)S(1)}, f32[12,128]{1,0:T(8,128)S(1)}, u32[]{:S(2)}, u32[]{:S(2)}) %collective-permute-start.9) | collective-permute-done | bytes 6176 | tf_op jit(solution)/shard_map/ppermute | solution.py:37
  153.9 1.9 %collective-permute-start.10 = (f32[72,128]{1,0:T(8,128)S(1)}, f32[72,128]{1,0:T(8,128)S(1)}, u32[]{:S(2)}, u32[]{:S(2)}) collective-permute-start(f32[72,128]{1,0:T(8,128)S(1)} %maximum_maximum_fusion), channel_id=1, source_target_pairs={{0,32},{32,0},{64,96},{96,64},{128,160},{160,128},{192,224},{224,1... | collective-permute-start | bytes 110600 | tf_op jit(solution)/shard_map/ppermute | solution.py:252
  155.9 5.8 %collective-permute-done.10 = f32[72,128]{1,0:T(8,128)S(1)} collective-permute-done((f32[72,128]{1,0:T(8,128)S(1)}, f32[72,128]{1,0:T(8,128)S(1)}, u32[]{:S(2)}, u32[]{:S(2)}) %collective-permute-start.10) | collective-permute-done | bytes 36896 | tf_op jit(solution)/shard_map/ppermute | solution.py:252
  161.7 4.9 %collective-permute-start.11 = (f32[72,128]{1,0:T(8,128)S(1)}, f32[72,128]{1,0:T(8,128)S(1)}, u32[]{:S(2)}, u32[]{:S(2)}) collective-permute-start(f32[72,128]{1,0:T(8,128)S(1)} %fusion.53), channel_id=1, source_target_pairs={{0,64},{32,96},{64,0},{96,32},{128,192},{160,224},{192,128},{224,1... | collective-permute-start | bytes 110600 | tf_op jit(solution)/shard_map/ppermute | solution.py:252
  166.6 5.2 %collective-permute-done.11 = f32[72,128]{1,0:T(8,128)S(1)} collective-permute-done((f32[72,128]{1,0:T(8,128)S(1)}, f32[72,128]{1,0:T(8,128)S(1)}, u32[]{:S(2)}, u32[]{:S(2)}) %collective-permute-start.11) | collective-permute-done | bytes 36896 | tf_op jit(solution)/shard_map/ppermute | solution.py:252
  171.8 13.9 %collective-permute-start.12 = (f32[72,128]{1,0:T(8,128)S(1)}, f32[72,128]{1,0:T(8,128)S(1)}, u32[]{:S(2)}, u32[]{:S(2)}) collective-permute-start(f32[72,128]{1,0:T(8,128)S(1)} %add.203), channel_id=1, source_target_pairs={{0,128},{32,160},{64,192},{96,224},{128,0},{160,32},{192,64},{224,... | collective-permute-start | bytes 110600 | tf_op jit(solution)/shard_map/ppermute | solution.py:252
  185.8 2.3 %collective-permute-done.12 = f32[72,128]{1,0:T(8,128)S(1)} collective-permute-done((f32[72,128]{1,0:T(8,128)S(1)}, f32[72,128]{1,0:T(8,128)S(1)}, u32[]{:S(2)}, u32[]{:S(2)}) %collective-permute-start.12) | collective-permute-done | bytes 36896 | tf_op jit(solution)/shard_map/ppermute | solution.py:252
  (114 shorter events, 23.2 us)
Async XLA Ops:
  0.6 23.0 %copy-start = (bf16[256,2000]{0,1:T(8,128)(2,1)S(1)}, bf16[256,2000]{0,1:T(8,128)(2,1)}, u32[]{:S(2)}) copy-start(bf16[256,2000]{0,1:T(8,128)(2,1)} %param.14) | copy-start | bytes 3072004
  1.8 22.7 %copy-start.4 = (s32[1,2]{1,0:T(1,128)S(1)}, s32[1,2]{1,0:T(1,128)}, u32[]{:S(2)}) copy-start(s32[1,2]{1,0:T(1,128)} %param.15) | copy-start | bytes 28
  1.8 23.2 %copy-start.2 = (s32[256,1]{0,1:T(1,128)S(1)}, s32[256,1]{0,1:T(1,128)}, u32[]{:S(2)}) copy-start(s32[256,1]{0,1:T(1,128)} %param.17) | copy-start | bytes 3076
  1.8 23.2 %copy-start.5 = (s32[256]{0:T(256)S(1)}, s32[256]{0:T(256)}, u32[]{:S(2)}) copy-start(s32[256]{0:T(256)} %param.16) | copy-start | bytes 3076
  1.9 24.8 %copy-start.1 = (bf16[256,512]{1,0:T(8,128)(2,1)S(1)}, bf16[256,512]{1,0:T(8,128)(2,1)}, u32[]{:S(2)}) copy-start(bf16[256,512]{1,0:T(8,128)(2,1)} %param.9) | copy-start | bytes 786436
  1.9 37.6 %collective-permute-start.4 = (bf16[64,2048]{1,0:T(8,128)(2,1)S(1)}, bf16[64,2048]{1,0:T(8,128)(2,1)}, u32[]{:S(2)}, u32[]{:S(2)}) collective-permute-start(bf16[64,2048]{1,0:T(8,128)(2,1)S(1)} %get-tuple-element.19), channel_id=1, source_target_pairs={{0,4},{4,0},{8,260},{12,256},{256,12},{260,8},{264,268},{268,264},... | collective-permute-start | bytes 786440 | tf_op jit(solution)/shard_map/ppermute | solution.py:55
  5.4 35.1 %collective-permute-start.3 = (bf16[64,2048]{1,0:T(8,128)(2,1)S(1)}, bf16[64,2048]{1,0:T(8,128)(2,1)}, u32[]{:S(2)}, u32[]{:S(2)}) collective-permute-start(bf16[64,2048]{1,0:T(8,128)(2,1)S(1)} %get-tuple-element.18), channel_id=1, source_target_pairs={{0,0},{4,4},{8,256},{12,260},{256,8},{260,12},{264,264},{268,268},... | collective-permute-start | bytes 786440 | tf_op jit(solution)/shard_map/ppermute | solution.py:54
  8.5 31.0 %copy-start.3 = (f32[512]{0:T(512)S(1)}, f32[512]{0:T(512)}, u32[]{:S(2)}) copy-start(f32[512]{0:T(512)} %param.12) | copy-start | bytes 6148
  8.5 60.0 %all-to-all-start = ((bf16[8,64,512]{2,1,0:T(8,128)(2,1)}), bf16[8,64,512]{2,1,0:T(8,128)(2,1)S(1)}, u32[]{:S(2)}, u32[]{:S(2)}) async-start(bf16[8,64,512]{2,1,0:T(8,128)(2,1)} %broadcast_in_dim.85), calls=%async_computation | async-start | bytes 1048576 | tf_op jit(solution)/shard_map/all_to_all | solution.py:20
  26.7 28.0 %collective-permute-start = (bf16[264,512]{1,0:T(8,128)(2,1)S(1)}, bf16[264,512]{1,0:T(8,128)(2,1)S(1)}, u32[]{:S(2)}, u32[]{:S(2)}) collective-permute-start(bf16[264,512]{1,0:T(8,128)(2,1)S(1)} %get-tuple-element.23.own), channel_id=1, source_target_pairs={{0,16},{16,0},{1,17},{17,1},{2,18},{18,2},{3,19},{19,3},{4,20},{20... | collective-permute-start | bytes 811016 | tf_op jit(solution)/shard_map/ppermute | solution.py:37
  29.6 25.1 %collective-permute-start.1 = (bf16[264,512]{1,0:T(8,128)(2,1)S(1)}, bf16[264,512]{1,0:T(8,128)(2,1)S(1)}, u32[]{:S(2)}, u32[]{:S(2)}) collective-permute-start(bf16[264,512]{1,0:T(8,128)(2,1)S(1)} %get-tuple-element.23.own), channel_id=1, source_target_pairs={{0,256},{256,0},{1,257},{257,1},{2,258},{258,2},{3,259},{259,3},{4... | collective-permute-start | bytes 811016 | tf_op jit(solution)/shard_map/ppermute | solution.py:37
  36.3 26.8 %collective-permute-start.2 = (bf16[264,512]{1,0:T(8,128)(2,1)S(1)}, bf16[264,512]{1,0:T(8,128)(2,1)S(1)}, u32[]{:S(2)}, u32[]{:S(2)}) collective-permute-start(bf16[264,512]{1,0:T(8,128)(2,1)S(1)} %get-tuple-element.23.own), channel_id=1, source_target_pairs={{0,272},{16,256},{256,16},{272,0},{1,273},{17,257},{257,17},{273,1... | collective-permute-start | bytes 811016 | tf_op jit(solution)/shard_map/ppermute | solution.py:37
  42.2 21.2 %collective-permute-start.5 = (bf16[128,1024]{1,0:T(8,128)(2,1)}, bf16[128,1024]{1,0:T(8,128)(2,1)S(1)}, u32[]{:S(2)}, u32[]{:S(2)}) collective-permute-start(bf16[128,1024]{1,0:T(8,128)(2,1)} %pad_maximum_fusion.3), channel_id=1, source_target_pairs={{0,2},{2,0},{1,3},{3,1},{4,6},{6,4},{5,7},{7,5},{8,10},{10,8},{9,1... | collective-permute-start | bytes 786440 | tf_op jit(solution)/shard_map/ppermute | solution.py:37
  64.8 3.6 %collective-permute-start.6 = (bf16[256,512]{1,0:T(8,128)(2,1)}, bf16[256,512]{1,0:T(8,128)(2,1)S(1)}, u32[]{:S(2)}, u32[]{:S(2)}) collective-permute-start(bf16[256,512]{1,0:T(8,128)(2,1)} %pad_maximum_fusion.5), channel_id=1, source_target_pairs={{0,1},{1,0},{2,3},{3,2},{4,5},{5,4},{6,7},{7,6},{8,9},{9,8},{10,11... | collective-permute-start | bytes 786440 | tf_op jit(solution)/shard_map/ppermute | solution.py:37
  92.6 22.7 %all-to-all-start.2 = ((bf16[16,72,512]{2,1,0:T(8,128)(2,1)}), bf16[16,72,512]{2,1,0:T(8,128)(2,1)S(1)}, u32[]{:S(2)}, u32[]{:S(2)}) async-start(bf16[16,72,512]{2,1,0:T(8,128)(2,1)} %broadcast_in_dim.86), calls=%async_computation.2 | async-start | bytes 2359296 | tf_op jit(solution)/shard_map/all_to_all | solution.py:20
  117.4 72.1 %all-to-all-start.3 = ((bf16[8,64,512]{2,1,0:T(8,128)(2,1)}), bf16[8,64,512]{2,1,0:T(8,128)(2,1)S(1)}, u32[]{:S(2)}, u32[]{:S(2)}) async-start(bf16[8,64,512]{2,1,0:T(8,128)(2,1)} %bitcast.27), calls=%async_computation.3 | async-start | bytes 1048576 | tf_op jit(solution)/shard_map/all_to_all | solution.py:20
  129.4 21.5 %collective-permute-start.7 = (f32[12,128]{1,0:T(8,128)S(1)}, f32[12,128]{1,0:T(8,128)S(1)}, u32[]{:S(2)}, u32[]{:S(2)}) collective-permute-start(f32[12,128]{1,0:T(8,128)S(1)} %get-tuple-element.45), channel_id=1, source_target_pairs={{0,16},{16,0},{1,17},{17,1},{2,18},{18,2},{3,19},{19,3},{4,20},{20... | collective-permute-start | bytes 18440 | tf_op jit(solution)/shard_map/ppermute | solution.py:37
  132.3 18.6 %collective-permute-start.8 = (f32[12,128]{1,0:T(8,128)S(1)}, f32[12,128]{1,0:T(8,128)S(1)}, u32[]{:S(2)}, u32[]{:S(2)}) collective-permute-start(f32[12,128]{1,0:T(8,128)S(1)} %get-tuple-element.46), channel_id=1, source_target_pairs={{0,256},{256,0},{1,257},{257,1},{2,258},{258,2},{3,259},{259,3},{4... | collective-permute-start | bytes 18440 | tf_op jit(solution)/shard_map/ppermute | solution.py:37
  137.2 16.6 %collective-permute-start.9 = (f32[12,128]{1,0:T(8,128)S(1)}, f32[12,128]{1,0:T(8,128)S(1)}, u32[]{:S(2)}, u32[]{:S(2)}) collective-permute-start(f32[12,128]{1,0:T(8,128)S(1)} %get-tuple-element.47), channel_id=1, source_target_pairs={{0,272},{16,256},{256,16},{272,0},{1,273},{17,257},{257,17},{273,1... | collective-permute-start | bytes 18440 | tf_op jit(solution)/shard_map/ppermute | solution.py:37
  153.9 7.7 %collective-permute-start.10 = (f32[72,128]{1,0:T(8,128)S(1)}, f32[72,128]{1,0:T(8,128)S(1)}, u32[]{:S(2)}, u32[]{:S(2)}) collective-permute-start(f32[72,128]{1,0:T(8,128)S(1)} %maximum_maximum_fusion), channel_id=1, source_target_pairs={{0,32},{32,0},{64,96},{96,64},{128,160},{160,128},{192,224},{224,1... | collective-permute-start | bytes 110600 | tf_op jit(solution)/shard_map/ppermute | solution.py:252
  161.7 10.1 %collective-permute-start.11 = (f32[72,128]{1,0:T(8,128)S(1)}, f32[72,128]{1,0:T(8,128)S(1)}, u32[]{:S(2)}, u32[]{:S(2)}) collective-permute-start(f32[72,128]{1,0:T(8,128)S(1)} %fusion.53), channel_id=1, source_target_pairs={{0,64},{32,96},{64,0},{96,32},{128,192},{160,224},{192,128},{224,1... | collective-permute-start | bytes 110600 | tf_op jit(solution)/shard_map/ppermute | solution.py:252
  171.8 16.3 %collective-permute-start.12 = (f32[72,128]{1,0:T(8,128)S(1)}, f32[72,128]{1,0:T(8,128)S(1)}, u32[]{:S(2)}, u32[]{:S(2)}) collective-permute-start(f32[72,128]{1,0:T(8,128)S(1)} %add.203), channel_id=1, source_target_pairs={{0,128},{32,160},{64,192},{96,224},{128,0},{160,32},{192,64},{224,... | collective-permute-start | bytes 110600 | tf_op jit(solution)/shard_map/ppermute | solution.py:252

commit v2 on v1

--- a/solution.py
+++ b/solution.py
@@ -69,10 +69,9 @@
     return [part.reshape(4, slab, width) for part in parts], 4 * (x % 2) + 2 * b + c
 
 
-def project(place, own, left, right, cross, wd, kept, came, gains, side, out):
+def project(place, near, far, wd, kept, came, gains, side, out):
     slab = wd.shape[1]
     mine = out.shape[1] - side.shape[1]
-    rows = 4 * mine
     here = place[0]
     draft_gain, target_gain = gains[0:1], gains[1:2]
     for pair in range(4):
@@ -85,12 +84,12 @@
             merged.append(wd[k].astype(jnp.float32) * draft_gain - wt * target_gain)
         merged = jnp.concatenate(merged).astype(jnp.bfloat16)
         lanes = slice(pair * 2 * slab, (pair + 1) * 2 * slab)
-        for quad, block in enumerate((own, left, right, cross)):
+        for half, block in enumerate((near, far)):
             value = lax.dot_general(
-                block[:rows], merged, (((1,), (1,)), ((), ())), preferred_element_type=jnp.float32
+                block[...], merged, (((1,), (1,)), ((), ())), preferred_element_type=jnp.float32
             )
-            out[4 * quad : 4 * quad + 4, :mine, lanes] = value.astype(jnp.bfloat16).reshape(
-                4, mine, 2 * slab
+            out[8 * half : 8 * half + 8, :mine, lanes] = value.astype(jnp.bfloat16).reshape(
+                8, mine, 2 * slab
             )
     out[:, mine:] = side[...]
 
@@ -154,14 +153,11 @@
     kinds = facts.shape[0]
 
     wd = spread(draft_weight, "zh").reshape(columns, width)
-    carried = jnp.concatenate(
-        [hidden, jnp.pad(facts, ((0, 0), (0, width - rows)))], axis=0
-    )
-    blocks = [carried]
-    blocks += [flipped(carried, axes) for axes in (("zl",), ("a",), ("a", "zl"))]
-    carried = jnp.stack(blocks)
-    features_here = carried[:, :rows].reshape(all_rows, width)
-    facts_here = carried[:, rows:, :rows]
+    near = jnp.concatenate([hidden, flipped(hidden, ("a",))], axis=0)
+    far = flipped(near, ("zl",))
+    facts_here = jnp.stack([facts, flipped(facts, ("a",))])
+    facts_here = jnp.concatenate([facts_here, flipped(facts_here, ("zl",))], axis=0)
+    features_here = jnp.concatenate([near, far], axis=0)
     (kept, came), place = teacher_block(target_weight, a, zl, slab, width)
 
     gain_slice = lax.dynamic_slice_in_dim(target_gain, model * width, width)
@@ -176,7 +172,7 @@
         project,
         out_shape=jax.ShapeDtypeStruct((models, mine + 8, columns), jnp.bfloat16),
         in_specs=[pl.BlockSpec(memory_space=pltpu.SMEM)]
-        + [pl.BlockSpec(memory_space=pltpu.VMEM)] * 9,
+        + [pl.BlockSpec(memory_space=pltpu.VMEM)] * 7,
         out_specs=pl.BlockSpec(memory_space=pltpu.VMEM),
         cost_estimate=pl.CostEstimate(
             flops=2 * all_rows * width * columns,
@@ -185,7 +181,7 @@
         ),
         compiler_params=pltpu.CompilerParams(vmem_limit_bytes=16 * 2**20),
         name="project",
-    )(place.reshape(1), *blocks, wd.reshape(pairs, slab, width), kept, came, gains, side)
+    )(place.reshape(1), near, far, wd.reshape(pairs, slab, width), kept, came, gains, side)
     got = exchange(partial, MP)
     summed = jnp.sum(got[:, :mine].astype(jnp.float32), axis=0)
     side = got[:, mine:].reshape(models, 8 * columns)[:, : (kinds + 2) * mine]
@@ -218,7 +214,8 @@
     gain = jnp.sum(grad * wd.astype(jnp.float32), axis=0)
 
     named = tail[2][None, :] == jnp.arange(groups, dtype=jnp.bfloat16)[:, None]
-    quad = (jnp.arange(all_rows, dtype=jnp.int32) // rows) ^ (2 * a + zl)
+    block = jnp.arange(all_rows, dtype=jnp.int32) // rows
+    quad = 2 * (a ^ (block % 2)) + (zl ^ (block // 2))
     place = quad * CAP + tail[3].astype(jnp.int32)
     there = place[:, None] == jnp.arange(128, dtype=jnp.int32)[None, :]
     zero = jnp.zeros((), jnp.bfloat16)
@@ -231,7 +228,6 @@
         ),
         preferred_element_type=jnp.float32,
     )
-    parts = exchange(grad.astype(jnp.bfloat16).reshape(pairs, slab, width), "zh")
     slots = slots.reshape(2, pairs, 2, 128)
 
     def toward(swap_a, swap_zl):
@@ -243,18 +239,19 @@
     small += flipped(toward(0, 1), ("zl",))
     small += flipped(toward(1, 0), ("a",))
     small += flipped(toward(1, 1), ("a", "zl"))
-    zh = lax.axis_index("zh")
-    source = jnp.arange(pairs, dtype=jnp.int32)[:, None, None]
-    slots = jnp.where(source == zh, small[None, :pairs], 0.0).reshape(pairs * pairs, 128)
-    small = jnp.concatenate([slots, small[pairs:], jnp.zeros((4, 128), jnp.float32)], axis=0)
-    for step in (1, 2, 4):
-        moves = [(k, k ^ step) for k in range(pairs)]
-        small += lax.ppermute(small, "zh", moves)
-    grad_weight = jnp.sum(parts.astype(jnp.float32), axis=0) * draft_gain
-    grad_gain = small[pairs * pairs : pairs * pairs + width // 128].reshape(width)
-    slots = lax.dynamic_index_in_dim(
-        small[: pairs * pairs].reshape(pairs, pairs, 128), zh, axis=1, keepdims=False
-    )[:, : quads * CAP]
+    gain_halves = [half.reshape(1, width) for half in halves(small[pairs:])]
+    extra = jnp.broadcast_to(jnp.concatenate(gain_halves)[None], (pairs, 2, width))
+    slot_halves = jnp.concatenate(halves(small[:pairs]), axis=1)[:, None]
+    extra = jnp.concatenate([extra, jnp.pad(slot_halves, ((0, 0), (0, 0), (0, width - 256)))], axis=1)
+    extra = jnp.pad(extra, ((0, 0), (0, 5), (0, 0)))
+    parts = exchange(
+        jnp.concatenate([grad.astype(jnp.bfloat16).reshape(pairs, slab, width), extra], axis=1),
+        "zh",
+    )
+    grad_weight = jnp.sum(parts[:, :slab].astype(jnp.float32), axis=0) * draft_gain
+    extra = parts[:, slab : slab + 3].astype(jnp.float32)
+    grad_gain = jnp.sum(extra[:, :2], axis=(0, 1))
+    slots = extra[:, 2, : quads * CAP] + extra[:, 2, 128 : 128 + quads * CAP]
     slots = slots.reshape(pairs, 2, 2, CAP).transpose(1, 0, 2, 3)
     return (grad_weight, grad_gain, slots.reshape(groups * CAP))
 

time: 191 us -> 183 us (0.958)
  the two profiles are of different devices: /device:TPU:16 before, /device:TPU:8 now
where the time goes in v2:
time: 183 us; the launch traced here: 182 us
  blocking collectives  68.5 us (37%)
  starting transfers between devices  54.5 us (30%)
  waiting for transfers between devices  40.5 us (22%)
  local copies, waits for them, and re-layouts  9.51 us (5%)
  other arithmetic  5.88 us (3%)
    all_to_all x2, blocking collectives, exchange(): return lax.all_to_all(value, axes, split_axis=0, concat_axis=0, tiled=True)  68.5 us
    ppermute x9, starting transfers between devices, flipped(): return lax.ppermute(value, axes, [(k, last - k) for k in range(last + 1)])  27.3 us
    ppermute x9, waiting for transfers between devices, flipped(): return lax.ppermute(value, axes, [(k, last - k) for k in range(last + 1)])  21.2 us
    all_to_all x2, waiting for transfers between devices, exchange(): return lax.all_to_all(value, axes, split_axis=0, concat_axis=0, tiled=True)  19.3 us
    all_to_all x2, starting transfers between devices, exchange(): return lax.all_to_all(value, axes, split_axis=0, concat_axis=0, tiled=True)  18.8 us
    ppermute x1, starting transfers between devices, teacher_block(): far = lax.ppermute(piece(2 * a + 1 - x % 2), ('a', 'x'), turn(1))  4.69 us
    ppermute x1, starting transfers between devices, teacher_block(): near = lax.ppermute(piece(2 * a + x % 2), ('a', 'x'), turn(0))  3.72 us
  transfers between devices with their start and end apart: 13, of which 5 were waited for; matrix products, arithmetic and copies ran while one was open for 5% of the time, Pallas kernels for 0%

profile of v2, /device:TPU:8, one launch (start us, length us, event | category | flops | bytes accessed | tf_op | source)
XLA Modules:
  0.0 182.5 jit_solution(12529586005050008502)
XLA Ops:
  0.7 1.2 fusion.70
  1.9 4.7 %collective-permute-start.3 = (bf16[64,2048]{1,0:T(8,128)(2,1)S(1)}, bf16[64,2048]{1,0:T(8,128)(2,1)}, u32[]{:S(2)}, u32[]{:S(2)}) collective-permute-start(bf16[64,2048]{1,0:T(8,128)(2,1)S(1)} %get-tuple-element.19), channel_id=1, source_target_pairs={{0,4},{4,0},{8,260},{12,256},{256,12},{260,8},{264,268},{268,264},... | collective-permute-start | bytes 786440 | tf_op jit(solution)/shard_map/ppermute | solution.py:55
  6.6 3.7 %collective-permute-start.2 = (bf16[64,2048]{1,0:T(8,128)(2,1)S(1)}, bf16[64,2048]{1,0:T(8,128)(2,1)}, u32[]{:S(2)}, u32[]{:S(2)}) collective-permute-start(bf16[64,2048]{1,0:T(8,128)(2,1)S(1)} %get-tuple-element.18), channel_id=1, source_target_pairs={{0,0},{4,4},{8,256},{12,260},{256,8},{260,12},{264,264},{268,268},... | collective-permute-start | bytes 786440 | tf_op jit(solution)/shard_map/ppermute | solution.py:54
  11.8 1.3 and_convert_fusion
  13.3 2.7 %collective-permute-start.6 = (bf16[8,256]{1,0:T(8,128)(2,1)S(1)}, bf16[8,256]{1,0:T(8,128)(2,1)S(1)}, u32[]{:S(2)}, u32[]{:S(2)}) collective-permute-start(bf16[8,256]{1,0:T(8,128)(2,1)S(1)} %stack.44), channel_id=1, source_target_pairs={{0,256},{256,0},{1,257},{257,1},{2,258},{258,2},{3,259},{259,3},{4... | collective-permute-start | bytes 12296 | tf_op jit(solution)/shard_map/ppermute | solution.py:37
  16.0 3.1 %collective-permute-start = (bf16[256,512]{1,0:T(8,128)(2,1)S(1)}, bf16[256,512]{1,0:T(8,128)(2,1)S(1)}, u32[]{:S(2)}, u32[]{:S(2)}) collective-permute-start(bf16[256,512]{1,0:T(8,128)(2,1)S(1)} %copy-done.1), channel_id=1, source_target_pairs={{0,256},{256,0},{1,257},{257,1},{2,258},{258,2},{3,259},{259,3},{4... | collective-permute-start | bytes 786440 | tf_op jit(solution)/shard_map/ppermute | solution.py:37
  20.0 15.1 %all-to-all-start = ((bf16[8,64,512]{2,1,0:T(8,128)(2,1)}), bf16[8,64,512]{2,1,0:T(8,128)(2,1)S(1)}, u32[]{:S(2)}, u32[]{:S(2)}) async-start(bf16[8,64,512]{2,1,0:T(8,128)(2,1)} %broadcast_in_dim.61), calls=%async_computation | async-start | bytes 1048576 | tf_op jit(solution)/shard_map/all_to_all | solution.py:20
  35.9 2.9 %collective-permute-start.7 = (bf16[2,8,256]{2,1,0:T(8,128)(2,1)S(1)}, bf16[2,8,256]{2,1,0:T(8,128)(2,1)S(1)}, u32[]{:S(2)}, u32[]{:S(2)}) collective-permute-start(bf16[2,8,256]{2,1,0:T(8,128)(2,1)S(1)} %pad_maximum_fusion.8), channel_id=1, source_target_pairs={{0,16},{16,0},{1,17},{17,1},{2,18},{18,2},{3,19},{19,3},{4,20},{20... | collective-permute-start | bytes 24584 | tf_op jit(solution)/shard_map/ppermute | solution.py:37
  38.9 1.0 constant_dynamic-slice_fusion.8
  41.6 4.2 %collective-permute-start.4 = (bf16[128,1024]{1,0:T(8,128)(2,1)}, bf16[128,1024]{1,0:T(8,128)(2,1)}, u32[]{:S(2)}, u32[]{:S(2)}) collective-permute-start(bf16[128,1024]{1,0:T(8,128)(2,1)} %pad_maximum_fusion), channel_id=1, source_target_pairs={{0,2},{2,0},{1,3},{3,1},{4,6},{6,4},{5,7},{7,5},{8,10},{10,8},{9,1... | collective-permute-start | bytes 786440 | tf_op jit(solution)/shard_map/ppermute | solution.py:37
  45.9 2.9 %collective-permute-start.1 = (bf16[512,512]{1,0:T(8,128)(2,1)S(1)}, bf16[512,512]{1,0:T(8,128)(2,1)S(1)}, u32[]{:S(2)}, u32[]{:S(2)}) collective-permute-start(bf16[512,512]{1,0:T(8,128)(2,1)S(1)} %get-tuple-element.23.near), channel_id=1, source_target_pairs={{0,16},{16,0},{1,17},{17,1},{2,18},{18,2},{3,19},{19,3},{4,20},{20... | collective-permute-start | bytes 1572872 | tf_op jit(solution)/shard_map/ppermute | solution.py:37
  48.8 10.4 %collective-permute-done.7 = bf16[2,8,256]{2,1,0:T(8,128)(2,1)S(1)} collective-permute-done((bf16[2,8,256]{2,1,0:T(8,128)(2,1)S(1)}, bf16[2,8,256]{2,1,0:T(8,128)(2,1)S(1)}, u32[]{:S(2)}, u32[]{:S(2)}) %collective-permute-start.7) | collective-permute-done | bytes 8224 | tf_op jit(solution)/shard_map/ppermute | solution.py:37
  60.4 1.9 %collective-permute-start.5 = (bf16[256,512]{1,0:T(8,128)(2,1)S(1)}, bf16[256,512]{1,0:T(8,128)(2,1)S(1)}, u32[]{:S(2)}, u32[]{:S(2)}) collective-permute-start(bf16[256,512]{1,0:T(8,128)(2,1)S(1)} %pad_maximum_fusion.2), channel_id=1, source_target_pairs={{0,1},{1,0},{2,3},{3,2},{4,5},{5,4},{6,7},{7,6},{8,9},{9,8},{10,11... | collective-permute-start | bytes 786440 | tf_op jit(solution)/shard_map/ppermute | solution.py:37
  62.3 7.2 %collective-permute-done.1.far = bf16[512,512]{1,0:T(8,128)(2,1)S(1)} collective-permute-done((bf16[512,512]{1,0:T(8,128)(2,1)S(1)}, bf16[512,512]{1,0:T(8,128)(2,1)S(1)}, u32[]{:S(2)}, u32[]{:S(2)}) %collective-permute-start.1) | collective-permute-done | bytes 524320 | tf_op jit(solution)/shard_map/ppermute | solution.py:37
  70.2 1.3 project.1
  71.4 23.8 %all_to_all.20 = bf16[16,72,512]{2,1,0:T(8,128)(2,1)S(1)} all-to-all(bf16[16,72,512]{2,1,0:T(8,128)(2,1)S(1)} %project.1), channel_id=1, replica_groups=mesh['a'=2,'zh'=8,'zl'=2,'x'=4,'b'=2,'c'=2] {'x','b','c'}, dimensions={0} | all-to-all | bytes 2359296 | tf_op jit(solution)/shard_map/all_to_all | solution.py:20
  96.0 1.1 broadcast_in_dim.64
  97.0 3.7 %all-to-all-start.2 = ((bf16[16,72,512]{2,1,0:T(8,128)(2,1)}), bf16[16,72,512]{2,1,0:T(8,128)(2,1)S(1)}, u32[]{:S(2)}, u32[]{:S(2)}) async-start(bf16[16,72,512]{2,1,0:T(8,128)(2,1)} %broadcast_in_dim.64), calls=%async_computation.2 | async-start | bytes 2359296 | tf_op jit(solution)/shard_map/all_to_all | solution.py:20
  100.8 19.3 %all-to-all-done.2 = bf16[16,72,512]{2,1,0:T(8,128)(2,1)S(1)} async-done(((bf16[16,72,512]{2,1,0:T(8,128)(2,1)}), bf16[16,72,512]{2,1,0:T(8,128)(2,1)S(1)}, u32[]{:S(2)}, u32[]{:S(2)}) %all-to-all-start.2) | async-done | bytes 1179680 | tf_op jit(solution)/shard_map/all_to_all | solution.py:20
  122.2 4.8 %collective-permute-start.10 = (f32[12,128]{1,0:T(8,128)S(1)}, f32[12,128]{1,0:T(8,128)S(1)}, u32[]{:S(2)}, u32[]{:S(2)}) collective-permute-start(f32[12,128]{1,0:T(8,128)S(1)} %get-tuple-element.49), channel_id=1, source_target_pairs={{0,272},{16,256},{256,16},{272,0},{1,273},{17,257},{257,17},{273,1... | collective-permute-start | bytes 18440 | tf_op jit(solution)/shard_map/ppermute | solution.py:37
  127.0 2.8 %collective-permute-start.8 = (f32[12,128]{1,0:T(8,128)S(1)}, f32[12,128]{1,0:T(8,128)S(1)}, u32[]{:S(2)}, u32[]{:S(2)}) collective-permute-start(f32[12,128]{1,0:T(8,128)S(1)} %get-tuple-element.47), channel_id=1, source_target_pairs={{0,16},{16,0},{1,17},{17,1},{2,18},{18,2},{3,19},{19,3},{4,20},{20... | collective-permute-start | bytes 18440 | tf_op jit(solution)/shard_map/ppermute | solution.py:37
  129.8 1.9 %collective-permute-start.9 = (f32[12,128]{1,0:T(8,128)S(1)}, f32[12,128]{1,0:T(8,128)S(1)}, u32[]{:S(2)}, u32[]{:S(2)}) collective-permute-start(f32[12,128]{1,0:T(8,128)S(1)} %get-tuple-element.48), channel_id=1, source_target_pairs={{0,256},{256,0},{1,257},{257,1},{2,258},{258,2},{3,259},{259,3},{4... | collective-permute-start | bytes 18440 | tf_op jit(solution)/shard_map/ppermute | solution.py:37
  132.5 2.8 %collective-permute-done.9 = f32[12,128]{1,0:T(8,128)S(1)} collective-permute-done((f32[12,128]{1,0:T(8,128)S(1)}, f32[12,128]{1,0:T(8,128)S(1)}, u32[]{:S(2)}, u32[]{:S(2)}) %collective-permute-start.9) | collective-permute-done | bytes 6176 | tf_op jit(solution)/shard_map/ppermute | solution.py:37
  135.6 44.7 %all_to_all.21 = bf16[8,72,512]{2,1,0:T(8,128)(2,1)S(1)} all-to-all(bf16[8,72,512]{2,1,0:T(8,128)(2,1)S(1)} %fusion.3), channel_id=1, replica_groups=mesh['a'=2,'zh'=8,'zl'=2,'x'=4,'b'=2,'c'=2] {'zh'}, dimensions={0} | all-to-all | bytes 1179648 | tf_op jit(solution)/shard_map/all_to_all | solution.py:20
  (113 shorter events, 12.6 us)
Async XLA Ops:
  0.6 9.7 %copy-start = (bf16[256,2000]{0,1:T(8,128)(2,1)S(1)}, bf16[256,2000]{0,1:T(8,128)(2,1)}, u32[]{:S(2)}) copy-start(bf16[256,2000]{0,1:T(8,128)(2,1)} %param.14) | copy-start | bytes 3072004
  1.8 9.3 %copy-start.5 = (s32[1,2]{1,0:T(1,128)S(1)}, s32[1,2]{1,0:T(1,128)}, u32[]{:S(2)}) copy-start(s32[1,2]{1,0:T(1,128)} %param.15) | copy-start | bytes 28
  1.8 9.9 %copy-start.6 = (s32[256]{0:T(256)S(1)}, s32[256]{0:T(256)}, u32[]{:S(2)}) copy-start(s32[256]{0:T(256)} %param.16) | copy-start | bytes 3076
  1.9 11.2 %copy-start.3 = (s32[256,1]{0,1:T(1,128)S(1)}, s32[256,1]{0,1:T(1,128)}, u32[]{:S(2)}) copy-start(s32[256,1]{0,1:T(1,128)} %param.17) | copy-start | bytes 3076
  1.9 14.1 %copy-start.1 = (bf16[256,512]{1,0:T(8,128)(2,1)S(1)}, bf16[256,512]{1,0:T(8,128)(2,1)}, u32[]{:S(2)}) copy-start(bf16[256,512]{1,0:T(8,128)(2,1)} %param.9) | copy-start | bytes 786436
  1.9 17.3 %copy-start.2 = (bf16[64,512]{1,0:T(8,128)(2,1)S(1)}, bf16[64,512]{1,0:T(8,128)(2,1)}, u32[]{:S(2)}) copy-start(bf16[64,512]{1,0:T(8,128)(2,1)} %param.13) | copy-start | bytes 196612
  1.9 37.0 %collective-permute-start.3 = (bf16[64,2048]{1,0:T(8,128)(2,1)S(1)}, bf16[64,2048]{1,0:T(8,128)(2,1)}, u32[]{:S(2)}, u32[]{:S(2)}) collective-permute-start(bf16[64,2048]{1,0:T(8,128)(2,1)S(1)} %get-tuple-element.19), channel_id=1, source_target_pairs={{0,4},{4,0},{8,260},{12,256},{256,12},{260,8},{264,268},{268,264},... | collective-permute-start | bytes 786440 | tf_op jit(solution)/shard_map/ppermute | solution.py:55
  6.6 33.3 %collective-permute-start.2 = (bf16[64,2048]{1,0:T(8,128)(2,1)S(1)}, bf16[64,2048]{1,0:T(8,128)(2,1)}, u32[]{:S(2)}, u32[]{:S(2)}) collective-permute-start(bf16[64,2048]{1,0:T(8,128)(2,1)S(1)} %get-tuple-element.18), channel_id=1, source_target_pairs={{0,0},{4,4},{8,256},{12,260},{256,8},{260,12},{264,264},{268,268},... | collective-permute-start | bytes 786440 | tf_op jit(solution)/shard_map/ppermute | solution.py:54
  13.3 22.6 %copy-start.4 = (f32[512]{0:T(512)S(1)}, f32[512]{0:T(512)}, u32[]{:S(2)}) copy-start(f32[512]{0:T(512)} %param.12) | copy-start | bytes 6148
  13.3 22.6 %collective-permute-start.6 = (bf16[8,256]{1,0:T(8,128)(2,1)S(1)}, bf16[8,256]{1,0:T(8,128)(2,1)S(1)}, u32[]{:S(2)}, u32[]{:S(2)}) collective-permute-start(bf16[8,256]{1,0:T(8,128)(2,1)S(1)} %stack.44), channel_id=1, source_target_pairs={{0,256},{256,0},{1,257},{257,1},{2,258},{258,2},{3,259},{259,3},{4... | collective-permute-start | bytes 12296 | tf_op jit(solution)/shard_map/ppermute | solution.py:37
  16.0 29.8 %collective-permute-start = (bf16[256,512]{1,0:T(8,128)(2,1)S(1)}, bf16[256,512]{1,0:T(8,128)(2,1)S(1)}, u32[]{:S(2)}, u32[]{:S(2)}) collective-permute-start(bf16[256,512]{1,0:T(8,128)(2,1)S(1)} %copy-done.1), channel_id=1, source_target_pairs={{0,256},{256,0},{1,257},{257,1},{2,258},{258,2},{3,259},{259,3},{4... | collective-permute-start | bytes 786440 | tf_op jit(solution)/shard_map/ppermute | solution.py:37
  20.0 50.2 %all-to-all-start = ((bf16[8,64,512]{2,1,0:T(8,128)(2,1)}), bf16[8,64,512]{2,1,0:T(8,128)(2,1)S(1)}, u32[]{:S(2)}, u32[]{:S(2)}) async-start(bf16[8,64,512]{2,1,0:T(8,128)(2,1)} %broadcast_in_dim.61), calls=%async_computation | async-start | bytes 1048576 | tf_op jit(solution)/shard_map/all_to_all | solution.py:20
  35.9 23.3 %collective-permute-start.7 = (bf16[2,8,256]{2,1,0:T(8,128)(2,1)S(1)}, bf16[2,8,256]{2,1,0:T(8,128)(2,1)S(1)}, u32[]{:S(2)}, u32[]{:S(2)}) collective-permute-start(bf16[2,8,256]{2,1,0:T(8,128)(2,1)S(1)} %pad_maximum_fusion.8), channel_id=1, source_target_pairs={{0,16},{16,0},{1,17},{17,1},{2,18},{18,2},{3,19},{19,3},{4,20},{20... | collective-permute-start | bytes 24584 | tf_op jit(solution)/shard_map/ppermute | solution.py:37
  41.6 17.7 %collective-permute-start.4 = (bf16[128,1024]{1,0:T(8,128)(2,1)}, bf16[128,1024]{1,0:T(8,128)(2,1)}, u32[]{:S(2)}, u32[]{:S(2)}) collective-permute-start(bf16[128,1024]{1,0:T(8,128)(2,1)} %pad_maximum_fusion), channel_id=1, source_target_pairs={{0,2},{2,0},{1,3},{3,1},{4,6},{6,4},{5,7},{7,5},{8,10},{10,8},{9,1... | collective-permute-start | bytes 786440 | tf_op jit(solution)/shard_map/ppermute | solution.py:37
  45.9 23.6 %collective-permute-start.1 = (bf16[512,512]{1,0:T(8,128)(2,1)S(1)}, bf16[512,512]{1,0:T(8,128)(2,1)S(1)}, u32[]{:S(2)}, u32[]{:S(2)}) collective-permute-start(bf16[512,512]{1,0:T(8,128)(2,1)S(1)} %get-tuple-element.23.near), channel_id=1, source_target_pairs={{0,16},{16,0},{1,17},{17,1},{2,18},{18,2},{3,19},{19,3},{4,20},{20... | collective-permute-start | bytes 1572872 | tf_op jit(solution)/shard_map/ppermute | solution.py:37
  60.4 9.7 %collective-permute-start.5 = (bf16[256,512]{1,0:T(8,128)(2,1)S(1)}, bf16[256,512]{1,0:T(8,128)(2,1)S(1)}, u32[]{:S(2)}, u32[]{:S(2)}) collective-permute-start(bf16[256,512]{1,0:T(8,128)(2,1)S(1)} %pad_maximum_fusion.2), channel_id=1, source_target_pairs={{0,1},{1,0},{2,3},{3,2},{4,5},{5,4},{6,7},{7,6},{8,9},{9,8},{10,11... | collective-permute-start | bytes 786440 | tf_op jit(solution)/shard_map/ppermute | solution.py:37
  97.0 23.0 %all-to-all-start.2 = ((bf16[16,72,512]{2,1,0:T(8,128)(2,1)}), bf16[16,72,512]{2,1,0:T(8,128)(2,1)S(1)}, u32[]{:S(2)}, u32[]{:S(2)}) async-start(bf16[16,72,512]{2,1,0:T(8,128)(2,1)} %broadcast_in_dim.64), calls=%async_computation.2 | async-start | bytes 2359296 | tf_op jit(solution)/shard_map/all_to_all | solution.py:20
  122.2 9.6 %collective-permute-start.10 = (f32[12,128]{1,0:T(8,128)S(1)}, f32[12,128]{1,0:T(8,128)S(1)}, u32[]{:S(2)}, u32[]{:S(2)}) collective-permute-start(f32[12,128]{1,0:T(8,128)S(1)} %get-tuple-element.49), channel_id=1, source_target_pairs={{0,272},{16,256},{256,16},{272,0},{1,273},{17,257},{257,17},{273,1... | collective-permute-start | bytes 18440 | tf_op jit(solution)/shard_map/ppermute | solution.py:37
  127.0 5.5 %collective-permute-start.8 = (f32[12,128]{1,0:T(8,128)S(1)}, f32[12,128]{1,0:T(8,128)S(1)}, u32[]{:S(2)}, u32[]{:S(2)}) collective-permute-start(f32[12,128]{1,0:T(8,128)S(1)} %get-tuple-element.47), channel_id=1, source_target_pairs={{0,16},{16,0},{1,17},{17,1},{2,18},{18,2},{3,19},{19,3},{4,20},{20... | collective-permute-start | bytes 18440 | tf_op jit(solution)/shard_map/ppermute | solution.py:37
  129.8 5.5 %collective-permute-start.9 = (f32[12,128]{1,0:T(8,128)S(1)}, f32[12,128]{1,0:T(8,128)S(1)}, u32[]{:S(2)}, u32[]{:S(2)}) collective-permute-start(f32[12,128]{1,0:T(8,128)S(1)} %get-tuple-element.48), channel_id=1, source_target_pairs={{0,256},{256,0},{1,257},{257,1},{2,258},{258,2},{3,259},{259,3},{4... | collective-permute-start | bytes 18440 | tf_op jit(solution)/shard_map/ppermute | solution.py:37

commit v3 on v2

--- a/solution.py
+++ b/solution.py
@@ -69,7 +69,7 @@
     return [part.reshape(4, slab, width) for part in parts], 4 * (x % 2) + 2 * b + c
 
 
-def project(place, near, far, wd, kept, came, gains, side, out):
+def project(place, own, across, beside, both, wd, kept, came, gains, side, out):
     slab = wd.shape[1]
     mine = out.shape[1] - side.shape[1]
     here = place[0]
@@ -84,12 +84,15 @@
             merged.append(wd[k].astype(jnp.float32) * draft_gain - wt * target_gain)
         merged = jnp.concatenate(merged).astype(jnp.bfloat16)
         lanes = slice(pair * 2 * slab, (pair + 1) * 2 * slab)
-        for half, block in enumerate((near, far)):
+        for quad, block in enumerate((own, across, beside, both)):
             value = lax.dot_general(
-                block[...], merged, (((1,), (1,)), ((), ())), preferred_element_type=jnp.float32
+                block[: 4 * mine],
+                merged,
+                (((1,), (1,)), ((), ())),
+                preferred_element_type=jnp.float32,
             )
-            out[8 * half : 8 * half + 8, :mine, lanes] = value.astype(jnp.bfloat16).reshape(
-                8, mine, 2 * slab
+            out[4 * quad : 4 * quad + 4, :mine, lanes] = value.astype(jnp.bfloat16).reshape(
+                4, mine, 2 * slab
             )
     out[:, mine:] = side[...]
 
@@ -153,17 +156,18 @@
     kinds = facts.shape[0]
 
     wd = spread(draft_weight, "zh").reshape(columns, width)
-    near = jnp.concatenate([hidden, flipped(hidden, ("a",))], axis=0)
-    far = flipped(near, ("zl",))
-    facts_here = jnp.stack([facts, flipped(facts, ("a",))])
-    facts_here = jnp.concatenate([facts_here, flipped(facts_here, ("zl",))], axis=0)
-    features_here = jnp.concatenate([near, far], axis=0)
+    own = jnp.concatenate([hidden, jnp.pad(facts, ((0, 0), (0, width - rows)))], axis=0)
+    across = flipped(own, ("a",))
+    beside = flipped(own, ("zl",))
+    both = flipped(across, ("zl",))
+    blocks = (own, across, beside, both)
+    facts_here = jnp.stack([block[rows:, :rows] for block in blocks])
     (kept, came), place = teacher_block(target_weight, a, zl, slab, width)
 
     gain_slice = lax.dynamic_slice_in_dim(target_gain, model * width, width)
     gains = jnp.stack([draft_gain, gain_slice])
-    float_rows = features_here.astype(jnp.float32)
-    squares = jnp.stack(halves(jnp.sum(float_rows * float_rows, axis=1))).reshape(2, models, mine)
+    squares = [jnp.sum(block[:rows].astype(jnp.float32) ** 2, axis=1) for block in blocks]
+    squares = jnp.stack(halves(jnp.stack(squares))).reshape(2, models, mine)
     facts_here = facts_here.swapaxes(0, 1).reshape(kinds, models, mine)
     side = jnp.concatenate([facts_here, squares], axis=0).swapaxes(0, 1)
     side = side.reshape(models, 1, (kinds + 2) * mine)
@@ -172,7 +176,7 @@
         project,
         out_shape=jax.ShapeDtypeStruct((models, mine + 8, columns), jnp.bfloat16),
         in_specs=[pl.BlockSpec(memory_space=pltpu.SMEM)]
-        + [pl.BlockSpec(memory_space=pltpu.VMEM)] * 7,
+        + [pl.BlockSpec(memory_space=pltpu.VMEM)] * 9,
         out_specs=pl.BlockSpec(memory_space=pltpu.VMEM),
         cost_estimate=pl.CostEstimate(
             flops=2 * all_rows * width * columns,
@@ -181,8 +185,11 @@
         ),
         compiler_params=pltpu.CompilerParams(vmem_limit_bytes=16 * 2**20),
         name="project",
-    )(place.reshape(1), near, far, wd.reshape(pairs, slab, width), kept, came, gains, side)
+    )(place.reshape(1), *blocks, wd.reshape(pairs, slab, width), kept, came, gains, side)
     got = exchange(partial, MP)
+    features_here = lax.optimization_barrier(
+        jnp.concatenate([block[:rows] for block in blocks], axis=0)
+    )
     summed = jnp.sum(got[:, :mine].astype(jnp.float32), axis=0)
     side = got[:, mine:].reshape(models, 8 * columns)[:, : (kinds + 2) * mine]
     side = side.reshape(models, kinds + 2, mine).astype(jnp.float32)
@@ -248,7 +255,8 @@
         jnp.concatenate([grad.astype(jnp.bfloat16).reshape(pairs, slab, width), extra], axis=1),
         "zh",
     )
-    grad_weight = jnp.sum(parts[:, :slab].astype(jnp.float32), axis=0) * draft_gain
+    spread_gain = lax.optimization_barrier(jnp.broadcast_to(draft_gain, (slab, width)) + 0.0)
+    grad_weight = jnp.sum(parts[:, :slab].astype(jnp.float32), axis=0) * spread_gain
     extra = parts[:, slab : slab + 3].astype(jnp.float32)
     grad_gain = jnp.sum(extra[:, :2], axis=(0, 1))
     slots = extra[:, 2, : quads * CAP] + extra[:, 2, 128 : 128 + quads * CAP]

time: 183 us -> 178 us (0.973)
  the two profiles are of different devices: /device:TPU:8 before, /device:TPU:72 now
where the time goes in v3:
time: 178 us; the launch traced here: 177 us
  waiting for transfers between devices  73.3 us (41%)
  starting transfers between devices  62.1 us (35%)
  blocking collectives  22.5 us (13%)
  other arithmetic  8.59 us (5%)
  local copies, waits for them, and re-layouts  6.92 us (4%)
    all_to_all x3, waiting for transfers between devices, exchange(): return lax.all_to_all(value, axes, split_axis=0, concat_axis=0, tiled=True)  51.3 us
    all_to_all x3, starting transfers between devices, exchange(): return lax.all_to_all(value, axes, split_axis=0, concat_axis=0, tiled=True)  27.6 us
    ppermute x8, starting transfers between devices, flipped(): return lax.ppermute(value, axes, [(k, last - k) for k in range(last + 1)])  25 us
    all_to_all x1, blocking collectives, exchange(): return lax.all_to_all(value, axes, split_axis=0, concat_axis=0, tiled=True)  22.5 us
    ppermute x8, waiting for transfers between devices, flipped(): return lax.ppermute(value, axes, [(k, last - k) for k in range(last + 1)])  22 us
    ppermute x1, starting transfers between devices, teacher_block(): near = lax.ppermute(piece(2 * a + x % 2), ('a', 'x'), turn(0))  4.94 us
    ppermute x1, starting transfers between devices, teacher_block(): far = lax.ppermute(piece(2 * a + 1 - x % 2), ('a', 'x'), turn(1))  4.55 us
  transfers between devices with their start and end apart: 13, of which 6 were waited for; matrix products, arithmetic and copies ran while one was open for 5% of the time, Pallas kernels for 0%

profile of v3, /device:TPU:72, one launch (start us, length us, event | category | flops | bytes accessed | tf_op | source)
XLA Modules:
  0.0 177.0 jit_solution(12984513445362168495)
XLA Ops:
  0.7 1.2 fusion.72
  1.9 4.6 %collective-permute-start.4 = (bf16[64,2048]{1,0:T(8,128)(2,1)S(1)}, bf16[64,2048]{1,0:T(8,128)(2,1)S(1)}, u32[]{:S(2)}, u32[]{:S(2)}) collective-permute-start(bf16[64,2048]{1,0:T(8,128)(2,1)S(1)} %get-tuple-element.19), channel_id=1, source_target_pairs={{0,4},{4,0},{8,260},{12,256},{256,12},{260,8},{264,268},{268,264},... | collective-permute-start | bytes 786440 | tf_op jit(solution)/shard_map/ppermute | solution.py:55
  6.5 1.5 reduce_max.25
  9.1 1.3 and_convert_fusion
  10.7 1.9 %collective-permute-start = (bf16[264,512]{1,0:T(8,128)(2,1)S(1)}, bf16[264,512]{1,0:T(8,128)(2,1)S(1)}, u32[]{:S(2)}, u32[]{:S(2)}) collective-permute-start(bf16[264,512]{1,0:T(8,128)(2,1)S(1)} %fusion.11.own), channel_id=1, source_target_pairs={{0,256},{256,0},{1,257},{257,1},{2,258},{258,2},{3,259},{259,3},{4... | collective-permute-start | bytes 811016 | tf_op jit(solution)/shard_map/ppermute | solution.py:37
  12.6 3.8 %collective-permute-start.1 = (bf16[264,512]{1,0:T(8,128)(2,1)S(1)}, bf16[264,512]{1,0:T(8,128)(2,1)S(1)}, u32[]{:S(2)}, u32[]{:S(2)}) collective-permute-start(bf16[264,512]{1,0:T(8,128)(2,1)S(1)} %fusion.11.own), channel_id=1, source_target_pairs={{0,16},{16,0},{1,17},{17,1},{2,18},{18,2},{3,19},{19,3},{4,20},{20... | collective-permute-start | bytes 811016 | tf_op jit(solution)/shard_map/ppermute | solution.py:37
  16.4 4.9 %collective-permute-start.3 = (bf16[64,2048]{1,0:T(8,128)(2,1)S(1)}, bf16[64,2048]{1,0:T(8,128)(2,1)S(1)}, u32[]{:S(2)}, u32[]{:S(2)}) collective-permute-start(bf16[64,2048]{1,0:T(8,128)(2,1)S(1)} %get-tuple-element.18), channel_id=1, source_target_pairs={{0,0},{4,4},{8,256},{12,260},{256,8},{260,12},{264,264},{268,268},... | collective-permute-start | bytes 786440 | tf_op jit(solution)/shard_map/ppermute | solution.py:54
  22.2 13.8 %all-to-all-start = ((bf16[8,64,512]{2,1,0:T(8,128)(2,1)}), bf16[8,64,512]{2,1,0:T(8,128)(2,1)S(1)}, u32[]{:S(2)}, u32[]{:S(2)}) async-start(bf16[8,64,512]{2,1,0:T(8,128)(2,1)} %broadcast_in_dim.65), calls=%async_computation | async-start | bytes 1048576 | tf_op jit(solution)/shard_map/all_to_all | solution.py:20
  37.1 4.2 %collective-permute-start.5 = (bf16[128,1024]{1,0:T(8,128)(2,1)S(1)}, bf16[128,1024]{1,0:T(8,128)(2,1)S(1)}, u32[]{:S(2)}, u32[]{:S(2)}) collective-permute-start(bf16[128,1024]{1,0:T(8,128)(2,1)S(1)} %pad_maximum_fusion.1), channel_id=1, source_target_pairs={{0,2},{2,0},{1,3},{3,1},{4,6},{6,4},{5,7},{7,5},{8,10},{10,8},{9,1... | collective-permute-start | bytes 786440 | tf_op jit(solution)/shard_map/ppermute | solution.py:37
  41.4 2.9 %collective-permute-start.2 = (bf16[264,512]{1,0:T(8,128)(2,1)S(1)}, bf16[264,512]{1,0:T(8,128)(2,1)S(1)}, u32[]{:S(2)}, u32[]{:S(2)}) collective-permute-start(bf16[264,512]{1,0:T(8,128)(2,1)S(1)} %collective-permute-done.across), channel_id=1, source_target_pairs={{0,16},{16,0},{1,17},{17,1},{2,18},{18,2},{3,19},{19,3},{4,20},{20... | collective-permute-start | bytes 811016 | tf_op jit(solution)/shard_map/ppermute | solution.py:37
  44.6 2.3 %collective-permute-done.5 = bf16[128,1024]{1,0:T(8,128)(2,1)S(1)} collective-permute-done((bf16[128,1024]{1,0:T(8,128)(2,1)S(1)}, bf16[128,1024]{1,0:T(8,128)(2,1)S(1)}, u32[]{:S(2)}, u32[]{:S(2)}) %collective-permute-start.5) | collective-permute-done | bytes 262176 | tf_op jit(solution)/shard_map/ppermute | solution.py:37
  46.9 1.9 %collective-permute-start.6 = (bf16[256,512]{1,0:T(8,128)(2,1)S(1)}, bf16[256,512]{1,0:T(8,128)(2,1)S(1)}, u32[]{:S(2)}, u32[]{:S(2)}) collective-permute-start(bf16[256,512]{1,0:T(8,128)(2,1)S(1)} %pad_maximum_fusion.3), channel_id=1, source_target_pairs={{0,1},{1,0},{2,3},{3,2},{4,5},{5,4},{6,7},{7,6},{8,9},{9,8},{10,11... | collective-permute-start | bytes 786440 | tf_op jit(solution)/shard_map/ppermute | solution.py:37
  48.9 15.2 %collective-permute-done.2.both = bf16[264,512]{1,0:T(8,128)(2,1)S(1)} collective-permute-done((bf16[264,512]{1,0:T(8,128)(2,1)S(1)}, bf16[264,512]{1,0:T(8,128)(2,1)S(1)}, u32[]{:S(2)}, u32[]{:S(2)}) %collective-permute-start.2) | collective-permute-done | bytes 270368 | tf_op jit(solution)/shard_map/ppermute | solution.py:37
  64.7 1.2 all-to-all-done.wd
  65.9 1.3 project.1
  67.1 22.5 %all_to_all.20 = bf16[16,72,512]{2,1,0:T(8,128)(2,1)S(1)} all-to-all(bf16[16,72,512]{2,1,0:T(8,128)(2,1)S(1)} %project.1), channel_id=1, replica_groups=mesh['a'=2,'zh'=8,'zl'=2,'x'=4,'b'=2,'c'=2] {'x','b','c'}, dimensions={0} | all-to-all | bytes 2359296 | tf_op jit(solution)/shard_map/all_to_all | solution.py:20
  91.5 3.7 %all-to-all-start.2 = ((bf16[16,72,512]{2,1,0:T(8,128)(2,1)}), bf16[16,72,512]{2,1,0:T(8,128)(2,1)S(1)}, u32[]{:S(2)}, u32[]{:S(2)}) async-start(bf16[16,72,512]{2,1,0:T(8,128)(2,1)} %broadcast_in_dim.66), calls=%async_computation.2 | async-start | bytes 2359296 | tf_op jit(solution)/shard_map/all_to_all | solution.py:20
  96.4 18.1 %all-to-all-done.2 = bf16[16,72,512]{2,1,0:T(8,128)(2,1)S(1)} async-done(((bf16[16,72,512]{2,1,0:T(8,128)(2,1)}), bf16[16,72,512]{2,1,0:T(8,128)(2,1)S(1)}, u32[]{:S(2)}, u32[]{:S(2)}) %all-to-all-start.2) | async-done | bytes 1179680 | tf_op jit(solution)/shard_map/all_to_all | solution.py:20
  117.0 4.0 %collective-permute-start.7 = (f32[12,128]{1,0:T(8,128)S(1)}, f32[12,128]{1,0:T(8,128)S(1)}, u32[]{:S(2)}, u32[]{:S(2)}) collective-permute-start(f32[12,128]{1,0:T(8,128)S(1)} %get-tuple-element.43), channel_id=1, source_target_pairs={{0,16},{16,0},{1,17},{17,1},{2,18},{18,2},{3,19},{19,3},{4,20},{20... | collective-permute-start | bytes 18440 | tf_op jit(solution)/shard_map/ppermute | solution.py:37
  121.0 4.2 %collective-permute-start.8 = (f32[12,128]{1,0:T(8,128)S(1)}, f32[12,128]{1,0:T(8,128)S(1)}, u32[]{:S(2)}, u32[]{:S(2)}) collective-permute-start(f32[12,128]{1,0:T(8,128)S(1)} %get-tuple-element.44), channel_id=1, source_target_pairs={{0,256},{256,0},{1,257},{257,1},{2,258},{258,2},{3,259},{259,3},{4... | collective-permute-start | bytes 18440 | tf_op jit(solution)/shard_map/ppermute | solution.py:37
  125.3 1.9 %collective-permute-start.9 = (f32[12,128]{1,0:T(8,128)S(1)}, f32[12,128]{1,0:T(8,128)S(1)}, u32[]{:S(2)}, u32[]{:S(2)}) collective-permute-start(f32[12,128]{1,0:T(8,128)S(1)} %get-tuple-element.45), channel_id=1, source_target_pairs={{0,272},{16,256},{256,16},{272,0},{1,273},{17,257},{257,17},{273,1... | collective-permute-start | bytes 18440 | tf_op jit(solution)/shard_map/ppermute | solution.py:37
  127.2 4.5 %collective-permute-done.9 = f32[12,128]{1,0:T(8,128)S(1)} collective-permute-done((f32[12,128]{1,0:T(8,128)S(1)}, f32[12,128]{1,0:T(8,128)S(1)}, u32[]{:S(2)}, u32[]{:S(2)}) %collective-permute-start.9) | collective-permute-done | bytes 6176 | tf_op jit(solution)/shard_map/ppermute | solution.py:37
  132.7 10.1 %all-to-all-start.3 = ((bf16[8,72,512]{2,1,0:T(8,128)(2,1)}), bf16[8,72,512]{2,1,0:T(8,128)(2,1)S(1)}, u32[]{:S(2)}, u32[]{:S(2)}) async-start(bf16[8,72,512]{2,1,0:T(8,128)(2,1)} %fusion.3), calls=%async_computation.3 | async-start | bytes 1179648 | tf_op jit(solution)/shard_map/all_to_all | solution.py:20
  142.8 32.0 %all-to-all-done.3 = bf16[8,72,512]{2,1,0:T(8,128)(2,1)S(1)} async-done(((bf16[8,72,512]{2,1,0:T(8,128)(2,1)}), bf16[8,72,512]{2,1,0:T(8,128)(2,1)S(1)}, u32[]{:S(2)}, u32[]{:S(2)}) %all-to-all-start.3) | async-done | bytes 589856 | tf_op jit(solution)/shard_map/all_to_all | solution.py:20
  (123 shorter events, 12.5 us)
Async XLA Ops:
  0.6 7.3 %copy-start = (bf16[256,2000]{0,1:T(8,128)(2,1)S(1)}, bf16[256,2000]{0,1:T(8,128)(2,1)}, u32[]{:S(2)}) copy-start(bf16[256,2000]{0,1:T(8,128)(2,1)} %param.14) | copy-start | bytes 3072004
  0.6 7.9 %copy-start.6 = (s32[1,2]{1,0:T(1,128)S(1)}, s32[1,2]{1,0:T(1,128)}, u32[]{:S(2)}) copy-start(s32[1,2]{1,0:T(1,128)} %param.15) | copy-start | bytes 28
  0.7 8.5 %copy-start.7 = (s32[256]{0:T(256)S(1)}, s32[256]{0:T(256)}, u32[]{:S(2)}) copy-start(s32[256]{0:T(256)} %param.16) | copy-start | bytes 3076
  0.7 9.8 %copy-start.4 = (s32[256,1]{0,1:T(1,128)S(1)}, s32[256,1]{0,1:T(1,128)}, u32[]{:S(2)}) copy-start(s32[256,1]{0,1:T(1,128)} %param.17) | copy-start | bytes 3076
  0.7 10.0 %copy-start.1 = (bf16[256,512]{1,0:T(8,128)(2,1)S(1)}, bf16[256,512]{1,0:T(8,128)(2,1)}, u32[]{:S(2)}) copy-start(bf16[256,512]{1,0:T(8,128)(2,1)} %param.9) | copy-start | bytes 786436
  0.7 20.7 %copy-start.3 = (bf16[64,512]{1,0:T(8,128)(2,1)S(1)}, bf16[64,512]{1,0:T(8,128)(2,1)}, u32[]{:S(2)}) copy-start(bf16[64,512]{1,0:T(8,128)(2,1)} %param.13) | copy-start | bytes 196612
  1.9 34.9 %copy-start.5 = (f32[512]{0:T(512)S(1)}, f32[512]{0:T(512)}, u32[]{:S(2)}) copy-start(f32[512]{0:T(512)} %param.12) | copy-start | bytes 6148
  1.9 35.1 %collective-permute-start.4 = (bf16[64,2048]{1,0:T(8,128)(2,1)S(1)}, bf16[64,2048]{1,0:T(8,128)(2,1)S(1)}, u32[]{:S(2)}, u32[]{:S(2)}) collective-permute-start(bf16[64,2048]{1,0:T(8,128)(2,1)S(1)} %get-tuple-element.19), channel_id=1, source_target_pairs={{0,4},{4,0},{8,260},{12,256},{256,12},{260,8},{264,268},{268,264},... | collective-permute-start | bytes 786440 | tf_op jit(solution)/shard_map/ppermute | solution.py:55
  10.7 30.7 %collective-permute-start = (bf16[264,512]{1,0:T(8,128)(2,1)S(1)}, bf16[264,512]{1,0:T(8,128)(2,1)S(1)}, u32[]{:S(2)}, u32[]{:S(2)}) collective-permute-start(bf16[264,512]{1,0:T(8,128)(2,1)S(1)} %fusion.11.own), channel_id=1, source_target_pairs={{0,256},{256,0},{1,257},{257,1},{2,258},{258,2},{3,259},{259,3},{4... | collective-permute-start | bytes 811016 | tf_op jit(solution)/shard_map/ppermute | solution.py:37
  12.6 31.8 %collective-permute-start.1 = (bf16[264,512]{1,0:T(8,128)(2,1)S(1)}, bf16[264,512]{1,0:T(8,128)(2,1)S(1)}, u32[]{:S(2)}, u32[]{:S(2)}) collective-permute-start(bf16[264,512]{1,0:T(8,128)(2,1)S(1)} %fusion.11.own), channel_id=1, source_target_pairs={{0,16},{16,0},{1,17},{17,1},{2,18},{18,2},{3,19},{19,3},{4,20},{20... | collective-permute-start | bytes 811016 | tf_op jit(solution)/shard_map/ppermute | solution.py:37
  16.4 20.6 %collective-permute-start.3 = (bf16[64,2048]{1,0:T(8,128)(2,1)S(1)}, bf16[64,2048]{1,0:T(8,128)(2,1)S(1)}, u32[]{:S(2)}, u32[]{:S(2)}) collective-permute-start(bf16[64,2048]{1,0:T(8,128)(2,1)S(1)} %get-tuple-element.18), channel_id=1, source_target_pairs={{0,0},{4,4},{8,256},{12,260},{256,8},{260,12},{264,264},{268,268},... | collective-permute-start | bytes 786440 | tf_op jit(solution)/shard_map/ppermute | solution.py:54
  22.2 43.6 %all-to-all-start = ((bf16[8,64,512]{2,1,0:T(8,128)(2,1)}), bf16[8,64,512]{2,1,0:T(8,128)(2,1)S(1)}, u32[]{:S(2)}, u32[]{:S(2)}) async-start(bf16[8,64,512]{2,1,0:T(8,128)(2,1)} %broadcast_in_dim.65), calls=%async_computation | async-start | bytes 1048576 | tf_op jit(solution)/shard_map/all_to_all | solution.py:20
  37.1 9.8 %collective-permute-start.5 = (bf16[128,1024]{1,0:T(8,128)(2,1)S(1)}, bf16[128,1024]{1,0:T(8,128)(2,1)S(1)}, u32[]{:S(2)}, u32[]{:S(2)}) collective-permute-start(bf16[128,1024]{1,0:T(8,128)(2,1)S(1)} %pad_maximum_fusion.1), channel_id=1, source_target_pairs={{0,2},{2,0},{1,3},{3,1},{4,6},{6,4},{5,7},{7,5},{8,10},{10,8},{9,1... | collective-permute-start | bytes 786440 | tf_op jit(solution)/shard_map/ppermute | solution.py:37
  41.4 22.7 %collective-permute-start.2 = (bf16[264,512]{1,0:T(8,128)(2,1)S(1)}, bf16[264,512]{1,0:T(8,128)(2,1)S(1)}, u32[]{:S(2)}, u32[]{:S(2)}) collective-permute-start(bf16[264,512]{1,0:T(8,128)(2,1)S(1)} %collective-permute-done.across), channel_id=1, source_target_pairs={{0,16},{16,0},{1,17},{17,1},{2,18},{18,2},{3,19},{19,3},{4,20},{20... | collective-permute-start | bytes 811016 | tf_op jit(solution)/shard_map/ppermute | solution.py:37
  46.9 17.7 %collective-permute-start.6 = (bf16[256,512]{1,0:T(8,128)(2,1)S(1)}, bf16[256,512]{1,0:T(8,128)(2,1)S(1)}, u32[]{:S(2)}, u32[]{:S(2)}) collective-permute-start(bf16[256,512]{1,0:T(8,128)(2,1)S(1)} %pad_maximum_fusion.3), channel_id=1, source_target_pairs={{0,1},{1,0},{2,3},{3,2},{4,5},{5,4},{6,7},{7,6},{8,9},{9,8},{10,11... | collective-permute-start | bytes 786440 | tf_op jit(solution)/shard_map/ppermute | solution.py:37
  91.5 23.0 %all-to-all-start.2 = ((bf16[16,72,512]{2,1,0:T(8,128)(2,1)}), bf16[16,72,512]{2,1,0:T(8,128)(2,1)S(1)}, u32[]{:S(2)}, u32[]{:S(2)}) async-start(bf16[16,72,512]{2,1,0:T(8,128)(2,1)} %broadcast_in_dim.66), calls=%async_computation.2 | async-start | bytes 2359296 | tf_op jit(solution)/shard_map/all_to_all | solution.py:20
  115.0 1.2 copy-start.2
  117.0 10.2 %collective-permute-start.7 = (f32[12,128]{1,0:T(8,128)S(1)}, f32[12,128]{1,0:T(8,128)S(1)}, u32[]{:S(2)}, u32[]{:S(2)}) collective-permute-start(f32[12,128]{1,0:T(8,128)S(1)} %get-tuple-element.43), channel_id=1, source_target_pairs={{0,16},{16,0},{1,17},{17,1},{2,18},{18,2},{3,19},{19,3},{4,20},{20... | collective-permute-start | bytes 18440 | tf_op jit(solution)/shard_map/ppermute | solution.py:37
  121.0 6.2 %collective-permute-start.8 = (f32[12,128]{1,0:T(8,128)S(1)}, f32[12,128]{1,0:T(8,128)S(1)}, u32[]{:S(2)}, u32[]{:S(2)}) collective-permute-start(f32[12,128]{1,0:T(8,128)S(1)} %get-tuple-element.44), channel_id=1, source_target_pairs={{0,256},{256,0},{1,257},{257,1},{2,258},{258,2},{3,259},{259,3},{4... | collective-permute-start | bytes 18440 | tf_op jit(solution)/shard_map/ppermute | solution.py:37
  125.3 6.4 %collective-permute-start.9 = (f32[12,128]{1,0:T(8,128)S(1)}, f32[12,128]{1,0:T(8,128)S(1)}, u32[]{:S(2)}, u32[]{:S(2)}) collective-permute-start(f32[12,128]{1,0:T(8,128)S(1)} %get-tuple-element.45), channel_id=1, source_target_pairs={{0,272},{16,256},{256,16},{272,0},{1,273},{17,257},{257,17},{273,1... | collective-permute-start | bytes 18440 | tf_op jit(solution)/shard_map/ppermute | solution.py:37
  132.7 42.1 %all-to-all-start.3 = ((bf16[8,72,512]{2,1,0:T(8,128)(2,1)}), bf16[8,72,512]{2,1,0:T(8,128)(2,1)S(1)}, u32[]{:S(2)}, u32[]{:S(2)}) async-start(bf16[8,72,512]{2,1,0:T(8,128)(2,1)} %fusion.3), calls=%async_computation.3 | async-start | bytes 1179648 | tf_op jit(solution)/shard_map/all_to_all | solution.py:20

commit v4 on v3

--- a/solution.py
+++ b/solution.py
@@ -235,17 +235,11 @@
         ),
         preferred_element_type=jnp.float32,
     )
-    slots = slots.reshape(2, pairs, 2, 128)
-
-    def toward(swap_a, swap_zl):
-        for_them = lax.dynamic_index_in_dim(slots, a ^ swap_a, axis=0, keepdims=False)
-        for_them = lax.dynamic_index_in_dim(for_them, zl ^ swap_zl, axis=1, keepdims=False)
-        return jnp.concatenate([for_them, gain.reshape(width // 128, 128)], axis=0)
-
-    small = toward(0, 0)
-    small += flipped(toward(0, 1), ("zl",))
-    small += flipped(toward(1, 0), ("a",))
-    small += flipped(toward(1, 1), ("a", "zl"))
+    slots = slots.reshape(2, pairs, 2, 128).transpose(0, 2, 1, 3).reshape(quads, pairs, 128)
+    gain = jnp.broadcast_to(gain.reshape(1, width // 128, 128), (quads, width // 128, 128))
+    small = jnp.concatenate([slots, gain, jnp.zeros((quads, 4, 128), jnp.float32)], axis=1)
+    small = jnp.sum(exchange(small, ("a", "zl")), axis=0)
+    small = small[: pairs + width // 128]
     gain_halves = [half.reshape(1, width) for half in halves(small[pairs:])]
     extra = jnp.broadcast_to(jnp.concatenate(gain_halves)[None], (pairs, 2, width))
     slot_halves = jnp.concatenate(halves(small[:pairs]), axis=1)[:, None]

time: 178 us -> 174 us (0.978)
  the two profiles are of different devices: /device:TPU:72 before, /device:TPU:64 now
where the time goes in v4:
time: 174 us; the launch traced here: 173 us
  waiting for transfers between devices  69 us (40%)
  starting transfers between devices  50.4 us (29%)
  blocking collectives  34.4 us (20%)
  other arithmetic  8.66 us (5%)
  local copies, waits for them, and re-layouts  7 us (4%)
    all_to_all x3, waiting for transfers between devices, exchange(): return lax.all_to_all(value, axes, split_axis=0, concat_axis=0, tiled=True)  52.3 us
    all_to_all x2, blocking collectives, exchange(): return lax.all_to_all(value, axes, split_axis=0, concat_axis=0, tiled=True)  34.4 us
    all_to_all x3, starting transfers between devices, exchange(): return lax.all_to_all(value, axes, split_axis=0, concat_axis=0, tiled=True)  27.9 us
    ppermute x5, starting transfers between devices, flipped(): return lax.ppermute(value, axes, [(k, last - k) for k in range(last + 1)])  18.4 us
    ppermute x5, waiting for transfers between devices, flipped(): return lax.ppermute(value, axes, [(k, last - k) for k in range(last + 1)])  16.7 us
  transfers between devices with their start and end apart: 10, of which 5 were waited for; matrix products, arithmetic and copies ran while one was open for 5% of the time, Pallas kernels for 0%

profile of v4, /device:TPU:64, one launch (start us, length us, event | category | flops | bytes accessed | tf_op | source)
XLA Modules:
  0.0 173.0 jit_solution(10462565768510782000)
XLA Ops:
  0.7 1.2 fusion.69
  1.9 3.4 %collective-permute-start.4 = (bf16[64,2048]{1,0:T(8,128)(2,1)S(1)}, bf16[64,2048]{1,0:T(8,128)(2,1)S(1)}, u32[]{:S(2)}, u32[]{:S(2)}) collective-permute-start(bf16[64,2048]{1,0:T(8,128)(2,1)S(1)} %get-tuple-element.19), channel_id=1, source_target_pairs={{0,4},{4,0},{8,260},{12,256},{256,12},{260,8},{264,268},{268,264},... | collective-permute-start | bytes 786440 | tf_op jit(solution)/shard_map/ppermute | solution.py:55
  5.3 1.5 reduce_max.25
  8.0 1.3 and_convert_fusion
  9.5 4.6 %collective-permute-start = (bf16[264,512]{1,0:T(8,128)(2,1)S(1)}, bf16[264,512]{1,0:T(8,128)(2,1)S(1)}, u32[]{:S(2)}, u32[]{:S(2)}) collective-permute-start(bf16[264,512]{1,0:T(8,128)(2,1)S(1)} %fusion.11.own), channel_id=1, source_target_pairs={{0,256},{256,0},{1,257},{257,1},{2,258},{258,2},{3,259},{259,3},{4... | collective-permute-start | bytes 811016 | tf_op jit(solution)/shard_map/ppermute | solution.py:37
  14.2 3.8 %collective-permute-start.1 = (bf16[264,512]{1,0:T(8,128)(2,1)S(1)}, bf16[264,512]{1,0:T(8,128)(2,1)S(1)}, u32[]{:S(2)}, u32[]{:S(2)}) collective-permute-start(bf16[264,512]{1,0:T(8,128)(2,1)S(1)} %fusion.11.own), channel_id=1, source_target_pairs={{0,16},{16,0},{1,17},{17,1},{2,18},{18,2},{3,19},{19,3},{4,20},{20... | collective-permute-start | bytes 811016 | tf_op jit(solution)/shard_map/ppermute | solution.py:37
  18.7 0.8 broadcast_in_dim.75
  19.5 13.8 %all-to-all-start = ((bf16[8,64,512]{2,1,0:T(8,128)(2,1)}), bf16[8,64,512]{2,1,0:T(8,128)(2,1)S(1)}, u32[]{:S(2)}, u32[]{:S(2)}) async-start(bf16[8,64,512]{2,1,0:T(8,128)(2,1)} %broadcast_in_dim.75), calls=%async_computation | async-start | bytes 1048576 | tf_op jit(solution)/shard_map/all_to_all | solution.py:20
  34.4 5.1 %collective-permute-start.5 = (bf16[128,1024]{1,0:T(8,128)(2,1)S(1)}, bf16[128,1024]{1,0:T(8,128)(2,1)S(1)}, u32[]{:S(2)}, u32[]{:S(2)}) collective-permute-start(bf16[128,1024]{1,0:T(8,128)(2,1)S(1)} %pad_maximum_fusion.1), channel_id=1, source_target_pairs={{0,2},{2,0},{1,3},{3,1},{4,6},{6,4},{5,7},{7,5},{8,10},{10,8},{9,1... | collective-permute-start | bytes 786440 | tf_op jit(solution)/shard_map/ppermute | solution.py:37
  39.6 2.9 %collective-permute-start.2 = (bf16[264,512]{1,0:T(8,128)(2,1)S(1)}, bf16[264,512]{1,0:T(8,128)(2,1)S(1)}, u32[]{:S(2)}, u32[]{:S(2)}) collective-permute-start(bf16[264,512]{1,0:T(8,128)(2,1)S(1)} %collective-permute-done.across), channel_id=1, source_target_pairs={{0,16},{16,0},{1,17},{17,1},{2,18},{18,2},{3,19},{19,3},{4,20},{20... | collective-permute-start | bytes 811016 | tf_op jit(solution)/shard_map/ppermute | solution.py:37
  42.8 1.7 collective-permute-done.5
  44.5 1.9 %collective-permute-start.6 = (bf16[256,512]{1,0:T(8,128)(2,1)S(1)}, bf16[256,512]{1,0:T(8,128)(2,1)S(1)}, u32[]{:S(2)}, u32[]{:S(2)}) collective-permute-start(bf16[256,512]{1,0:T(8,128)(2,1)S(1)} %pad_maximum_fusion.3), channel_id=1, source_target_pairs={{0,1},{1,0},{2,3},{3,2},{4,5},{5,4},{6,7},{7,6},{8,9},{9,8},{10,11... | collective-permute-start | bytes 786440 | tf_op jit(solution)/shard_map/ppermute | solution.py:37
  46.5 15.0 %collective-permute-done.2.both = bf16[264,512]{1,0:T(8,128)(2,1)S(1)} collective-permute-done((bf16[264,512]{1,0:T(8,128)(2,1)S(1)}, bf16[264,512]{1,0:T(8,128)(2,1)S(1)}, u32[]{:S(2)}, u32[]{:S(2)}) %collective-permute-start.2) | collective-permute-done | bytes 270368 | tf_op jit(solution)/shard_map/ppermute | solution.py:37
  62.1 1.7 all-to-all-done.wd
  63.7 1.3 project.1
  65.0 27.0 %all_to_all.25 = bf16[16,72,512]{2,1,0:T(8,128)(2,1)S(1)} all-to-all(bf16[16,72,512]{2,1,0:T(8,128)(2,1)S(1)} %project.1), channel_id=1, replica_groups=mesh['a'=2,'zh'=8,'zl'=2,'x'=4,'b'=2,'c'=2] {'x','b','c'}, dimensions={0} | all-to-all | bytes 2359296 | tf_op jit(solution)/shard_map/all_to_all | solution.py:20
  92.8 1.1 broadcast_in_dim.76
  93.8 3.7 %all-to-all-start.2 = ((bf16[16,72,512]{2,1,0:T(8,128)(2,1)}), bf16[16,72,512]{2,1,0:T(8,128)(2,1)S(1)}, u32[]{:S(2)}, u32[]{:S(2)}) async-start(bf16[16,72,512]{2,1,0:T(8,128)(2,1)} %broadcast_in_dim.76), calls=%async_computation.2 | async-start | bytes 2359296 | tf_op jit(solution)/shard_map/all_to_all | solution.py:20
  97.7 1.1 pad_maximum_fusion
  98.8 18.1 %all-to-all-done.2 = bf16[16,72,512]{2,1,0:T(8,128)(2,1)S(1)} async-done(((bf16[16,72,512]{2,1,0:T(8,128)(2,1)}), bf16[16,72,512]{2,1,0:T(8,128)(2,1)S(1)}, u32[]{:S(2)}, u32[]{:S(2)}) %all-to-all-start.2) | async-done | bytes 1179680 | tf_op jit(solution)/shard_map/all_to_all | solution.py:20
  119.4 7.4 %all_to_all.26 = f32[4,16,128]{2,1,0:T(8,128)S(1)} all-to-all(f32[4,16,128]{2,1,0:T(8,128)S(1)} %maximum_maximum_fusion), channel_id=1, replica_groups=mesh['a'=2,'zh'=8,'zl'=2,'x'=4,'b'=2,'c'=2] {'a','zl'}, dimensions={0} | all-to-all | bytes 65536 | tf_op jit(solution)/shard_map/all_to_all | solution.py:20
  127.0 0.9 fusion.3
  127.9 10.4 %all-to-all-start.4 = ((bf16[8,72,512]{2,1,0:T(8,128)(2,1)}), bf16[8,72,512]{2,1,0:T(8,128)(2,1)S(1)}, u32[]{:S(2)}, u32[]{:S(2)}) async-start(bf16[8,72,512]{2,1,0:T(8,128)(2,1)} %fusion.3), calls=%async_computation.4 | async-start | bytes 1179648 | tf_op jit(solution)/shard_map/all_to_all | solution.py:20
  138.3 32.5 %all-to-all-done.4 = bf16[8,72,512]{2,1,0:T(8,128)(2,1)S(1)} async-done(((bf16[8,72,512]{2,1,0:T(8,128)(2,1)}), bf16[8,72,512]{2,1,0:T(8,128)(2,1)S(1)}, u32[]{:S(2)}, u32[]{:S(2)}) %all-to-all-start.4) | async-done | bytes 589856 | tf_op jit(solution)/shard_map/all_to_all | solution.py:20
  (121 shorter events, 9.5 us)
Async XLA Ops:
  0.6 6.2 %copy-start = (bf16[256,2000]{0,1:T(8,128)(2,1)S(1)}, bf16[256,2000]{0,1:T(8,128)(2,1)}, u32[]{:S(2)}) copy-start(bf16[256,2000]{0,1:T(8,128)(2,1)} %param.14) | copy-start | bytes 3072004
  0.6 6.7 %copy-start.6 = (s32[1,2]{1,0:T(1,128)S(1)}, s32[1,2]{1,0:T(1,128)}, u32[]{:S(2)}) copy-start(s32[1,2]{1,0:T(1,128)} %param.15) | copy-start | bytes 28
  0.7 7.3 %copy-start.7 = (s32[256]{0:T(256)S(1)}, s32[256]{0:T(256)}, u32[]{:S(2)}) copy-start(s32[256]{0:T(256)} %param.16) | copy-start | bytes 3076
  0.7 8.6 %copy-start.4 = (s32[256,1]{0,1:T(1,128)S(1)}, s32[256,1]{0,1:T(1,128)}, u32[]{:S(2)}) copy-start(s32[256,1]{0,1:T(1,128)} %param.17) | copy-start | bytes 3076
  0.7 8.8 %copy-start.1 = (bf16[256,512]{1,0:T(8,128)(2,1)S(1)}, bf16[256,512]{1,0:T(8,128)(2,1)}, u32[]{:S(2)}) copy-start(bf16[256,512]{1,0:T(8,128)(2,1)} %param.9) | copy-start | bytes 786436
  0.7 18.0 %copy-start.3 = (bf16[64,512]{1,0:T(8,128)(2,1)S(1)}, bf16[64,512]{1,0:T(8,128)(2,1)}, u32[]{:S(2)}) copy-start(bf16[64,512]{1,0:T(8,128)(2,1)} %param.13) | copy-start | bytes 196612
  1.9 32.2 %copy-start.5 = (f32[512]{0:T(512)S(1)}, f32[512]{0:T(512)}, u32[]{:S(2)}) copy-start(f32[512]{0:T(512)} %param.12) | copy-start | bytes 6148
  1.9 32.4 %collective-permute-start.4 = (bf16[64,2048]{1,0:T(8,128)(2,1)S(1)}, bf16[64,2048]{1,0:T(8,128)(2,1)S(1)}, u32[]{:S(2)}, u32[]{:S(2)}) collective-permute-start(bf16[64,2048]{1,0:T(8,128)(2,1)S(1)} %get-tuple-element.19), channel_id=1, source_target_pairs={{0,4},{4,0},{8,260},{12,256},{256,12},{260,8},{264,268},{268,264},... | collective-permute-start | bytes 786440 | tf_op jit(solution)/shard_map/ppermute | solution.py:55
  9.5 30.0 %collective-permute-start = (bf16[264,512]{1,0:T(8,128)(2,1)S(1)}, bf16[264,512]{1,0:T(8,128)(2,1)S(1)}, u32[]{:S(2)}, u32[]{:S(2)}) collective-permute-start(bf16[264,512]{1,0:T(8,128)(2,1)S(1)} %fusion.11.own), channel_id=1, source_target_pairs={{0,256},{256,0},{1,257},{257,1},{2,258},{258,2},{3,259},{259,3},{4... | collective-permute-start | bytes 811016 | tf_op jit(solution)/shard_map/ppermute | solution.py:37
  14.2 28.5 %collective-permute-start.1 = (bf16[264,512]{1,0:T(8,128)(2,1)S(1)}, bf16[264,512]{1,0:T(8,128)(2,1)S(1)}, u32[]{:S(2)}, u32[]{:S(2)}) collective-permute-start(bf16[264,512]{1,0:T(8,128)(2,1)S(1)} %fusion.11.own), channel_id=1, source_target_pairs={{0,16},{16,0},{1,17},{17,1},{2,18},{18,2},{3,19},{19,3},{4,20},{20... | collective-permute-start | bytes 811016 | tf_op jit(solution)/shard_map/ppermute | solution.py:37
  18.0 16.3 %collective-permute-start.3 = (bf16[64,2048]{1,0:T(8,128)(2,1)S(1)}, bf16[64,2048]{1,0:T(8,128)(2,1)S(1)}, u32[]{:S(2)}, u32[]{:S(2)}) collective-permute-start(bf16[64,2048]{1,0:T(8,128)(2,1)S(1)} %get-tuple-element.18), channel_id=1, source_target_pairs={{0,0},{4,4},{8,256},{12,260},{256,8},{260,12},{264,264},{268,268},... | collective-permute-start | bytes 786440 | tf_op jit(solution)/shard_map/ppermute | solution.py:54
  19.5 44.2 %all-to-all-start = ((bf16[8,64,512]{2,1,0:T(8,128)(2,1)}), bf16[8,64,512]{2,1,0:T(8,128)(2,1)S(1)}, u32[]{:S(2)}, u32[]{:S(2)}) async-start(bf16[8,64,512]{2,1,0:T(8,128)(2,1)} %broadcast_in_dim.75), calls=%async_computation | async-start | bytes 1048576 | tf_op jit(solution)/shard_map/all_to_all | solution.py:20
  34.4 10.0 %collective-permute-start.5 = (bf16[128,1024]{1,0:T(8,128)(2,1)S(1)}, bf16[128,1024]{1,0:T(8,128)(2,1)S(1)}, u32[]{:S(2)}, u32[]{:S(2)}) collective-permute-start(bf16[128,1024]{1,0:T(8,128)(2,1)S(1)} %pad_maximum_fusion.1), channel_id=1, source_target_pairs={{0,2},{2,0},{1,3},{3,1},{4,6},{6,4},{5,7},{7,5},{8,10},{10,8},{9,1... | collective-permute-start | bytes 786440 | tf_op jit(solution)/shard_map/ppermute | solution.py:37
  39.6 21.9 %collective-permute-start.2 = (bf16[264,512]{1,0:T(8,128)(2,1)S(1)}, bf16[264,512]{1,0:T(8,128)(2,1)S(1)}, u32[]{:S(2)}, u32[]{:S(2)}) collective-permute-start(bf16[264,512]{1,0:T(8,128)(2,1)S(1)} %collective-permute-done.across), channel_id=1, source_target_pairs={{0,16},{16,0},{1,17},{17,1},{2,18},{18,2},{3,19},{19,3},{4,20},{20... | collective-permute-start | bytes 811016 | tf_op jit(solution)/shard_map/ppermute | solution.py:37
  44.5 17.6 %collective-permute-start.6 = (bf16[256,512]{1,0:T(8,128)(2,1)S(1)}, bf16[256,512]{1,0:T(8,128)(2,1)S(1)}, u32[]{:S(2)}, u32[]{:S(2)}) collective-permute-start(bf16[256,512]{1,0:T(8,128)(2,1)S(1)} %pad_maximum_fusion.3), channel_id=1, source_target_pairs={{0,1},{1,0},{2,3},{3,2},{4,5},{5,4},{6,7},{7,6},{8,9},{9,8},{10,11... | collective-permute-start | bytes 786440 | tf_op jit(solution)/shard_map/ppermute | solution.py:37
  93.8 23.0 %all-to-all-start.2 = ((bf16[16,72,512]{2,1,0:T(8,128)(2,1)}), bf16[16,72,512]{2,1,0:T(8,128)(2,1)S(1)}, u32[]{:S(2)}, u32[]{:S(2)}) async-start(bf16[16,72,512]{2,1,0:T(8,128)(2,1)} %broadcast_in_dim.76), calls=%async_computation.2 | async-start | bytes 2359296 | tf_op jit(solution)/shard_map/all_to_all | solution.py:20
  117.3 1.2 copy-start.2
  127.9 42.9 %all-to-all-start.4 = ((bf16[8,72,512]{2,1,0:T(8,128)(2,1)}), bf16[8,72,512]{2,1,0:T(8,128)(2,1)S(1)}, u32[]{:S(2)}, u32[]{:S(2)}) async-start(bf16[8,72,512]{2,1,0:T(8,128)(2,1)} %fusion.3), calls=%async_computation.4 | async-start | bytes 1179648 | tf_op jit(solution)/shard_map/all_to_all | solution.py:20

commit v5 on v4

--- a/solution.py
+++ b/solution.py
@@ -69,9 +69,12 @@
     return [part.reshape(4, slab, width) for part in parts], 4 * (x % 2) + 2 * b + c
 
 
+LANES = 128
+
+
 def project(place, own, across, beside, both, wd, kept, came, gains, side, out):
     slab = wd.shape[1]
-    mine = out.shape[1] - side.shape[1]
+    mine = (out.shape[1] - side.shape[1]) // 4
     here = place[0]
     draft_gain, target_gain = gains[0:1], gains[1:2]
     for pair in range(4):
@@ -83,7 +86,6 @@
             wt = jnp.where(away % 2 == 1, parts[1].astype(jnp.float32), parts[0].astype(jnp.float32))
             merged.append(wd[k].astype(jnp.float32) * draft_gain - wt * target_gain)
         merged = jnp.concatenate(merged).astype(jnp.bfloat16)
-        lanes = slice(pair * 2 * slab, (pair + 1) * 2 * slab)
         for quad, block in enumerate((own, across, beside, both)):
             value = lax.dot_general(
                 block[: 4 * mine],
@@ -91,10 +93,52 @@
                 (((1,), (1,)), ((), ())),
                 preferred_element_type=jnp.float32,
             )
-            out[4 * quad : 4 * quad + 4, :mine, lanes] = value.astype(jnp.bfloat16).reshape(
-                4, mine, 2 * slab
+            out[4 * quad : 4 * quad + 4, pair * mine : (pair + 1) * mine] = value.astype(
+                jnp.bfloat16
+            ).reshape(4, mine, 2 * slab)
+    out[:, 4 * mine :] = side[...]
+
+
+def backward(got, own, across, beside, both, wd, out, gain):
+    _, slab, width = wd.shape
+    mine = slab
+    total = jnp.zeros((1, width), jnp.float32)
+    for chunk in range(4):
+        grad = jnp.zeros((LANES, width), jnp.float32)
+        for quad, block in enumerate((own, across, beside, both)):
+            slope = got[4 * quad : 4 * quad + 4, chunk * mine : (chunk + 1) * mine]
+            grad += lax.dot_general(
+                slope.reshape(4 * mine, LANES),
+                block[: 4 * mine],
+                (((0,), (0,)), ((), ())),
+                preferred_element_type=jnp.float32,
             )
-    out[:, mine:] = side[...]
+        for k in range(2):
+            rows = grad[k * slab : (k + 1) * slab]
+            total += jnp.sum(rows * wd[2 * chunk + k].astype(jnp.float32), axis=0, keepdims=True)
+            for part in range(width // LANES):
+                out[2 * chunk + k, part * slab : (part + 1) * slab] = rows[
+                    :, part * LANES : (part + 1) * LANES
+                ].astype(jnp.bfloat16)
+    gain[...] = total
+
+
+def on_chip(kernel, out_shape, flops, moved, *args, scalars=0):
+    space = [pl.BlockSpec(memory_space=pltpu.SMEM)] * scalars
+    space += [pl.BlockSpec(memory_space=pltpu.VMEM)] * (len(args) - scalars)
+    return pl.pallas_call(
+        kernel,
+        out_shape=out_shape,
+        in_specs=space,
+        out_specs=jax.tree.map(lambda _: pl.BlockSpec(memory_space=pltpu.VMEM), out_shape),
+        cost_estimate=pl.CostEstimate(flops=flops, bytes_accessed=moved, transcendentals=0),
+        compiler_params=pltpu.CompilerParams(vmem_limit_bytes=16 * 2**20),
+    )(*args)
+
+
+def spread_gain(part, slab):
+    part = part.reshape(-1, 1, LANES)
+    return lax.optimization_barrier(jnp.broadcast_to(part, (part.shape[0], slab, LANES)))
 
 
 def softmax_parts(logit_rows):
@@ -170,28 +214,24 @@
     squares = jnp.stack(halves(jnp.stack(squares))).reshape(2, models, mine)
     facts_here = facts_here.swapaxes(0, 1).reshape(kinds, models, mine)
     side = jnp.concatenate([facts_here, squares], axis=0).swapaxes(0, 1)
-    side = side.reshape(models, 1, (kinds + 2) * mine)
-    side = jnp.pad(side, ((0, 0), (0, 0), (0, 8 * columns - side.shape[2]))).reshape(models, 8, columns)
-    partial = pl.pallas_call(
+    side = side.reshape(models, (kinds + 2) * mine // LANES, LANES)
+    side = jnp.pad(side, ((0, 0), (0, 8 - side.shape[1]), (0, 0)))
+    held = columns // LANES * mine
+    flops = 2 * all_rows * width * columns
+    moved = 2 * (2 * all_rows * width + 2 * columns * width)
+    wd = wd.reshape(pairs, slab, width)
+    partial = on_chip(
         project,
-        out_shape=jax.ShapeDtypeStruct((models, mine + 8, columns), jnp.bfloat16),
-        in_specs=[pl.BlockSpec(memory_space=pltpu.SMEM)]
-        + [pl.BlockSpec(memory_space=pltpu.VMEM)] * 9,
-        out_specs=pl.BlockSpec(memory_space=pltpu.VMEM),
-        cost_estimate=pl.CostEstimate(
-            flops=2 * all_rows * width * columns,
-            bytes_accessed=2 * (2 * all_rows * width + 2 * columns * width),
-            transcendentals=0,
-        ),
-        compiler_params=pltpu.CompilerParams(vmem_limit_bytes=16 * 2**20),
-        name="project",
-    )(place.reshape(1), *blocks, wd.reshape(pairs, slab, width), kept, came, gains, side)
+        jax.ShapeDtypeStruct((models, held + 8, LANES), jnp.bfloat16),
+        flops,
+        moved,
+        *(place.reshape(1), *blocks, wd, kept, came, gains, side),
+        scalars=1,
+    )
     got = exchange(partial, MP)
-    features_here = lax.optimization_barrier(
-        jnp.concatenate([block[:rows] for block in blocks], axis=0)
-    )
-    summed = jnp.sum(got[:, :mine].astype(jnp.float32), axis=0)
-    side = got[:, mine:].reshape(models, 8 * columns)[:, : (kinds + 2) * mine]
+    first_gain = spread_gain(draft_gain[: width // 2], slab)
+    summed = jnp.sum(got[:, :held].astype(jnp.float32), axis=0).reshape(held // mine, mine, LANES)
+    side = got[:, held : held + (kinds + 2) * mine // LANES]
     side = side.reshape(models, kinds + 2, mine).astype(jnp.float32)
     peaks = side[:, 0]
     totals = side[:, 1] + side[:, 2]
@@ -205,20 +245,26 @@
     weight = (side[0, 5] * entropy / math.log(VOCAB)).astype(jnp.bfloat16).astype(jnp.float32)
     square = jnp.sum(side[:, 8] + side[:, 9], axis=0)
     inverse = lax.rsqrt(square / features + EPSILON)
-    error = summed * inverse[:, None]
-    loss = 0.5 * weight * jnp.sum(error * error, axis=1) * scale
-    slope = (error * (weight * inverse * scale)[:, None]).astype(jnp.bfloat16)
+    error = summed * inverse[None, :, None]
+    loss = 0.5 * weight * jnp.sum(error * error, axis=(0, 2)) * scale
+    slope = (error * (weight * inverse * scale)[None, :, None]).astype(jnp.bfloat16)
     tail = jnp.concatenate(
         [jnp.stack(halves(loss)), side[0, 6:8].astype(jnp.bfloat16)], axis=0
-    )
-    tail = jnp.pad(tail, ((0, 4), (0, columns - mine)))
-    got = spread(jnp.concatenate([slope, tail], axis=0), MP)
-    slope = got[:, :mine].reshape(all_rows, columns)
-    tail = got[:, mine : mine + 4, :mine].swapaxes(0, 1).reshape(4, all_rows)
-    grad = lax.dot_general(
-        slope, features_here, (((0,), (0,)), ((), ())), preferred_element_type=jnp.float32
-    )
-    gain = jnp.sum(grad * wd.astype(jnp.float32), axis=0)
+    ).reshape(4 * mine // LANES, LANES)
+    tail = jnp.pad(tail, ((0, 8 - tail.shape[0]), (0, 0)))
+    got = spread(jnp.concatenate([slope.reshape(held, LANES), tail], axis=0), MP)
+    tail = got[:, held : held + 4 * mine // LANES].reshape(models, 4, mine)
+    tail = tail.swapaxes(0, 1).reshape(4, all_rows)
+    grad, gain = on_chip(
+        backward,
+        (
+            jax.ShapeDtypeStruct((pairs, width // LANES * slab, LANES), jnp.bfloat16),
+            jax.ShapeDtypeStruct((1, width), jnp.float32),
+        ),
+        flops,
+        moved,
+        *(got, *blocks, wd),
+    )
 
     named = tail[2][None, :] == jnp.arange(groups, dtype=jnp.bfloat16)[:, None]
     block = jnp.arange(all_rows, dtype=jnp.int32) // rows
@@ -240,20 +286,22 @@
     small = jnp.concatenate([slots, gain, jnp.zeros((quads, 4, 128), jnp.float32)], axis=1)
     small = jnp.sum(exchange(small, ("a", "zl")), axis=0)
     small = small[: pairs + width // 128]
-    gain_halves = [half.reshape(1, width) for half in halves(small[pairs:])]
-    extra = jnp.broadcast_to(jnp.concatenate(gain_halves)[None], (pairs, 2, width))
-    slot_halves = jnp.concatenate(halves(small[:pairs]), axis=1)[:, None]
-    extra = jnp.concatenate([extra, jnp.pad(slot_halves, ((0, 0), (0, 0), (0, width - 256)))], axis=1)
-    extra = jnp.pad(extra, ((0, 0), (0, 5), (0, 0)))
-    parts = exchange(
-        jnp.concatenate([grad.astype(jnp.bfloat16).reshape(pairs, slab, width), extra], axis=1),
-        "zh",
-    )
-    spread_gain = lax.optimization_barrier(jnp.broadcast_to(draft_gain, (slab, width)) + 0.0)
-    grad_weight = jnp.sum(parts[:, :slab].astype(jnp.float32), axis=0) * spread_gain
-    extra = parts[:, slab : slab + 3].astype(jnp.float32)
-    grad_gain = jnp.sum(extra[:, :2], axis=(0, 1))
-    slots = extra[:, 2, : quads * CAP] + extra[:, 2, 128 : 128 + quads * CAP]
+    sent_gain = jnp.broadcast_to(
+        small[pairs:].astype(jnp.bfloat16)[None], (pairs, width // LANES, LANES)
+    )
+    sent_slots = jnp.concatenate([half[:, :64] for half in halves(small[:pairs])], axis=1)
+    extra = jnp.concatenate([sent_gain, sent_slots[:, None]], axis=1)
+    extra = jnp.pad(extra, ((0, 0), (0, 8 - extra.shape[1]), (0, 0)))
+    parts = exchange(jnp.concatenate([grad, extra], axis=1), "zh")
+    last_gain = spread_gain(draft_gain[width // 2 :], slab)
+    chunks = width // LANES
+    grad_weight = jnp.sum(parts[:, : chunks * slab].astype(jnp.float32), axis=0)
+    grad_weight = grad_weight.reshape(chunks, slab, LANES)
+    grad_weight *= jnp.concatenate([first_gain, last_gain], axis=0)
+    grad_weight = grad_weight.swapaxes(0, 1).reshape(slab, width)
+    extra = parts[:, chunks * slab :].astype(jnp.float32)
+    grad_gain = jnp.sum(extra[:, :chunks], axis=0).reshape(width)
+    slots = extra[:, chunks, : quads * CAP] + extra[:, chunks, 64 : 64 + quads * CAP]
     slots = slots.reshape(pairs, 2, 2, CAP).transpose(1, 0, 2, 3)
     return (grad_weight, grad_gain, slots.reshape(groups * CAP))
 

time: 174 us -> 170 us (0.977)
  waiting for transfers between devices: 69 us -> 67 us
    all_to_all x3, waiting for transfers between devices: 52.3 us -> 50.3 us  [exchange(): return lax.all_to_all(value, axes, split_axis=0, concat_axis=0, tiled=True)]
  transfers between devices with their start and end apart: 10 -> 10, of which waited for: 5 -> 5; matrix products, arithmetic and copies ran while one was open for 5% -> 4% of each run, Pallas kernels for 0% -> 0%
where the time goes in v5:
time: 170 us; the launch traced here: 169 us
  waiting for transfers between devices  67 us (39%)
  starting transfers between devices  50.3 us (30%)
  blocking collectives  33.8 us (20%)
  other arithmetic  7.62 us (4%)
  local copies, waits for them, and re-layouts  6.71 us (4%)
  Pallas kernels  2.02 us (1%)
    all_to_all x3, waiting for transfers between devices, exchange(): return lax.all_to_all(value, axes, split_axis=0, concat_axis=0, tiled=True)  50.3 us
    all_to_all x2, blocking collectives, exchange(): return lax.all_to_all(value, axes, split_axis=0, concat_axis=0, tiled=True)  33.8 us
    all_to_all x3, starting transfers between devices, exchange(): return lax.all_to_all(value, axes, split_axis=0, concat_axis=0, tiled=True)  27.9 us
    ppermute x5, starting transfers between devices, flipped(): return lax.ppermute(value, axes, [(k, last - k) for k in range(last + 1)])  18.4 us
    ppermute x5, waiting for transfers between devices, flipped(): return lax.ppermute(value, axes, [(k, last - k) for k in range(last + 1)])  16.7 us
  transfers between devices with their start and end apart: 10, of which 5 were waited for; matrix products, arithmetic and copies ran while one was open for 4% of the time, Pallas kernels for 0%

profile of v5, /device:TPU:64, one launch (start us, length us, event | category | flops | bytes accessed | tf_op | source)
XLA Modules:
  0.0 168.8 jit_solution(15286113401480850469)
XLA Ops:
  0.7 1.2 fusion.58
  1.9 3.4 %collective-permute-start.4 = (bf16[64,2048]{1,0:T(8,128)(2,1)S(1)}, bf16[64,2048]{1,0:T(8,128)(2,1)S(1)}, u32[]{:S(2)}, u32[]{:S(2)}) collective-permute-start(bf16[64,2048]{1,0:T(8,128)(2,1)S(1)} %get-tuple-element.20), channel_id=1, source_target_pairs={{0,4},{4,0},{8,260},{12,256},{256,12},{260,8},{264,268},{268,264},... | collective-permute-start | bytes 786440 | tf_op jit(solution)/shard_map/ppermute | solution.py:55
  5.3 1.5 reduce_max.25
  8.0 1.3 and_convert_fusion
  9.5 4.6 %collective-permute-start = (bf16[264,512]{1,0:T(8,128)(2,1)S(1)}, bf16[264,512]{1,0:T(8,128)(2,1)S(1)}, u32[]{:S(2)}, u32[]{:S(2)}) collective-permute-start(bf16[264,512]{1,0:T(8,128)(2,1)S(1)} %fusion.8.own), channel_id=1, source_target_pairs={{0,256},{256,0},{1,257},{257,1},{2,258},{258,2},{3,259},{259,3},{4... | collective-permute-start | bytes 811016 | tf_op jit(solution)/shard_map/ppermute | solution.py:37
  14.2 3.8 %collective-permute-start.1 = (bf16[264,512]{1,0:T(8,128)(2,1)S(1)}, bf16[264,512]{1,0:T(8,128)(2,1)S(1)}, u32[]{:S(2)}, u32[]{:S(2)}) collective-permute-start(bf16[264,512]{1,0:T(8,128)(2,1)S(1)} %fusion.8.own), channel_id=1, source_target_pairs={{0,16},{16,0},{1,17},{17,1},{2,18},{18,2},{3,19},{19,3},{4,20},{20... | collective-permute-start | bytes 811016 | tf_op jit(solution)/shard_map/ppermute | solution.py:37
  18.7 0.8 broadcast_in_dim.82
  19.5 13.8 %all-to-all-start = ((bf16[8,64,512]{2,1,0:T(8,128)(2,1)}), bf16[8,64,512]{2,1,0:T(8,128)(2,1)S(1)}, u32[]{:S(2)}, u32[]{:S(2)}) async-start(bf16[8,64,512]{2,1,0:T(8,128)(2,1)} %broadcast_in_dim.82), calls=%async_computation | async-start | bytes 1048576 | tf_op jit(solution)/shard_map/all_to_all | solution.py:20
  33.4 0.8 dynamic_slice.43
  34.4 5.1 %collective-permute-start.5 = (bf16[128,1024]{1,0:T(8,128)(2,1)S(1)}, bf16[128,1024]{1,0:T(8,128)(2,1)S(1)}, u32[]{:S(2)}, u32[]{:S(2)}) collective-permute-start(bf16[128,1024]{1,0:T(8,128)(2,1)S(1)} %pad_maximum_fusion.1), channel_id=1, source_target_pairs={{0,2},{2,0},{1,3},{3,1},{4,6},{6,4},{5,7},{7,5},{8,10},{10,8},{9,1... | collective-permute-start | bytes 786440 | tf_op jit(solution)/shard_map/ppermute | solution.py:37
  39.6 2.9 %collective-permute-start.2 = (bf16[264,512]{1,0:T(8,128)(2,1)S(1)}, bf16[264,512]{1,0:T(8,128)(2,1)S(1)}, u32[]{:S(2)}, u32[]{:S(2)}) collective-permute-start(bf16[264,512]{1,0:T(8,128)(2,1)S(1)} %collective-permute-done.across), channel_id=1, source_target_pairs={{0,16},{16,0},{1,17},{17,1},{2,18},{18,2},{3,19},{19,3},{4,20},{20... | collective-permute-start | bytes 811016 | tf_op jit(solution)/shard_map/ppermute | solution.py:37
  42.8 1.7 collective-permute-done.5
  44.5 1.9 %collective-permute-start.6 = (bf16[256,512]{1,0:T(8,128)(2,1)S(1)}, bf16[256,512]{1,0:T(8,128)(2,1)S(1)}, u32[]{:S(2)}, u32[]{:S(2)}) collective-permute-start(bf16[256,512]{1,0:T(8,128)(2,1)S(1)} %pad_maximum_fusion.3), channel_id=1, source_target_pairs={{0,1},{1,0},{2,3},{3,2},{4,5},{5,4},{6,7},{7,6},{8,9},{9,8},{10,11... | collective-permute-start | bytes 786440 | tf_op jit(solution)/shard_map/ppermute | solution.py:37
  46.4 15.0 %collective-permute-done.2.both = bf16[264,512]{1,0:T(8,128)(2,1)S(1)} collective-permute-done((bf16[264,512]{1,0:T(8,128)(2,1)S(1)}, bf16[264,512]{1,0:T(8,128)(2,1)S(1)}, u32[]{:S(2)}, u32[]{:S(2)}) %collective-permute-start.2) | collective-permute-done | bytes 270368 | tf_op jit(solution)/shard_map/ppermute | solution.py:37
  62.0 1.7 %all-to-all-done.wd = bf16[8,64,512]{2,1,0:T(8,128)(2,1)S(1)} async-done(((bf16[8,64,512]{2,1,0:T(8,128)(2,1)}), bf16[8,64,512]{2,1,0:T(8,128)(2,1)S(1)}, u32[]{:S(2)}, u32[]{:S(2)}) %all-to-all-start) | async-done | bytes 524320 | tf_op jit(solution)/shard_map/all_to_all | solution.py:20
  63.7 1.3 shard_map.112
  65.0 26.3 %all_to_all.25 = bf16[16,264,128]{2,1,0:T(8,128)(2,1)S(1)} all-to-all(bf16[16,264,128]{2,1,0:T(8,128)(2,1)S(1)} %shard_map.112), channel_id=1, replica_groups=mesh['a'=2,'zh'=8,'zl'=2,'x'=4,'b'=2,'c'=2] {'x','b','c'}, dimensions={0} | all-to-all | bytes 2162688 | tf_op jit(solution)/shard_map/all_to_all | solution.py:20
  92.4 1.1 broadcast_in_dim.83
  93.5 3.7 %all-to-all-start.2 = ((bf16[16,264,128]{2,1,0:T(8,128)(2,1)}), bf16[16,264,128]{2,1,0:T(8,128)(2,1)S(1)}, u32[]{:S(2)}, u32[]{:S(2)}) async-start(bf16[16,264,128]{2,1,0:T(8,128)(2,1)} %broadcast_in_dim.83), calls=%async_computation.2 | async-start | bytes 2162688 | tf_op jit(solution)/shard_map/all_to_all | solution.py:20
  97.3 18.2 %all-to-all-done.2.got = bf16[16,264,128]{2,1,0:T(8,128)(2,1)S(1)} async-done(((bf16[16,264,128]{2,1,0:T(8,128)(2,1)}), bf16[16,264,128]{2,1,0:T(8,128)(2,1)S(1)}, u32[]{:S(2)}, u32[]{:S(2)}) %all-to-all-start.2) | async-done | bytes 1081376 | tf_op jit(solution)/shard_map/all_to_all | solution.py:20
  117.5 7.4 %all_to_all.26 = f32[4,16,128]{2,1,0:T(8,128)S(1)} all-to-all(f32[4,16,128]{2,1,0:T(8,128)S(1)} %maximum_maximum_fusion), channel_id=1, replica_groups=mesh['a'=2,'zh'=8,'zl'=2,'x'=4,'b'=2,'c'=2] {'a','zl'}, dimensions={0} | all-to-all | bytes 65536 | tf_op jit(solution)/shard_map/all_to_all | solution.py:20
  125.1 0.8 pad_maximum_fusion
  125.9 10.3 %all-to-all-start.4 = ((bf16[8,264,128]{2,1,0:T(8,128)(2,1)}), bf16[8,264,128]{2,1,0:T(8,128)(2,1)S(1)}, u32[]{:S(2)}, u32[]{:S(2)}) async-start(bf16[8,264,128]{2,1,0:T(8,128)(2,1)} %pad_maximum_fusion), calls=%async_computation.4 | async-start | bytes 1081344 | tf_op jit(solution)/shard_map/all_to_all | solution.py:20
  136.3 30.4 %all-to-all-done.4 = bf16[8,264,128]{2,1,0:T(8,128)(2,1)S(1)} async-done(((bf16[8,264,128]{2,1,0:T(8,128)(2,1)}), bf16[8,264,128]{2,1,0:T(8,128)(2,1)S(1)}, u32[]{:S(2)}, u32[]{:S(2)}) %all-to-all-start.4) | async-done | bytes 540704 | tf_op jit(solution)/shard_map/all_to_all | solution.py:20
  (117 shorter events, 8.5 us)
Async XLA Ops:
  0.6 6.2 %copy-start = (bf16[256,2000]{0,1:T(8,128)(2,1)S(1)}, bf16[256,2000]{0,1:T(8,128)(2,1)}, u32[]{:S(2)}) copy-start(bf16[256,2000]{0,1:T(8,128)(2,1)} %param.14) | copy-start | bytes 3072004
  0.6 6.7 %copy-start.5 = (s32[1,2]{1,0:T(1,128)S(1)}, s32[1,2]{1,0:T(1,128)}, u32[]{:S(2)}) copy-start(s32[1,2]{1,0:T(1,128)} %param.15) | copy-start | bytes 28
  0.7 7.3 %copy-start.6 = (s32[256]{0:T(256)S(1)}, s32[256]{0:T(256)}, u32[]{:S(2)}) copy-start(s32[256]{0:T(256)} %param.16) | copy-start | bytes 3076
  0.7 8.6 %copy-start.3 = (s32[256,1]{0,1:T(1,128)S(1)}, s32[256,1]{0,1:T(1,128)}, u32[]{:S(2)}) copy-start(s32[256,1]{0,1:T(1,128)} %param.17) | copy-start | bytes 3076
  0.7 8.8 %copy-start.1 = (bf16[256,512]{1,0:T(8,128)(2,1)S(1)}, bf16[256,512]{1,0:T(8,128)(2,1)}, u32[]{:S(2)}) copy-start(bf16[256,512]{1,0:T(8,128)(2,1)} %param.9) | copy-start | bytes 786436
  0.7 18.0 %copy-start.2 = (bf16[64,512]{1,0:T(8,128)(2,1)S(1)}, bf16[64,512]{1,0:T(8,128)(2,1)}, u32[]{:S(2)}) copy-start(bf16[64,512]{1,0:T(8,128)(2,1)} %param.13) | copy-start | bytes 196612
  1.9 32.2 %copy-start.4 = (f32[512]{0:T(512)S(1)}, f32[512]{0:T(512)}, u32[]{:S(2)}) copy-start(f32[512]{0:T(512)} %param.12) | copy-start | bytes 6148
  1.9 32.4 %collective-permute-start.4 = (bf16[64,2048]{1,0:T(8,128)(2,1)S(1)}, bf16[64,2048]{1,0:T(8,128)(2,1)S(1)}, u32[]{:S(2)}, u32[]{:S(2)}) collective-permute-start(bf16[64,2048]{1,0:T(8,128)(2,1)S(1)} %get-tuple-element.20), channel_id=1, source_target_pairs={{0,4},{4,0},{8,260},{12,256},{256,12},{260,8},{264,268},{268,264},... | collective-permute-start | bytes 786440 | tf_op jit(solution)/shard_map/ppermute | solution.py:55
  9.5 30.0 %collective-permute-start = (bf16[264,512]{1,0:T(8,128)(2,1)S(1)}, bf16[264,512]{1,0:T(8,128)(2,1)S(1)}, u32[]{:S(2)}, u32[]{:S(2)}) collective-permute-start(bf16[264,512]{1,0:T(8,128)(2,1)S(1)} %fusion.8.own), channel_id=1, source_target_pairs={{0,256},{256,0},{1,257},{257,1},{2,258},{258,2},{3,259},{259,3},{4... | collective-permute-start | bytes 811016 | tf_op jit(solution)/shard_map/ppermute | solution.py:37
  14.2 28.5 %collective-permute-start.1 = (bf16[264,512]{1,0:T(8,128)(2,1)S(1)}, bf16[264,512]{1,0:T(8,128)(2,1)S(1)}, u32[]{:S(2)}, u32[]{:S(2)}) collective-permute-start(bf16[264,512]{1,0:T(8,128)(2,1)S(1)} %fusion.8.own), channel_id=1, source_target_pairs={{0,16},{16,0},{1,17},{17,1},{2,18},{18,2},{3,19},{19,3},{4,20},{20... | collective-permute-start | bytes 811016 | tf_op jit(solution)/shard_map/ppermute | solution.py:37
  18.0 16.3 %collective-permute-start.3 = (bf16[64,2048]{1,0:T(8,128)(2,1)S(1)}, bf16[64,2048]{1,0:T(8,128)(2,1)S(1)}, u32[]{:S(2)}, u32[]{:S(2)}) collective-permute-start(bf16[64,2048]{1,0:T(8,128)(2,1)S(1)} %get-tuple-element.19), channel_id=1, source_target_pairs={{0,0},{4,4},{8,256},{12,260},{256,8},{260,12},{264,264},{268,268},... | collective-permute-start | bytes 786440 | tf_op jit(solution)/shard_map/ppermute | solution.py:54
  19.5 44.2 %all-to-all-start = ((bf16[8,64,512]{2,1,0:T(8,128)(2,1)}), bf16[8,64,512]{2,1,0:T(8,128)(2,1)S(1)}, u32[]{:S(2)}, u32[]{:S(2)}) async-start(bf16[8,64,512]{2,1,0:T(8,128)(2,1)} %broadcast_in_dim.82), calls=%async_computation | async-start | bytes 1048576 | tf_op jit(solution)/shard_map/all_to_all | solution.py:20
  34.4 10.0 %collective-permute-start.5 = (bf16[128,1024]{1,0:T(8,128)(2,1)S(1)}, bf16[128,1024]{1,0:T(8,128)(2,1)S(1)}, u32[]{:S(2)}, u32[]{:S(2)}) collective-permute-start(bf16[128,1024]{1,0:T(8,128)(2,1)S(1)} %pad_maximum_fusion.1), channel_id=1, source_target_pairs={{0,2},{2,0},{1,3},{3,1},{4,6},{6,4},{5,7},{7,5},{8,10},{10,8},{9,1... | collective-permute-start | bytes 786440 | tf_op jit(solution)/shard_map/ppermute | solution.py:37
  39.6 21.9 %collective-permute-start.2 = (bf16[264,512]{1,0:T(8,128)(2,1)S(1)}, bf16[264,512]{1,0:T(8,128)(2,1)S(1)}, u32[]{:S(2)}, u32[]{:S(2)}) collective-permute-start(bf16[264,512]{1,0:T(8,128)(2,1)S(1)} %collective-permute-done.across), channel_id=1, source_target_pairs={{0,16},{16,0},{1,17},{17,1},{2,18},{18,2},{3,19},{19,3},{4,20},{20... | collective-permute-start | bytes 811016 | tf_op jit(solution)/shard_map/ppermute | solution.py:37
  44.5 17.5 %collective-permute-start.6 = (bf16[256,512]{1,0:T(8,128)(2,1)S(1)}, bf16[256,512]{1,0:T(8,128)(2,1)S(1)}, u32[]{:S(2)}, u32[]{:S(2)}) collective-permute-start(bf16[256,512]{1,0:T(8,128)(2,1)S(1)} %pad_maximum_fusion.3), channel_id=1, source_target_pairs={{0,1},{1,0},{2,3},{3,2},{4,5},{5,4},{6,7},{7,6},{8,9},{9,8},{10,11... | collective-permute-start | bytes 786440 | tf_op jit(solution)/shard_map/ppermute | solution.py:37
  93.5 22.0 %all-to-all-start.2 = ((bf16[16,264,128]{2,1,0:T(8,128)(2,1)}), bf16[16,264,128]{2,1,0:T(8,128)(2,1)S(1)}, u32[]{:S(2)}, u32[]{:S(2)}) async-start(bf16[16,264,128]{2,1,0:T(8,128)(2,1)} %broadcast_in_dim.83), calls=%async_computation.2 | async-start | bytes 2162688 | tf_op jit(solution)/shard_map/all_to_all | solution.py:20
  125.9 40.7 %all-to-all-start.4 = ((bf16[8,264,128]{2,1,0:T(8,128)(2,1)}), bf16[8,264,128]{2,1,0:T(8,128)(2,1)S(1)}, u32[]{:S(2)}, u32[]{:S(2)}) async-start(bf16[8,264,128]{2,1,0:T(8,128)(2,1)} %pad_maximum_fusion), calls=%async_computation.4 | async-start | bytes 1081344 | tf_op jit(solution)/shard_map/all_to_all | solution.py:20

commit v6 on v5

--- a/solution.py
+++ b/solution.py
@@ -123,6 +123,25 @@
     gain[...] = total
 
 
+def finish(parts, first_gain, last_gain, grad, gain, slots):
+    pairs = parts.shape[0]
+    slab, width = grad.shape
+    chunks = width // LANES
+    for chunk in range(chunks):
+        total = parts[0, chunk * slab : (chunk + 1) * slab].astype(jnp.float32)
+        for k in range(1, pairs):
+            total += parts[k, chunk * slab : (chunk + 1) * slab].astype(jnp.float32)
+        held = first_gain if chunk < chunks // 2 else last_gain
+        grad[:, chunk * LANES : (chunk + 1) * LANES] = total * held[chunk % (chunks // 2), 0:1]
+    total = parts[0, chunks * slab :].astype(jnp.float32)
+    slots[0:1] = total[chunks : chunks + 1]
+    for k in range(1, pairs):
+        extra = parts[k, chunks * slab :].astype(jnp.float32)
+        slots[k : k + 1] = extra[chunks : chunks + 1]
+        total += extra
+    gain[...] = total[:chunks]
+
+
 def on_chip(kernel, out_shape, flops, moved, *args, scalars=0):
     space = [pl.BlockSpec(memory_space=pltpu.SMEM)] * scalars
     space += [pl.BlockSpec(memory_space=pltpu.VMEM)] * (len(args) - scalars)
@@ -136,9 +155,9 @@
     )(*args)
 
 
-def spread_gain(part, slab):
+def spread_gain(part):
     part = part.reshape(-1, 1, LANES)
-    return lax.optimization_barrier(jnp.broadcast_to(part, (part.shape[0], slab, LANES)))
+    return lax.optimization_barrier(jnp.broadcast_to(part, (part.shape[0], 8, LANES)))
 
 
 def softmax_parts(logit_rows):
@@ -175,8 +194,9 @@
     scale = 1.0 / math.sqrt(rows * groups)
 
     index = jnp.arange(rows, dtype=jnp.int32)
-    length = jnp.where(index < LEN, seq_lens[0, 0], seq_lens[0, 1])
-    valid = jnp.logical_and(index % LEN < length - 1, tool_mask == 1)
+    position = jnp.arange(LEN, dtype=jnp.int32)[None, :]
+    reached = position < seq_lens[0][:, None] - 1
+    valid = jnp.logical_and(reached, tool_mask.reshape(-1, LEN) == 1).reshape(rows)
     owner = owners[:, 0]
     earlier = jnp.logical_and(
         owner[:, None] == owner[None, :], index[:, None] < index[None, :]
@@ -229,7 +249,7 @@
         scalars=1,
     )
     got = exchange(partial, MP)
-    first_gain = spread_gain(draft_gain[: width // 2], slab)
+    first_gain = spread_gain(draft_gain[: width // 2])
     summed = jnp.sum(got[:, :held].astype(jnp.float32), axis=0).reshape(held // mine, mine, LANES)
     side = got[:, held : held + (kinds + 2) * mine // LANES]
     side = side.reshape(models, kinds + 2, mine).astype(jnp.float32)
@@ -293,15 +313,20 @@
     extra = jnp.concatenate([sent_gain, sent_slots[:, None]], axis=1)
     extra = jnp.pad(extra, ((0, 0), (0, 8 - extra.shape[1]), (0, 0)))
     parts = exchange(jnp.concatenate([grad, extra], axis=1), "zh")
-    last_gain = spread_gain(draft_gain[width // 2 :], slab)
-    chunks = width // LANES
-    grad_weight = jnp.sum(parts[:, : chunks * slab].astype(jnp.float32), axis=0)
-    grad_weight = grad_weight.reshape(chunks, slab, LANES)
-    grad_weight *= jnp.concatenate([first_gain, last_gain], axis=0)
-    grad_weight = grad_weight.swapaxes(0, 1).reshape(slab, width)
-    extra = parts[:, chunks * slab :].astype(jnp.float32)
-    grad_gain = jnp.sum(extra[:, :chunks], axis=0).reshape(width)
-    slots = extra[:, chunks, : quads * CAP] + extra[:, chunks, 64 : 64 + quads * CAP]
+    last_gain = spread_gain(draft_gain[width // 2 :])
+    grad_weight, grad_gain, slots = on_chip(
+        finish,
+        (
+            jax.ShapeDtypeStruct((slab, width), jnp.float32),
+            jax.ShapeDtypeStruct((width // LANES, LANES), jnp.float32),
+            jax.ShapeDtypeStruct((pairs, LANES), jnp.float32),
+        ),
+        pairs * slab * width,
+        (2 * pairs + 4) * slab * width,
+        *(parts, first_gain, last_gain),
+    )
+    grad_gain = grad_gain.reshape(width)
+    slots = slots[:, : quads * CAP] + slots[:, 64 : 64 + quads * CAP]
     slots = slots.reshape(pairs, 2, 2, CAP).transpose(1, 0, 2, 3)
     return (grad_weight, grad_gain, slots.reshape(groups * CAP))
 

time: 170 us -> 167 us (0.982)
  other arithmetic: 7.62 us -> 5.05 us
  transfers between devices with their start and end apart: 10 -> 10, of which waited for: 5 -> 5; matrix products, arithmetic and copies ran while one was open for 4% -> 3% of each run, Pallas kernels for 0% -> 0%
where the time goes in v6:
time: 167 us; the launch traced here: 166 us
  waiting for transfers between devices  67 us (40%)
  starting transfers between devices  50.3 us (30%)
  blocking collectives  33.8 us (20%)
  local copies, waits for them, and re-layouts  6.12 us (4%)
  other arithmetic  5.05 us (3%)
  Pallas kernels  2.76 us (2%)
    all_to_all x3, waiting for transfers between devices, exchange(): return lax.all_to_all(value, axes, split_axis=0, concat_axis=0, tiled=True)  50.3 us
    all_to_all x2, blocking collectives, exchange(): return lax.all_to_all(value, axes, split_axis=0, concat_axis=0, tiled=True)  33.8 us
    all_to_all x3, starting transfers between devices, exchange(): return lax.all_to_all(value, axes, split_axis=0, concat_axis=0, tiled=True)  27.9 us
    ppermute x5, starting transfers between devices, flipped(): return lax.ppermute(value, axes, [(k, last - k) for k in range(last + 1)])  18.4 us
    ppermute x5, waiting for transfers between devices, flipped(): return lax.ppermute(value, axes, [(k, last - k) for k in range(last + 1)])  16.7 us
    ppermute x1, starting transfers between devices, teacher_block(): far = lax.ppermute(piece(2 * a + 1 - x % 2), ('a', 'x'), turn(1))  3.4 us
  transfers between devices with their start and end apart: 10, of which 5 were waited for; matrix products, arithmetic and copies ran while one was open for 3% of the time, Pallas kernels for 0%

profile of v6, /device:TPU:64, one launch (start us, length us, event | category | flops | bytes accessed | tf_op | source)
XLA Modules:
  0.0 166.4 jit_solution(8270532803691095829)
XLA Ops:
  0.7 1.2 fusion.56
  1.9 3.4 %collective-permute-start.4 = (bf16[64,2048]{1,0:T(8,128)(2,1)S(1)}, bf16[64,2048]{1,0:T(8,128)(2,1)S(1)}, u32[]{:S(2)}, u32[]{:S(2)}) collective-permute-start(bf16[64,2048]{1,0:T(8,128)(2,1)S(1)} %get-tuple-element.26), channel_id=1, source_target_pairs={{0,4},{4,0},{8,260},{12,256},{256,12},{260,8},{264,268},{268,264},... | collective-permute-start | bytes 786440 | tf_op jit(solution)/shard_map/ppermute | solution.py:55
  5.3 1.5 reduce_max.25
  7.7 4.6 %collective-permute-start = (bf16[264,512]{1,0:T(8,128)(2,1)S(1)}, bf16[264,512]{1,0:T(8,128)(2,1)S(1)}, u32[]{:S(2)}, u32[]{:S(2)}) collective-permute-start(bf16[264,512]{1,0:T(8,128)(2,1)S(1)} %fusion.8.own), channel_id=1, source_target_pairs={{0,256},{256,0},{1,257},{257,1},{2,258},{258,2},{3,259},{259,3},{4... | collective-permute-start | bytes 811016 | tf_op jit(solution)/shard_map/ppermute | solution.py:37
  12.4 3.8 %collective-permute-start.1 = (bf16[264,512]{1,0:T(8,128)(2,1)S(1)}, bf16[264,512]{1,0:T(8,128)(2,1)S(1)}, u32[]{:S(2)}, u32[]{:S(2)}) collective-permute-start(bf16[264,512]{1,0:T(8,128)(2,1)S(1)} %fusion.8.own), channel_id=1, source_target_pairs={{0,16},{16,0},{1,17},{17,1},{2,18},{18,2},{3,19},{19,3},{4,20},{20... | collective-permute-start | bytes 811016 | tf_op jit(solution)/shard_map/ppermute | solution.py:37
  16.9 0.8 broadcast_in_dim.40
  17.7 13.8 %all-to-all-start = ((bf16[8,64,512]{2,1,0:T(8,128)(2,1)}), bf16[8,64,512]{2,1,0:T(8,128)(2,1)S(1)}, u32[]{:S(2)}, u32[]{:S(2)}) async-start(bf16[8,64,512]{2,1,0:T(8,128)(2,1)} %broadcast_in_dim.40), calls=%async_computation | async-start | bytes 1048576 | tf_op jit(solution)/shard_map/all_to_all | solution.py:20
  31.6 0.8 dynamic_slice.43
  32.6 5.1 %collective-permute-start.5 = (bf16[128,1024]{1,0:T(8,128)(2,1)S(1)}, bf16[128,1024]{1,0:T(8,128)(2,1)S(1)}, u32[]{:S(2)}, u32[]{:S(2)}) collective-permute-start(bf16[128,1024]{1,0:T(8,128)(2,1)S(1)} %pad_maximum_fusion.1), channel_id=1, source_target_pairs={{0,2},{2,0},{1,3},{3,1},{4,6},{6,4},{5,7},{7,5},{8,10},{10,8},{9,1... | collective-permute-start | bytes 786440 | tf_op jit(solution)/shard_map/ppermute | solution.py:37
  37.8 2.9 %collective-permute-start.2 = (bf16[264,512]{1,0:T(8,128)(2,1)S(1)}, bf16[264,512]{1,0:T(8,128)(2,1)S(1)}, u32[]{:S(2)}, u32[]{:S(2)}) collective-permute-start(bf16[264,512]{1,0:T(8,128)(2,1)S(1)} %collective-permute-done.across), channel_id=1, source_target_pairs={{0,16},{16,0},{1,17},{17,1},{2,18},{18,2},{3,19},{19,3},{4,20},{20... | collective-permute-start | bytes 811016 | tf_op jit(solution)/shard_map/ppermute | solution.py:37
  41.0 1.7 %collective-permute-done.5 = bf16[128,1024]{1,0:T(8,128)(2,1)S(1)} collective-permute-done((bf16[128,1024]{1,0:T(8,128)(2,1)S(1)}, bf16[128,1024]{1,0:T(8,128)(2,1)S(1)}, u32[]{:S(2)}, u32[]{:S(2)}) %collective-permute-start.5) | collective-permute-done | bytes 262176 | tf_op jit(solution)/shard_map/ppermute | solution.py:37
  42.7 1.9 %collective-permute-start.6 = (bf16[256,512]{1,0:T(8,128)(2,1)S(1)}, bf16[256,512]{1,0:T(8,128)(2,1)S(1)}, u32[]{:S(2)}, u32[]{:S(2)}) collective-permute-start(bf16[256,512]{1,0:T(8,128)(2,1)S(1)} %pad_maximum_fusion.3), channel_id=1, source_target_pairs={{0,1},{1,0},{2,3},{3,2},{4,5},{5,4},{6,7},{7,6},{8,9},{9,8},{10,11... | collective-permute-start | bytes 786440 | tf_op jit(solution)/shard_map/ppermute | solution.py:37
  44.6 15.0 %collective-permute-done.2.both = bf16[264,512]{1,0:T(8,128)(2,1)S(1)} collective-permute-done((bf16[264,512]{1,0:T(8,128)(2,1)S(1)}, bf16[264,512]{1,0:T(8,128)(2,1)S(1)}, u32[]{:S(2)}, u32[]{:S(2)}) %collective-permute-start.2) | collective-permute-done | bytes 270368 | tf_op jit(solution)/shard_map/ppermute | solution.py:37
  60.2 1.7 %all-to-all-done.wd = bf16[8,64,512]{2,1,0:T(8,128)(2,1)S(1)} async-done(((bf16[8,64,512]{2,1,0:T(8,128)(2,1)}), bf16[8,64,512]{2,1,0:T(8,128)(2,1)S(1)}, u32[]{:S(2)}, u32[]{:S(2)}) %all-to-all-start) | async-done | bytes 524320 | tf_op jit(solution)/shard_map/all_to_all | solution.py:20
  61.9 1.3 shard_map.112
  63.2 26.3 %all_to_all.25 = bf16[16,264,128]{2,1,0:T(8,128)(2,1)S(1)} all-to-all(bf16[16,264,128]{2,1,0:T(8,128)(2,1)S(1)} %shard_map.112), channel_id=1, replica_groups=mesh['a'=2,'zh'=8,'zl'=2,'x'=4,'b'=2,'c'=2] {'x','b','c'}, dimensions={0} | all-to-all | bytes 2162688 | tf_op jit(solution)/shard_map/all_to_all | solution.py:20
  90.6 1.1 broadcast_in_dim.74
  91.7 3.7 %all-to-all-start.2 = ((bf16[16,264,128]{2,1,0:T(8,128)(2,1)}), bf16[16,264,128]{2,1,0:T(8,128)(2,1)S(1)}, u32[]{:S(2)}, u32[]{:S(2)}) async-start(bf16[16,264,128]{2,1,0:T(8,128)(2,1)} %broadcast_in_dim.74), calls=%async_computation.2 | async-start | bytes 2162688 | tf_op jit(solution)/shard_map/all_to_all | solution.py:20
  95.5 18.2 %all-to-all-done.2.got = bf16[16,264,128]{2,1,0:T(8,128)(2,1)S(1)} async-done(((bf16[16,264,128]{2,1,0:T(8,128)(2,1)}), bf16[16,264,128]{2,1,0:T(8,128)(2,1)S(1)}, u32[]{:S(2)}, u32[]{:S(2)}) %all-to-all-start.2) | async-done | bytes 1081376 | tf_op jit(solution)/shard_map/all_to_all | solution.py:20
  114.9 0.8 shard_map.113
  115.7 7.4 %all_to_all.26 = f32[4,16,128]{2,1,0:T(8,128)S(1)} all-to-all(f32[4,16,128]{2,1,0:T(8,128)S(1)} %maximum_maximum_fusion), channel_id=1, replica_groups=mesh['a'=2,'zh'=8,'zl'=2,'x'=4,'b'=2,'c'=2] {'a','zl'}, dimensions={0} | all-to-all | bytes 65536 | tf_op jit(solution)/shard_map/all_to_all | solution.py:20
  123.3 0.8 pad_maximum_fusion
  124.1 10.3 %all-to-all-start.4 = ((bf16[8,264,128]{2,1,0:T(8,128)(2,1)}), bf16[8,264,128]{2,1,0:T(8,128)(2,1)S(1)}, u32[]{:S(2)}, u32[]{:S(2)}) async-start(bf16[8,264,128]{2,1,0:T(8,128)(2,1)} %pad_maximum_fusion), calls=%async_computation.4 | async-start | bytes 1081344 | tf_op jit(solution)/shard_map/all_to_all | solution.py:20
  134.5 30.4 %all-to-all-done.4.parts = bf16[8,264,128]{2,1,0:T(8,128)(2,1)S(1)} async-done(((bf16[8,264,128]{2,1,0:T(8,128)(2,1)}), bf16[8,264,128]{2,1,0:T(8,128)(2,1)S(1)}, u32[]{:S(2)}, u32[]{:S(2)}) %all-to-all-start.4) | async-done | bytes 540704 | tf_op jit(solution)/shard_map/all_to_all | solution.py:20
  (114 shorter events, 6.6 us)
Async XLA Ops:
  0.6 6.2 %copy-start = (bf16[256,2000]{0,1:T(8,128)(2,1)S(1)}, bf16[256,2000]{0,1:T(8,128)(2,1)}, u32[]{:S(2)}) copy-start(bf16[256,2000]{0,1:T(8,128)(2,1)} %param.14) | copy-start | bytes 3072004
  0.6 6.7 %copy-start.3 = (s32[256,1]{0,1:T(1,128)S(1)}, s32[256,1]{0,1:T(1,128)}, u32[]{:S(2)}) copy-start(s32[256,1]{0,1:T(1,128)} %param.17) | copy-start | bytes 3076
  0.7 6.9 %copy-start.6 = (s32[1,2]{1,0:T(1,128)S(1)}, s32[1,2]{1,0:T(1,128)}, u32[]{:S(2)}) copy-start(s32[1,2]{1,0:T(1,128)} %param.15) | copy-start | bytes 28
  0.7 6.9 %copy-start.5 = (s32[256]{0:T(256)S(1)}, s32[256]{0:T(256)}, u32[]{:S(2)}) copy-start(s32[256]{0:T(256)} %param.16) | copy-start | bytes 3076
  0.7 7.0 %copy-start.1 = (bf16[256,512]{1,0:T(8,128)(2,1)S(1)}, bf16[256,512]{1,0:T(8,128)(2,1)}, u32[]{:S(2)}) copy-start(bf16[256,512]{1,0:T(8,128)(2,1)} %param.9) | copy-start | bytes 786436
  0.7 16.2 %copy-start.2 = (bf16[64,512]{1,0:T(8,128)(2,1)S(1)}, bf16[64,512]{1,0:T(8,128)(2,1)}, u32[]{:S(2)}) copy-start(bf16[64,512]{1,0:T(8,128)(2,1)} %param.13) | copy-start | bytes 196612
  1.9 30.4 %copy-start.4 = (f32[512]{0:T(512)S(1)}, f32[512]{0:T(512)}, u32[]{:S(2)}) copy-start(f32[512]{0:T(512)} %param.12) | copy-start | bytes 6148
  1.9 30.6 %collective-permute-start.4 = (bf16[64,2048]{1,0:T(8,128)(2,1)S(1)}, bf16[64,2048]{1,0:T(8,128)(2,1)S(1)}, u32[]{:S(2)}, u32[]{:S(2)}) collective-permute-start(bf16[64,2048]{1,0:T(8,128)(2,1)S(1)} %get-tuple-element.26), channel_id=1, source_target_pairs={{0,4},{4,0},{8,260},{12,256},{256,12},{260,8},{264,268},{268,264},... | collective-permute-start | bytes 786440 | tf_op jit(solution)/shard_map/ppermute | solution.py:55
  7.7 30.0 %collective-permute-start = (bf16[264,512]{1,0:T(8,128)(2,1)S(1)}, bf16[264,512]{1,0:T(8,128)(2,1)S(1)}, u32[]{:S(2)}, u32[]{:S(2)}) collective-permute-start(bf16[264,512]{1,0:T(8,128)(2,1)S(1)} %fusion.8.own), channel_id=1, source_target_pairs={{0,256},{256,0},{1,257},{257,1},{2,258},{258,2},{3,259},{259,3},{4... | collective-permute-start | bytes 811016 | tf_op jit(solution)/shard_map/ppermute | solution.py:37
  12.4 28.5 %collective-permute-start.1 = (bf16[264,512]{1,0:T(8,128)(2,1)S(1)}, bf16[264,512]{1,0:T(8,128)(2,1)S(1)}, u32[]{:S(2)}, u32[]{:S(2)}) collective-permute-start(bf16[264,512]{1,0:T(8,128)(2,1)S(1)} %fusion.8.own), channel_id=1, source_target_pairs={{0,16},{16,0},{1,17},{17,1},{2,18},{18,2},{3,19},{19,3},{4,20},{20... | collective-permute-start | bytes 811016 | tf_op jit(solution)/shard_map/ppermute | solution.py:37
  16.2 16.3 %collective-permute-start.3 = (bf16[64,2048]{1,0:T(8,128)(2,1)S(1)}, bf16[64,2048]{1,0:T(8,128)(2,1)S(1)}, u32[]{:S(2)}, u32[]{:S(2)}) collective-permute-start(bf16[64,2048]{1,0:T(8,128)(2,1)S(1)} %get-tuple-element.25), channel_id=1, source_target_pairs={{0,0},{4,4},{8,256},{12,260},{256,8},{260,12},{264,264},{268,268},... | collective-permute-start | bytes 786440 | tf_op jit(solution)/shard_map/ppermute | solution.py:54
  17.7 44.2 %all-to-all-start = ((bf16[8,64,512]{2,1,0:T(8,128)(2,1)}), bf16[8,64,512]{2,1,0:T(8,128)(2,1)S(1)}, u32[]{:S(2)}, u32[]{:S(2)}) async-start(bf16[8,64,512]{2,1,0:T(8,128)(2,1)} %broadcast_in_dim.40), calls=%async_computation | async-start | bytes 1048576 | tf_op jit(solution)/shard_map/all_to_all | solution.py:20
  32.6 10.0 %collective-permute-start.5 = (bf16[128,1024]{1,0:T(8,128)(2,1)S(1)}, bf16[128,1024]{1,0:T(8,128)(2,1)S(1)}, u32[]{:S(2)}, u32[]{:S(2)}) collective-permute-start(bf16[128,1024]{1,0:T(8,128)(2,1)S(1)} %pad_maximum_fusion.1), channel_id=1, source_target_pairs={{0,2},{2,0},{1,3},{3,1},{4,6},{6,4},{5,7},{7,5},{8,10},{10,8},{9,1... | collective-permute-start | bytes 786440 | tf_op jit(solution)/shard_map/ppermute | solution.py:37
  37.8 21.9 %collective-permute-start.2 = (bf16[264,512]{1,0:T(8,128)(2,1)S(1)}, bf16[264,512]{1,0:T(8,128)(2,1)S(1)}, u32[]{:S(2)}, u32[]{:S(2)}) collective-permute-start(bf16[264,512]{1,0:T(8,128)(2,1)S(1)} %collective-permute-done.across), channel_id=1, source_target_pairs={{0,16},{16,0},{1,17},{17,1},{2,18},{18,2},{3,19},{19,3},{4,20},{20... | collective-permute-start | bytes 811016 | tf_op jit(solution)/shard_map/ppermute | solution.py:37
  42.7 17.5 %collective-permute-start.6 = (bf16[256,512]{1,0:T(8,128)(2,1)S(1)}, bf16[256,512]{1,0:T(8,128)(2,1)S(1)}, u32[]{:S(2)}, u32[]{:S(2)}) collective-permute-start(bf16[256,512]{1,0:T(8,128)(2,1)S(1)} %pad_maximum_fusion.3), channel_id=1, source_target_pairs={{0,1},{1,0},{2,3},{3,2},{4,5},{5,4},{6,7},{7,6},{8,9},{9,8},{10,11... | collective-permute-start | bytes 786440 | tf_op jit(solution)/shard_map/ppermute | solution.py:37
  91.7 22.0 %all-to-all-start.2 = ((bf16[16,264,128]{2,1,0:T(8,128)(2,1)}), bf16[16,264,128]{2,1,0:T(8,128)(2,1)S(1)}, u32[]{:S(2)}, u32[]{:S(2)}) async-start(bf16[16,264,128]{2,1,0:T(8,128)(2,1)} %broadcast_in_dim.74), calls=%async_computation.2 | async-start | bytes 2162688 | tf_op jit(solution)/shard_map/all_to_all | solution.py:20
  124.1 40.7 %all-to-all-start.4 = ((bf16[8,264,128]{2,1,0:T(8,128)(2,1)}), bf16[8,264,128]{2,1,0:T(8,128)(2,1)S(1)}, u32[]{:S(2)}, u32[]{:S(2)}) async-start(bf16[8,264,128]{2,1,0:T(8,128)(2,1)} %pad_maximum_fusion), calls=%async_computation.4 | async-start | bytes 1081344 | tf_op jit(solution)/shard_map/all_to_all | solution.py:20

commit v7 on v6

--- a/solution.py
+++ b/solution.py
@@ -39,20 +39,23 @@
 
 def teacher_block(target_weight, a, zl, slab, width):
     x, b, c = (lax.axis_index(axis) for axis in MP)
-    quarter = 4 * width
-
-    def piece(column):
-        return lax.dynamic_slice(target_weight, (zl * slab, column * quarter), (slab, quarter))
-
-    def turn(swap):
-        moves = []
-        for k in range(8):
-            side, at = divmod(k, 4)
-            moves.append((k, at // 2 * 4 + 2 * side + (at % 2) ^ swap))
-        return moves
-
-    near = lax.ppermute(piece(2 * a + x % 2), ("a", "x"), turn(0))
-    far = lax.ppermute(piece(2 * a + 1 - x % 2), ("a", "x"), turn(1))
+    half = 2 * width
+    ours = x // 2 == a
+
+    def piece(shift):
+        column = 2 * ((x + shift) % 4) + jnp.where(ours, b, 1 - b)
+        return lax.dynamic_slice(target_weight, (zl * slab, column * half), (slab, half))
+
+    pieces = lax.optimization_barrier([piece(shift) for shift in range(4)])
+    came = pieces[:1]
+    for shift in (1, 2, 3):
+        came.append(
+            lax.ppermute(pieces[shift], "x", [(k, (k + shift) % 4) for k in range(4)])
+        )
+    odd = ours == (x % 2 == 1)
+    kept = jnp.concatenate([jnp.where(ours, came[0], came[2]), jnp.where(odd, came[1], came[3])])
+    sent = jnp.concatenate([jnp.where(ours, came[2], came[0]), jnp.where(odd, came[3], came[1])])
+    parts = kept, flipped(sent, ("a", "b"))
 
     def halve(parts, mine, axis):
         half = parts[0].shape[1] // 2
@@ -64,7 +67,6 @@
 
         return side(mine), flipped(side(1 - mine), (axis,))
 
-    parts = halve((near, far), b, "b")
     parts = halve(parts, c, "c")
     return [part.reshape(4, slab, width) for part in parts], 4 * (x % 2) + 2 * b + c
 
@@ -230,7 +232,9 @@
 
     gain_slice = lax.dynamic_slice_in_dim(target_gain, model * width, width)
     gains = jnp.stack([draft_gain, gain_slice])
-    squares = [jnp.sum(block[:rows].astype(jnp.float32) ** 2, axis=1) for block in blocks]
+    squares = []
+    for block in blocks:
+        squares.append(jnp.sum(block[:rows].astype(jnp.float32) ** 2, axis=1))
     squares = jnp.stack(halves(jnp.stack(squares))).reshape(2, models, mine)
     facts_here = facts_here.swapaxes(0, 1).reshape(kinds, models, mine)
     side = jnp.concatenate([facts_here, squares], axis=0).swapaxes(0, 1)

time: 167 us -> 171 us (1.024)
  starting transfers between devices: 50.3 us -> 55.5 us
  blocking collectives: 33.8 us -> 30.8 us
    ppermute x2 -> x3, starting transfers between devices: 4.08 us -> 12 us  [teacher_block(): lax.ppermute(pieces[shift], 'x', [(k, (k + shift) % 4) for k in range(4)])]
    all_to_all x2, blocking collectives: 33.8 us -> 30.8 us  [exchange(): return lax.all_to_all(value, axes, split_axis=0, concat_axis=0, tiled=True)]
    ppermute x5, starting transfers between devices: 18.4 us -> 16.2 us  [flipped(): return lax.ppermute(value, axes, [(k, last - k) for k in range(last + 1)])]
  transfers between devices with their start and end apart: 10 -> 11, of which waited for: 5 -> 5; matrix products, arithmetic and copies ran while one was open for 3% -> 2% of each run, Pallas kernels for 0% -> 0%
where the time goes in v7:
time: 171 us; the launch traced here: 170 us
  waiting for transfers between devices  67 us (39%)
  starting transfers between devices  55.5 us (32%)
  blocking collectives  30.8 us (18%)
  other arithmetic  6.37 us (4%)
  local copies, waits for them, and re-layouts  6.04 us (4%)
  Pallas kernels  2.75 us (2%)
    all_to_all x3, waiting for transfers between devices, exchange(): return lax.all_to_all(value, axes, split_axis=0, concat_axis=0, tiled=True)  49.7 us
    all_to_all x2, blocking collectives, exchange(): return lax.all_to_all(value, axes, split_axis=0, concat_axis=0, tiled=True)  30.8 us
    all_to_all x3, starting transfers between devices, exchange(): return lax.all_to_all(value, axes, split_axis=0, concat_axis=0, tiled=True)  27.3 us
    ppermute x5, waiting for transfers between devices, flipped(): return lax.ppermute(value, axes, [(k, last - k) for k in range(last + 1)])  17.3 us
    ppermute x5, starting transfers between devices, flipped(): return lax.ppermute(value, axes, [(k, last - k) for k in range(last + 1)])  16.2 us
    ppermute x3, starting transfers between devices, teacher_block(): lax.ppermute(pieces[shift], 'x', [(k, (k + shift) % 4) for k in range(4)])  12 us
  transfers between devices with their start and end apart: 11, of which 5 were waited for; matrix products, arithmetic and copies ran while one was open for 2% of the time, Pallas kernels for 0%

profile of v7, /device:TPU:64, one launch (start us, length us, event | category | flops | bytes accessed | tf_op | source)
XLA Modules:
  0.0 170.0 jit_solution(15360785161344142220)
XLA Ops:
  0.7 1.5 reduce_max.25
  2.2 1.7 %fusion = (f32[256]{0:T(256)S(1)}, f32[256]{0:T(256)S(1)}) fusion(bf16[256,2000]{0,1:T(8,128)(2,1)} %param.14, f32[256]{0:T(256)S(1)} %reduce_max.27), kind=kLoop, calls=%fused_computation.3 | loop fusion | flops 2559488 | bytes 1027072 | tf_op jit(solution)/shard_map/reduce_sum | solution.py:170
  4.4 3.5 %collective-permute-start = (bf16[264,512]{1,0:T(8,128)(2,1)S(1)}, bf16[264,512]{1,0:T(8,128)(2,1)S(1)}, u32[]{:S(2)}, u32[]{:S(2)}) collective-permute-start(bf16[264,512]{1,0:T(8,128)(2,1)S(1)} %fusion.8.own), channel_id=1, source_target_pairs={{0,256},{256,0},{1,257},{257,1},{2,258},{258,2},{3,259},{259,3},{4... | collective-permute-start | bytes 811016 | tf_op jit(solution)/shard_map/ppermute | solution.py:37
  7.8 3.8 %collective-permute-start.1 = (bf16[264,512]{1,0:T(8,128)(2,1)S(1)}, bf16[264,512]{1,0:T(8,128)(2,1)S(1)}, u32[]{:S(2)}, u32[]{:S(2)}) collective-permute-start(bf16[264,512]{1,0:T(8,128)(2,1)S(1)} %fusion.8.own), channel_id=1, source_target_pairs={{0,16},{16,0},{1,17},{17,1},{2,18},{18,2},{3,19},{19,3},{4,20},{20... | collective-permute-start | bytes 811016 | tf_op jit(solution)/shard_map/ppermute | solution.py:37
  11.8 1.1 fusion.56
  12.9 4.9 %collective-permute-start.3 = (bf16[64,1024]{1,0:T(8,128)(2,1)S(1)}, bf16[64,1024]{1,0:T(8,128)(2,1)S(1)}, u32[]{:S(2)}, u32[]{:S(2)}) collective-permute-start(bf16[64,1024]{1,0:T(8,128)(2,1)S(1)} %get-tuple-element.13), channel_id=1, source_target_pairs={{0,8},{4,12},{8,0},{12,4},{1,9},{5,13},{9,1},{13,5},{2,10},{6,14},... | collective-permute-start | bytes 393224 | tf_op jit(solution)/shard_map/ppermute | solution.py:53
  17.9 2.5 %collective-permute-start.4 = (bf16[64,1024]{1,0:T(8,128)(2,1)S(1)}, bf16[64,1024]{1,0:T(8,128)(2,1)S(1)}, u32[]{:S(2)}, u32[]{:S(2)}) collective-permute-start(bf16[64,1024]{1,0:T(8,128)(2,1)S(1)} %get-tuple-element.14), channel_id=1, source_target_pairs={{0,4},{4,8},{8,12},{12,0},{1,5},{5,9},{9,13},{13,1},{2,6},{6,10},{... | collective-permute-start | bytes 393224 | tf_op jit(solution)/shard_map/ppermute | solution.py:53
  20.4 4.6 %collective-permute-start.5 = (bf16[64,1024]{1,0:T(8,128)(2,1)S(1)}, bf16[64,1024]{1,0:T(8,128)(2,1)S(1)}, u32[]{:S(2)}, u32[]{:S(2)}) collective-permute-start(bf16[64,1024]{1,0:T(8,128)(2,1)S(1)} %get-tuple-element.15), channel_id=1, source_target_pairs={{0,12},{4,0},{8,4},{12,8},{1,13},{5,1},{9,5},{13,9},{2,14},{6,2},{... | collective-permute-start | bytes 393224 | tf_op jit(solution)/shard_map/ppermute | solution.py:53
  24.9 0.8 broadcast_in_dim.40
  25.8 13.8 %all-to-all-start = ((bf16[8,64,512]{2,1,0:T(8,128)(2,1)}), bf16[8,64,512]{2,1,0:T(8,128)(2,1)S(1)}, u32[]{:S(2)}, u32[]{:S(2)}) async-start(bf16[8,64,512]{2,1,0:T(8,128)(2,1)} %broadcast_in_dim.40), calls=%async_computation | async-start | bytes 1048576 | tf_op jit(solution)/shard_map/all_to_all | solution.py:20
  40.7 4.1 %collective-permute-start.6 = (bf16[128,1024]{1,0:T(8,128)(2,1)S(1)}, bf16[128,1024]{1,0:T(8,128)(2,1)S(1)}, u32[]{:S(2)}, u32[]{:S(2)}) collective-permute-start(bf16[128,1024]{1,0:T(8,128)(2,1)S(1)} %pad_maximum_fusion.1), channel_id=1, source_target_pairs={{0,258},{2,256},{256,2},{258,0},{1,259},{3,257},{257,3},{259,1},{4... | collective-permute-start | bytes 786440 | tf_op jit(solution)/shard_map/ppermute | solution.py:37
  44.8 2.9 %collective-permute-start.2 = (bf16[264,512]{1,0:T(8,128)(2,1)S(1)}, bf16[264,512]{1,0:T(8,128)(2,1)S(1)}, u32[]{:S(2)}, u32[]{:S(2)}) collective-permute-start(bf16[264,512]{1,0:T(8,128)(2,1)S(1)} %collective-permute-done.across), channel_id=1, source_target_pairs={{0,16},{16,0},{1,17},{17,1},{2,18},{18,2},{3,19},{19,3},{4,20},{20... | collective-permute-start | bytes 811016 | tf_op jit(solution)/shard_map/ppermute | solution.py:37
  48.0 2.1 %collective-permute-done.6 = bf16[128,1024]{1,0:T(8,128)(2,1)S(1)} collective-permute-done((bf16[128,1024]{1,0:T(8,128)(2,1)S(1)}, bf16[128,1024]{1,0:T(8,128)(2,1)S(1)}, u32[]{:S(2)}, u32[]{:S(2)}) %collective-permute-start.6) | collective-permute-done | bytes 262176 | tf_op jit(solution)/shard_map/ppermute | solution.py:37
  50.2 1.9 %collective-permute-start.7 = (bf16[256,512]{1,0:T(8,128)(2,1)S(1)}, bf16[256,512]{1,0:T(8,128)(2,1)S(1)}, u32[]{:S(2)}, u32[]{:S(2)}) collective-permute-start(bf16[256,512]{1,0:T(8,128)(2,1)S(1)} %pad_maximum_fusion.3), channel_id=1, source_target_pairs={{0,1},{1,0},{2,3},{3,2},{4,5},{5,4},{6,7},{7,6},{8,9},{9,8},{10,11... | collective-permute-start | bytes 786440 | tf_op jit(solution)/shard_map/ppermute | solution.py:37
  52.1 15.2 %collective-permute-done.2.both = bf16[264,512]{1,0:T(8,128)(2,1)S(1)} collective-permute-done((bf16[264,512]{1,0:T(8,128)(2,1)S(1)}, bf16[264,512]{1,0:T(8,128)(2,1)S(1)}, u32[]{:S(2)}, u32[]{:S(2)}) %collective-permute-start.2) | collective-permute-done | bytes 270368 | tf_op jit(solution)/shard_map/ppermute | solution.py:37
  67.9 1.2 all-to-all-done.wd
  69.0 1.3 shard_map.112
  70.3 22.7 %all_to_all.25 = bf16[16,264,128]{2,1,0:T(8,128)(2,1)S(1)} all-to-all(bf16[16,264,128]{2,1,0:T(8,128)(2,1)S(1)} %shard_map.112), channel_id=1, replica_groups=mesh['a'=2,'zh'=8,'zl'=2,'x'=4,'b'=2,'c'=2] {'x','b','c'}, dimensions={0} | all-to-all | bytes 2162688 | tf_op jit(solution)/shard_map/all_to_all | solution.py:20
  94.0 1.1 broadcast_in_dim.74
  95.1 3.7 %all-to-all-start.2 = ((bf16[16,264,128]{2,1,0:T(8,128)(2,1)}), bf16[16,264,128]{2,1,0:T(8,128)(2,1)S(1)}, u32[]{:S(2)}, u32[]{:S(2)}) async-start(bf16[16,264,128]{2,1,0:T(8,128)(2,1)} %broadcast_in_dim.74), calls=%async_computation.2 | async-start | bytes 2162688 | tf_op jit(solution)/shard_map/all_to_all | solution.py:20
  98.9 18.2 %all-to-all-done.2.got = bf16[16,264,128]{2,1,0:T(8,128)(2,1)S(1)} async-done(((bf16[16,264,128]{2,1,0:T(8,128)(2,1)}), bf16[16,264,128]{2,1,0:T(8,128)(2,1)S(1)}, u32[]{:S(2)}, u32[]{:S(2)}) %all-to-all-start.2) | async-done | bytes 1081376 | tf_op jit(solution)/shard_map/all_to_all | solution.py:20
  119.1 8.1 %all_to_all.26 = f32[4,16,128]{2,1,0:T(8,128)S(1)} all-to-all(f32[4,16,128]{2,1,0:T(8,128)S(1)} %maximum_maximum_fusion), channel_id=1, replica_groups=mesh['a'=2,'zh'=8,'zl'=2,'x'=4,'b'=2,'c'=2] {'a','zl'}, dimensions={0} | all-to-all | bytes 65536 | tf_op jit(solution)/shard_map/all_to_all | solution.py:20
  128.2 9.8 %all-to-all-start.4 = ((bf16[8,264,128]{2,1,0:T(8,128)(2,1)}), bf16[8,264,128]{2,1,0:T(8,128)(2,1)S(1)}, u32[]{:S(2)}, u32[]{:S(2)}) async-start(bf16[8,264,128]{2,1,0:T(8,128)(2,1)} %pad_maximum_fusion), calls=%async_computation.4 | async-start | bytes 1081344 | tf_op jit(solution)/shard_map/all_to_all | solution.py:20
  138.0 30.4 %all-to-all-done.4.parts = bf16[8,264,128]{2,1,0:T(8,128)(2,1)S(1)} async-done(((bf16[8,264,128]{2,1,0:T(8,128)(2,1)}), bf16[8,264,128]{2,1,0:T(8,128)(2,1)S(1)}, u32[]{:S(2)}, u32[]{:S(2)}) %all-to-all-start.4) | async-done | bytes 540704 | tf_op jit(solution)/shard_map/all_to_all | solution.py:20
  (114 shorter events, 7.7 us)
Async XLA Ops:
  0.6 3.4 %copy-start.2 = (s32[256,1]{0,1:T(1,128)S(1)}, s32[256,1]{0,1:T(1,128)}, u32[]{:S(2)}) copy-start(s32[256,1]{0,1:T(1,128)} %param.17) | copy-start | bytes 3076
  0.6 3.5 %copy-start.5 = (s32[1,2]{1,0:T(1,128)S(1)}, s32[1,2]{1,0:T(1,128)}, u32[]{:S(2)}) copy-start(s32[1,2]{1,0:T(1,128)} %param.15) | copy-start | bytes 28
  0.7 3.5 %copy-start.4 = (s32[256]{0:T(256)S(1)}, s32[256]{0:T(256)}, u32[]{:S(2)}) copy-start(s32[256]{0:T(256)} %param.16) | copy-start | bytes 3076
  0.7 3.7 %copy-start = (bf16[256,512]{1,0:T(8,128)(2,1)S(1)}, bf16[256,512]{1,0:T(8,128)(2,1)}, u32[]{:S(2)}) copy-start(bf16[256,512]{1,0:T(8,128)(2,1)} %param.9) | copy-start | bytes 786436
  0.7 24.3 %copy-start.1 = (bf16[64,512]{1,0:T(8,128)(2,1)S(1)}, bf16[64,512]{1,0:T(8,128)(2,1)}, u32[]{:S(2)}) copy-start(bf16[64,512]{1,0:T(8,128)(2,1)} %param.13) | copy-start | bytes 196612
  2.2 38.1 %copy-start.3 = (f32[512]{0:T(512)S(1)}, f32[512]{0:T(512)}, u32[]{:S(2)}) copy-start(f32[512]{0:T(512)} %param.12) | copy-start | bytes 6148
  4.4 40.4 %collective-permute-start = (bf16[264,512]{1,0:T(8,128)(2,1)S(1)}, bf16[264,512]{1,0:T(8,128)(2,1)S(1)}, u32[]{:S(2)}, u32[]{:S(2)}) collective-permute-start(bf16[264,512]{1,0:T(8,128)(2,1)S(1)} %fusion.8.own), channel_id=1, source_target_pairs={{0,256},{256,0},{1,257},{257,1},{2,258},{258,2},{3,259},{259,3},{4... | collective-permute-start | bytes 811016 | tf_op jit(solution)/shard_map/ppermute | solution.py:37
  7.8 40.0 %collective-permute-start.1 = (bf16[264,512]{1,0:T(8,128)(2,1)S(1)}, bf16[264,512]{1,0:T(8,128)(2,1)S(1)}, u32[]{:S(2)}, u32[]{:S(2)}) collective-permute-start(bf16[264,512]{1,0:T(8,128)(2,1)S(1)} %fusion.8.own), channel_id=1, source_target_pairs={{0,16},{16,0},{1,17},{17,1},{2,18},{18,2},{3,19},{19,3},{4,20},{20... | collective-permute-start | bytes 811016 | tf_op jit(solution)/shard_map/ppermute | solution.py:37
  12.9 27.6 %collective-permute-start.3 = (bf16[64,1024]{1,0:T(8,128)(2,1)S(1)}, bf16[64,1024]{1,0:T(8,128)(2,1)S(1)}, u32[]{:S(2)}, u32[]{:S(2)}) collective-permute-start(bf16[64,1024]{1,0:T(8,128)(2,1)S(1)} %get-tuple-element.13), channel_id=1, source_target_pairs={{0,8},{4,12},{8,0},{12,4},{1,9},{5,13},{9,1},{13,5},{2,10},{6,14},... | collective-permute-start | bytes 393224 | tf_op jit(solution)/shard_map/ppermute | solution.py:53
  17.9 22.7 %collective-permute-start.4 = (bf16[64,1024]{1,0:T(8,128)(2,1)S(1)}, bf16[64,1024]{1,0:T(8,128)(2,1)S(1)}, u32[]{:S(2)}, u32[]{:S(2)}) collective-permute-start(bf16[64,1024]{1,0:T(8,128)(2,1)S(1)} %get-tuple-element.14), channel_id=1, source_target_pairs={{0,4},{4,8},{8,12},{12,0},{1,5},{5,9},{9,13},{13,1},{2,6},{6,10},{... | collective-permute-start | bytes 393224 | tf_op jit(solution)/shard_map/ppermute | solution.py:53
  20.4 20.2 %collective-permute-start.5 = (bf16[64,1024]{1,0:T(8,128)(2,1)S(1)}, bf16[64,1024]{1,0:T(8,128)(2,1)S(1)}, u32[]{:S(2)}, u32[]{:S(2)}) collective-permute-start(bf16[64,1024]{1,0:T(8,128)(2,1)S(1)} %get-tuple-element.15), channel_id=1, source_target_pairs={{0,12},{4,0},{8,4},{12,8},{1,13},{5,1},{9,5},{13,9},{2,14},{6,2},{... | collective-permute-start | bytes 393224 | tf_op jit(solution)/shard_map/ppermute | solution.py:53
  25.8 43.3 %all-to-all-start = ((bf16[8,64,512]{2,1,0:T(8,128)(2,1)}), bf16[8,64,512]{2,1,0:T(8,128)(2,1)S(1)}, u32[]{:S(2)}, u32[]{:S(2)}) async-start(bf16[8,64,512]{2,1,0:T(8,128)(2,1)} %broadcast_in_dim.40), calls=%async_computation | async-start | bytes 1048576 | tf_op jit(solution)/shard_map/all_to_all | solution.py:20
  40.7 9.5 %collective-permute-start.6 = (bf16[128,1024]{1,0:T(8,128)(2,1)S(1)}, bf16[128,1024]{1,0:T(8,128)(2,1)S(1)}, u32[]{:S(2)}, u32[]{:S(2)}) collective-permute-start(bf16[128,1024]{1,0:T(8,128)(2,1)S(1)} %pad_maximum_fusion.1), channel_id=1, source_target_pairs={{0,258},{2,256},{256,2},{258,0},{1,259},{3,257},{257,3},{259,1},{4... | collective-permute-start | bytes 786440 | tf_op jit(solution)/shard_map/ppermute | solution.py:37
  44.8 22.5 %collective-permute-start.2 = (bf16[264,512]{1,0:T(8,128)(2,1)S(1)}, bf16[264,512]{1,0:T(8,128)(2,1)S(1)}, u32[]{:S(2)}, u32[]{:S(2)}) collective-permute-start(bf16[264,512]{1,0:T(8,128)(2,1)S(1)} %collective-permute-done.across), channel_id=1, source_target_pairs={{0,16},{16,0},{1,17},{17,1},{2,18},{18,2},{3,19},{19,3},{4,20},{20... | collective-permute-start | bytes 811016 | tf_op jit(solution)/shard_map/ppermute | solution.py:37
  50.2 17.7 %collective-permute-start.7 = (bf16[256,512]{1,0:T(8,128)(2,1)S(1)}, bf16[256,512]{1,0:T(8,128)(2,1)S(1)}, u32[]{:S(2)}, u32[]{:S(2)}) collective-permute-start(bf16[256,512]{1,0:T(8,128)(2,1)S(1)} %pad_maximum_fusion.3), channel_id=1, source_target_pairs={{0,1},{1,0},{2,3},{3,2},{4,5},{5,4},{6,7},{7,6},{8,9},{9,8},{10,11... | collective-permute-start | bytes 786440 | tf_op jit(solution)/shard_map/ppermute | solution.py:37
  95.1 22.0 %all-to-all-start.2 = ((bf16[16,264,128]{2,1,0:T(8,128)(2,1)}), bf16[16,264,128]{2,1,0:T(8,128)(2,1)S(1)}, u32[]{:S(2)}, u32[]{:S(2)}) async-start(bf16[16,264,128]{2,1,0:T(8,128)(2,1)} %broadcast_in_dim.74), calls=%async_computation.2 | async-start | bytes 2162688 | tf_op jit(solution)/shard_map/all_to_all | solution.py:20
  128.2 40.2 %all-to-all-start.4 = ((bf16[8,264,128]{2,1,0:T(8,128)(2,1)}), bf16[8,264,128]{2,1,0:T(8,128)(2,1)S(1)}, u32[]{:S(2)}, u32[]{:S(2)}) async-start(bf16[8,264,128]{2,1,0:T(8,128)(2,1)} %pad_maximum_fusion), calls=%async_computation.4 | async-start | bytes 1081344 | tf_op jit(solution)/shard_map/all_to_all | solution.py:20
